TPU v7x, 256 devices: a whole 4x4x8 slice. The times are simulated.
256 devices in a mesh: row: 32 (over y, z), col: 8 (over x, core).
Axes of the slice: x: 4, y: 4, z: 8, core: 2. Of those that a mesh axis runs over, the one named last changes fastest.
Arguments:
- weights: bfloat16 [24576, 24576], P('row', 'col'), may hold values from -0.0390625 to 0.0390625
- rates: bfloat16 [5, 24576, 128], P(None, 'col'), may hold values from -0.94921875 to 0.94921875
Outputs:
- weight_grad: bfloat16 [24576, 24576], P('row', 'col')
All inputs are finite; a program needn't handle non-finite values.
Results may differ from a plain program's by a relative error of at most 0.02.
Values may be sent and summed in bfloat16 or wider, within the bound.
No kernel may reach another device: no remote copies, remote signals or barrier semaphores. Data moves between devices by JAX's collectives and lax.ppermute only.
A program may use at most 128 MiB of HBM per device.

v0:
```python
import jax
import jax.numpy as jnp
from jax import lax
from jax.experimental import pallas as pl
from jax.experimental.pallas import tpu as pltpu
from jax.sharding import Mesh, PartitionSpec as P

STEPS = 4
Y, Z, X, C = 4, 8, 4, 2
EVERY = ("y", "z", "x", "core")
SWAP = [(0, 1), (1, 0)]
HALF = 384
QUARTER = 768
TRIALS = 128
COLS = 3072
VMEM = pl.BlockSpec(memory_space=pltpu.VMEM)
SMEM = pl.BlockSpec(memory_space=pltpu.SMEM)
HBM = pl.BlockSpec(memory_space=pltpu.HBM)


def flat(y, z, x, core):
    return ((y % Y * Z + z) * X + x % X) * C + core


def across(shift):
    return [
        (flat(y, z, x, core), flat(x, z, y + shift, core))
        for y in range(Y) for z in range(Z) for x in range(X) for core in range(C)
    ]


def from_root(shift):
    return [
        (flat(y, z, y, core), flat(y, z, y + shift, core))
        for y in range(Y) for z in range(Z) for core in range(C)
    ]


def params(mib):
    return pltpu.CompilerParams(vmem_limit_bytes=mib << 20)


def cost(flops, moved):
    return pl.CostEstimate(flops=flops, bytes_accessed=moved, transcendentals=0)


def half(core):
    return pl.ds(pl.multiple_of(core * HALF, 128), HALF)


def first_kernel(at_ref, rates_ref, mine_ref, theirs_ref, last_ref, zero_ref, sems):
    core = at_ref[1]
    rows = pl.ds(pl.multiple_of(at_ref[0] * QUARTER, 16), QUARTER)
    copies = [
        pltpu.make_async_copy(rates_ref.at[STEPS, rows], last_ref, sems.at[0]),
        pltpu.make_async_copy(rates_ref.at[0, rows], zero_ref, sems.at[1]),
    ]
    for copy in copies:
        copy.start()
    for copy in copies:
        copy.wait()
    for out_ref, part in ((theirs_ref, 1 - core), (mine_ref, core)):
        part = pl.ds(pl.multiple_of(part * HALF, 16), HALF)
        last = last_ref[part, :].astype(jnp.float32)
        zero = zero_ref[part, :].astype(jnp.float32)
        out_ref[...] = ((last - zero) * (1.0 - last * last)).astype(jnp.bfloat16).T


def first(at, rates):
    shape = jax.ShapeDtypeStruct((TRIALS, HALF), jnp.bfloat16)
    return pl.pallas_call(
        first_kernel,
        in_specs=[SMEM, HBM],
        out_specs=[VMEM, VMEM],
        out_shape=[shape, shape],
        scratch_shapes=[
            pltpu.VMEM((QUARTER, TRIALS), jnp.bfloat16),
            pltpu.VMEM((QUARTER, TRIALS), jnp.bfloat16),
            pltpu.SemaphoreType.DMA((2,)),
        ],
        compiler_params=params(52),
        name="first",
    )(at, rates)


def split_kernel(at_ref, w_ref, theirs_ref, sems):
    columns = [pl.ds(pl.multiple_of((2 * q + 1 - at_ref[1]) * HALF, 128), HALF) for q in range(4)]
    copies = [
        pltpu.make_async_copy(w_ref.at[:, columns[q]], theirs_ref.at[q], sems.at[q])
        for q in range(4)
    ]
    for copy in copies:
        copy.start()
    for copy in copies:
        copy.wait()


def split(at, weights):
    return pl.pallas_call(
        split_kernel,
        in_specs=[SMEM, HBM],
        out_specs=VMEM,
        out_shape=jax.ShapeDtypeStruct((4, QUARTER, HALF), jnp.bfloat16),
        scratch_shapes=[pltpu.SemaphoreType.DMA((4,))],
        cost_estimate=cost(0, 4_718_592),
        compiler_params=params(50),
        name="split",
    )(at, weights)


def back_kernel(at_ref, own_ref, oth_ref, w_ref, theirs_ref, out_ref, g_ref, held_ref, sems):
    core = at_ref[1]
    copies = []
    for q in range(4):
        columns = pl.ds(pl.multiple_of((2 * q + core) * HALF, 128), HALF)
        copies.append(pltpu.make_async_copy(w_ref.at[:, columns], held_ref.at[q], sems.at[q]))
    for q in range(4):
        copies.append(pltpu.make_async_copy(theirs_ref.at[q], held_ref.at[4 + q], sems.at[4 + q]))
    for copy in copies:
        copy.start()
    g_ref[:, half(core)] = own_ref[...]
    g_ref[:, half(1 - core)] = oth_ref[...]
    for q in range(8):
        copies[q].wait()
        block = core if q < 4 else 1 - core
        out_ref[block * 4 + q % 4] = jnp.dot(
            g_ref[...], held_ref[q], preferred_element_type=jnp.float32
        ).astype(jnp.bfloat16)


def back(at, own, oth, weights, theirs):
    return pl.pallas_call(
        back_kernel,
        in_specs=[SMEM, VMEM, VMEM, HBM, HBM],
        out_specs=VMEM,
        out_shape=jax.ShapeDtypeStruct((8, TRIALS, HALF), jnp.bfloat16),
        scratch_shapes=[
            pltpu.VMEM((TRIALS, QUARTER), jnp.bfloat16),
            pltpu.VMEM((8, QUARTER, HALF), jnp.bfloat16),
            pltpu.SemaphoreType.DMA((8,)),
        ],
        cost_estimate=cost(2 * TRIALS * QUARTER * COLS, 6_000_000),
        compiler_params=params(48),
        name="back",
    )(at, own, oth, weights, theirs)


TILE = 1024


def gather_rows(core, pairs, g_ref):
    for t, (own_ref, oth_ref) in enumerate(pairs):
        for ref, part in ((own_ref, core), (oth_ref, 1 - core)):
            rows = pl.ds(pl.multiple_of(part * HALF, 16), HALF)
            g_ref[rows, t * TRIALS : (t + 1) * TRIALS] = ref[...].T


def early_kernel(at_ref, o3, o2, o1, p3, p2, p1, rates_ref, acc_ref, g_ref):
    j = pl.program_id(0)

    @pl.when(j == 0)
    def _():
        gather_rows(at_ref[1], ((o1, p1), (o2, p2), (o3, p3)), g_ref)

    before = jnp.concatenate([rates_ref[t] for t in range(1, STEPS)], axis=1)
    acc_ref[...] = lax.dot_general(
        g_ref[...], before, (((1,), (1,)), ((), ())), preferred_element_type=jnp.float32
    ).astype(jnp.bfloat16)


def early(at, owns, oths, rates):
    return pl.pallas_call(
        early_kernel,
        grid_spec=pltpu.PrefetchScalarGridSpec(
            num_scalar_prefetch=1,
            grid=(COLS // TILE,),
            in_specs=[VMEM] * 6 + [pl.BlockSpec((STEPS, TILE, TRIALS), lambda j, at: (0, j, 0))],
            out_specs=pl.BlockSpec((QUARTER, TILE), lambda j, at: (0, j)),
            scratch_shapes=[pltpu.VMEM((QUARTER, 3 * TRIALS), jnp.bfloat16)],
        ),
        out_shape=jax.ShapeDtypeStruct((QUARTER, COLS), jnp.bfloat16),
        cost_estimate=cost(2 * 3 * TRIALS * QUARTER * COLS, 10_000_000),
        compiler_params=params(50),
        name="early",
    )(at, *owns, *oths, rates)


def final_kernel(at_ref, own_ref, oth_ref, acc_ref, rates_ref, out_ref, g_ref):
    j = pl.program_id(0)

    @pl.when(j == 0)
    def _():
        gather_rows(at_ref[1], ((own_ref, oth_ref),), g_ref)

    out_ref[...] = (
        acc_ref[...].astype(jnp.float32)
        + lax.dot_general(
            g_ref[...], rates_ref[0], (((1,), (1,)), ((), ())), preferred_element_type=jnp.float32
        )
    ).astype(jnp.bfloat16)


def final(at, own, oth, acc, rates):
    return pl.pallas_call(
        final_kernel,
        grid_spec=pltpu.PrefetchScalarGridSpec(
            num_scalar_prefetch=1,
            grid=(COLS // TILE,),
            in_specs=[VMEM] * 2
            + [
                pl.BlockSpec((QUARTER, TILE), lambda j, at: (0, j)),
                pl.BlockSpec((1, TILE, TRIALS), lambda j, at: (0, j, 0)),
            ],
            out_specs=pl.BlockSpec((QUARTER, TILE), lambda j, at: (0, j)),
            scratch_shapes=[pltpu.VMEM((QUARTER, TRIALS), jnp.bfloat16)],
        ),
        out_shape=jax.ShapeDtypeStruct((QUARTER, COLS), jnp.bfloat16),
        cost_estimate=cost(2 * TRIALS * QUARTER * COLS, 11_000_000),
        compiler_params=params(52),
        name="final",
    )(at, own, oth, acc, rates)


def whole(weights, rates):
    y, z, x, core = (lax.axis_index(a) for a in EVERY)
    at = jnp.stack([z % 4, core]).astype(jnp.int32)
    is_root_core = core == z // 4

    def at_core(mine, theirs):
        return jnp.where(is_root_core, mine, lax.ppermute(theirs, "core", SWAP))

    def along_x(root):
        parts = [lax.ppermute(root, EVERY, from_root(shift)) for shift in (1, 2, 3)]
        return jnp.where(x == y, root, parts[0] + parts[1] + parts[2])

    root = at_core(*first(at, rates))
    own = along_x(root)
    theirs = split(at, lax.optimization_barrier((weights, root))[0])
    theirs = lax.ppermute(theirs, "core", SWAP)
    oth = lax.ppermute(own, "core", SWAP)
    owns, oths = [own], [oth]
    row_rates = None
    for step in range(STEPS - 1, 0, -1):
        shares = back(at, own, oth, weights, theirs)
        if row_rates is None:
            shares, later = lax.optimization_barrier((shares, rates[1:STEPS]))
            later = lax.dynamic_slice_in_dim(later, z % 4 * QUARTER, QUARTER, 1)
            halves = jnp.swapaxes(later.reshape(3, 2, HALF, TRIALS), 2, 3)
            halves = [
                lax.dynamic_index_in_dim(halves, part, 1, keepdims=False)
                for part in (core, 1 - core)
            ]
            row_rates = along_x(at_core(*halves))
        if step == 1:
            shares, owns, oths = lax.optimization_barrier((shares, owns, oths))
            acc = early(at, owns, oths, rates)
        parts = lax.all_to_all(shares, "z", 0, 0, tiled=True)
        summed = jnp.sum(parts.astype(jnp.float32), axis=0).astype(jnp.bfloat16)
        if step == 1:
            summed, acc = lax.optimization_barrier((summed, acc))
        adjoint = sum(
            lax.ppermute(summed, EVERY, across(shift)).astype(jnp.float32) for shift in range(X)
        )
        rate = row_rates[step - 1].astype(jnp.float32)
        own = (adjoint * (1.0 - rate * rate)).astype(jnp.bfloat16)
        oth = lax.ppermute(own, "core", SWAP)
        owns.append(own)
        oths.append(oth)
    return final(at, own, oth, acc, rates)


def solution(mesh):
    fine = Mesh(mesh.devices.reshape(Y, Z, X, C), EVERY)
    in_specs = (P(("y", "z"), ("x", "core")), P(None, ("x", "core"), None))
    out_specs = P(("y", "z"), ("x", "core"))
    return jax.shard_map(whole, mesh=fine, in_specs=in_specs, out_specs=out_specs, check_vma=False)
```

profile of v0, /device:TPU:7, one launch (start us, length us, event | category | flops | bytes accessed | tf_op | source)
XLA Modules:
  0.0 180.9 jit_solution(7923026442455807629)
XLA Ops:
  3.5 3.6 %split.1 = bf16[4,768,384]{2,1,0:T(8,128)(2,1)} custom-call(s32[2]{0:T(128)S(1)} %pad_add_fusion.at_ref, bf16[768,3072]{1,0:T(8,128)(2,1)} %w_ref.6), custom_call_target="tpu_custom_call" | custom-call | bytes 4718592 | tf_op jit(solution)/shard_map/split/pallas_call | solution.py:99
  10.2 4.6 %collective-permute-done.3 = bf16[128,384]{1,0:T(8,128)(2,1)S(1)} collective-permute-done((bf16[128,384]{1,0:T(8,128)(2,1)S(1)}, bf16[128,384]{1,0:T(8,128)(2,1)S(1)}, u32[]{:S(2)}, u32[]{:S(2)}) %collective-permute-start.3) | collective-permute-done | bytes 98336 | tf_op jit(solution)/shard_map/ppermute | solution.py:233
  16.0 3.3 %slice.12 = bf16[3,3072,128]{2,1,0:T(8,128)(2,1)} slice(bf16[5,3072,128]{2,1,0:T(8,128)(2,1)} %rates_ref.5), slice={[1:4], [0:3072], [0:128]} | slice | bytes 4718592 | tf_op jit(solution)/shard_map/slice | solution.py:246
  19.3 4.7 %back.3 = bf16[8,128,384]{2,1,0:T(8,128)(2,1)} custom-call(s32[2]{0:T(128)S(1)} %pad_add_fusion.at_ref, bf16[128,384]{1,0:T(8,128)(2,1)S(1)} %add_select_fusion.1.own_ref.o3, bf16[128,384]{1,0:T(8,128)(2,1)S(1)} %collective-permute-done.4.oth_ref.p3, bf16[768,3072]{1,0:T(8,128)(2,1)} %w_ref.6, bf16[4,768,384]{2,1,0:T(8,128)(2,1)S(1)} %collective-permute-done.5.theirs_ref), custom_call_target="tpu_custom_call" | custom-call | flops 603979776 | bytes 6000000 | tf_op jit(solution)/shard_map/back/pallas_call | solution.py:132
  24.0 8.2 %all-to-all-start = ((bf16[8,128,384]{2,1,0:T(8,128)(2,1)}), bf16[8,128,384]{2,1,0:T(8,128)(2,1)S(1)}, u32[]{:S(2)}, u32[]{:S(2)}) async-start(bf16[8,128,384]{2,1,0:T(8,128)(2,1)} %back.3), calls=%async_computation | async-start | bytes 1572864 | tf_op jit(solution)/shard_map/all_to_all | solution.py:257
  36.3 1.9 %copy.5 = bf16[3,1,384,128]{2,3,0,1:T(8,128)(2,1)} copy(bf16[3,1,384,128]{3,2,1,0:T(8,128)(2,1)} %get-tuple-element.33) | data formatting | bytes 589824
  44.1 11.8 %all-to-all-done = bf16[8,128,384]{2,1,0:T(8,128)(2,1)S(1)} async-done(((bf16[8,128,384]{2,1,0:T(8,128)(2,1)}), bf16[8,128,384]{2,1,0:T(8,128)(2,1)S(1)}, u32[]{:S(2)}, u32[]{:S(2)}) %all-to-all-start) | async-done | bytes 786464 | tf_op jit(solution)/shard_map/all_to_all | solution.py:257
  56.0 2.5 %collective-permute-start.9 = (bf16[128,384]{1,0:T(8,128)(2,1)S(1)}, bf16[128,384]{1,0:T(8,128)(2,1)S(1)}, u32[]{:S(2)}, u32[]{:S(2)}) collective-permute-start(bf16[128,384]{1,0:T(8,128)(2,1)S(1)} %reduce_sum.36), channel_id=1, source_target_pairs={{0,6},{1,7},{2,70},{3,71},{4,134},{5,135},{6,198},{7,199},{8,14},{... | collective-permute-start | bytes 294920 | tf_op jit(solution)/shard_map/ppermute | solution.py:262
  59.7 3.2 %collective-permute-start.7 = (bf16[128,384]{1,0:T(8,128)(2,1)S(1)}, bf16[128,384]{1,0:T(8,128)(2,1)S(1)}, u32[]{:S(2)}, u32[]{:S(2)}) collective-permute-start(bf16[128,384]{1,0:T(8,128)(2,1)S(1)} %reduce_sum.36), channel_id=1, source_target_pairs={{0,2},{1,3},{2,66},{3,67},{4,130},{5,131},{6,194},{7,195},{8,10},{... | collective-permute-start | bytes 294920 | tf_op jit(solution)/shard_map/ppermute | solution.py:262
  62.9 5.5 %collective-permute-start.6 = (bf16[128,384]{1,0:T(8,128)(2,1)S(1)}, bf16[128,384]{1,0:T(8,128)(2,1)S(1)}, u32[]{:S(2)}, u32[]{:S(2)}) collective-permute-start(bf16[128,384]{1,0:T(8,128)(2,1)S(1)} %reduce_sum.36), channel_id=1, source_target_pairs={{0,0},{1,1},{2,64},{3,65},{4,128},{5,129},{6,192},{7,193},{8,8},{9... | collective-permute-start | bytes 294920 | tf_op jit(solution)/shard_map/ppermute | solution.py:262
  69.6 4.6 %collective-permute-done.6 = bf16[128,384]{1,0:T(8,128)(2,1)S(1)} collective-permute-done((bf16[128,384]{1,0:T(8,128)(2,1)S(1)}, bf16[128,384]{1,0:T(8,128)(2,1)S(1)}, u32[]{:S(2)}, u32[]{:S(2)}) %collective-permute-start.6) | collective-permute-done | bytes 98336 | tf_op jit(solution)/shard_map/ppermute | solution.py:262
  75.9 3.8 %back.4 = bf16[8,128,384]{2,1,0:T(8,128)(2,1)S(1)} custom-call(s32[2]{0:T(128)S(1)} %pad_add_fusion.at_ref, bf16[128,384]{1,0:T(8,128)(2,1)S(1)} %fusion.2.own_ref.o2, bf16[128,384]{1,0:T(8,128)(2,1)S(1)} %collective-permute-done.14.oth_ref.p2, bf16[768,3072]{1,0:T(8,128)(2,1)} %w_ref.6, bf16[4,768,384]{2,1,0:T(8,128)(2,1)S(1)} %collective-permute-done.5.theirs_ref), custom_call_target="tpu_custom_call" | custom-call | flops 603979776 | bytes 6000000 | tf_op jit(solution)/shard_map/back/pallas_call | solution.py:132
  79.7 26.0 %all_to_all.15 = bf16[8,128,384]{2,1,0:T(8,128)(2,1)S(1)} all-to-all(bf16[8,128,384]{2,1,0:T(8,128)(2,1)S(1)} %back.4), channel_id=1, replica_groups=mesh['y'=4,'z'=8,'x'=4,'core'=2] {'z'}, dimensions={0} | all-to-all | bytes 1572864 | tf_op jit(solution)/shard_map/all_to_all | solution.py:257
  106.5 3.1 %collective-permute-start.16 = (bf16[128,384]{1,0:T(8,128)(2,1)}, bf16[128,384]{1,0:T(8,128)(2,1)S(1)}, u32[]{:S(2)}, u32[]{:S(2)}) collective-permute-start(bf16[128,384]{1,0:T(8,128)(2,1)} %reduce_sum.37), channel_id=1, source_target_pairs={{0,2},{1,3},{2,66},{3,67},{4,130},{5,131},{6,194},{7,195},{8,10},{... | collective-permute-start | bytes 294920 | tf_op jit(solution)/shard_map/ppermute | solution.py:262
  109.6 4.0 %collective-permute-start.15 = (bf16[128,384]{1,0:T(8,128)(2,1)}, bf16[128,384]{1,0:T(8,128)(2,1)S(1)}, u32[]{:S(2)}, u32[]{:S(2)}) collective-permute-start(bf16[128,384]{1,0:T(8,128)(2,1)} %reduce_sum.37), channel_id=1, source_target_pairs={{0,0},{1,1},{2,64},{3,65},{4,128},{5,129},{6,192},{7,193},{8,8},{9... | collective-permute-start | bytes 294920 | tf_op jit(solution)/shard_map/ppermute | solution.py:262
  114.3 6.9 %collective-permute-done.15 = bf16[128,384]{1,0:T(8,128)(2,1)S(1)} collective-permute-done((bf16[128,384]{1,0:T(8,128)(2,1)}, bf16[128,384]{1,0:T(8,128)(2,1)S(1)}, u32[]{:S(2)}, u32[]{:S(2)}) %collective-permute-start.15) | collective-permute-done | bytes 98336 | tf_op jit(solution)/shard_map/ppermute | solution.py:262
  124.3 4.7 %back.5 = bf16[8,128,384]{2,1,0:T(8,128)(2,1)} custom-call(s32[2]{0:T(128)S(1)} %pad_add_fusion.at_ref, bf16[128,384]{1,0:T(8,128)(2,1)S(1)} %fusion.1.own_ref.o1, bf16[128,384]{1,0:T(8,128)(2,1)S(1)} %collective-permute-done.19.oth_ref.p1, bf16[768,3072]{1,0:T(8,128)(2,1)} %w_ref.6, bf16[4,768,384]{2,1,0:T(8,128)(2,1)S(1)} %collective-permute-done.5.theirs_ref), custom_call_target="tpu_custom_call" | custom-call | flops 603979776 | bytes 6000000 | tf_op jit(solution)/shard_map/back/pallas_call | solution.py:132
  129.1 3.6 %all-to-all-start.2 = ((bf16[8,128,384]{2,1,0:T(8,128)(2,1)}), bf16[8,128,384]{2,1,0:T(8,128)(2,1)S(1)}, u32[]{:S(2)}, u32[]{:S(2)}) async-start(bf16[8,128,384]{2,1,0:T(8,128)(2,1)} %back.5), calls=%async_computation.2 | async-start | bytes 1572864 | tf_op jit(solution)/shard_map/all_to_all | solution.py:257
  132.6 7.0 %early.1.acc_ref = bf16[768,3072]{1,0:T(8,128)(2,1)} custom-call(s32[2]{0:T(128)S(1)} %pad_add_fusion.at_ref, bf16[128,384]{1,0:T(8,128)(2,1)S(1)} %add_select_fusion.1.own_ref.o3, bf16[128,384]{1,0:T(8,128)(2,1)S(1)} %fusion.2.own_ref.o2, bf16[128,384]{1,0:T(8,128)(2,1)S(1)} %fusion.1.own_ref.o1, bf16[128,384]{1,0:T(8,128)(2,1)S(1)} %collective-permute-done.4.oth_ref.p3, ...), custom_call_target="tpu_custom_call" | custom-call | flops 1811939328 | bytes 10000000 | tf_op jit(solution)/shard_map/early/pallas_call | solution.py:172
  139.7 16.5 %all-to-all-done.2 = bf16[8,128,384]{2,1,0:T(8,128)(2,1)S(1)} async-done(((bf16[8,128,384]{2,1,0:T(8,128)(2,1)}), bf16[8,128,384]{2,1,0:T(8,128)(2,1)S(1)}, u32[]{:S(2)}, u32[]{:S(2)}) %all-to-all-start.2) | async-done | bytes 786464 | tf_op jit(solution)/shard_map/all_to_all | solution.py:257
  156.5 3.4 %collective-permute-start.21 = (bf16[128,384]{1,0:T(8,128)(2,1)S(1)}, bf16[128,384]{1,0:T(8,128)(2,1)S(1)}, u32[]{:S(2)}, u32[]{:S(2)}) collective-permute-start(bf16[128,384]{1,0:T(8,128)(2,1)S(1)} %reduce_sum.38), channel_id=1, source_target_pairs={{0,2},{1,3},{2,66},{3,67},{4,130},{5,131},{6,194},{7,195},{8,10},{... | collective-permute-start | bytes 294920 | tf_op jit(solution)/shard_map/ppermute | solution.py:262
  159.9 3.4 %collective-permute-start.20 = (bf16[128,384]{1,0:T(8,128)(2,1)S(1)}, bf16[128,384]{1,0:T(8,128)(2,1)S(1)}, u32[]{:S(2)}, u32[]{:S(2)}) collective-permute-start(bf16[128,384]{1,0:T(8,128)(2,1)S(1)} %reduce_sum.38), channel_id=1, source_target_pairs={{0,0},{1,1},{2,64},{3,65},{4,128},{5,129},{6,192},{7,193},{8,8},{9... | collective-permute-start | bytes 294920 | tf_op jit(solution)/shard_map/ppermute | solution.py:262
  164.0 7.1 %collective-permute-done.20 = bf16[128,384]{1,0:T(8,128)(2,1)S(1)} collective-permute-done((bf16[128,384]{1,0:T(8,128)(2,1)S(1)}, bf16[128,384]{1,0:T(8,128)(2,1)S(1)}, u32[]{:S(2)}, u32[]{:S(2)}) %collective-permute-start.20) | collective-permute-done | bytes 98336 | tf_op jit(solution)/shard_map/ppermute | solution.py:262
  173.9 7.0 %final.1 = bf16[768,3072]{1,0:T(8,128)(2,1)} custom-call(s32[2]{0:T(128)S(1)} %pad_add_fusion.at_ref, bf16[128,384]{1,0:T(8,128)(2,1)S(1)} %fusion.own_ref, bf16[128,384]{1,0:T(8,128)(2,1)S(1)} %collective-permute-done.24.oth_ref, bf16[768,3072]{1,0:T(8,128)(2,1)} %early.1.acc_ref, bf16[5,3072,128]{2,1,0:T(8,128)(2,1)} %rates_ref.5), custom_call_target="tpu_custom_call" | custom-call | flops 603979776 | bytes 11000000 | tf_op jit(solution)/shard_map/final/pallas_call | solution.py:204
  (56 shorter events, 30.3 us)
Async XLA Ops:
  7.1 12.1 %collective-permute-start.5 = (bf16[4,768,384]{2,1,0:T(8,128)(2,1)}, bf16[4,768,384]{2,1,0:T(8,128)(2,1)S(1)}, u32[]{:S(2)}, u32[]{:S(2)}) collective-permute-start(bf16[4,768,384]{2,1,0:T(8,128)(2,1)} %split.1), channel_id=1, source_target_pairs={{0,1},{1,0},{2,3},{3,2},{4,5},{5,4},{6,7},{7,6},{8,9},{9,8},{10,11... | collective-permute-start | bytes 7077896 | tf_op jit(solution)/shard_map/ppermute | solution.py:239
  7.6 7.3 %collective-permute-start.3 = (bf16[128,384]{1,0:T(8,128)(2,1)S(1)}, bf16[128,384]{1,0:T(8,128)(2,1)S(1)}, u32[]{:S(2)}, u32[]{:S(2)}) collective-permute-start(bf16[128,384]{1,0:T(8,128)(2,1)S(1)} %broadcast_select_fusion), channel_id=1, source_target_pairs={{0,6},{1,7},{8,14},{9,15},{16,22},{17,23},{24,30},{25,31},{32,38},... | collective-permute-start | bytes 294920 | tf_op jit(solution)/shard_map/ppermute | solution.py:233
  8.9 6.0 %collective-permute-start.2 = (bf16[128,384]{1,0:T(8,128)(2,1)S(1)}, bf16[128,384]{1,0:T(8,128)(2,1)S(1)}, u32[]{:S(2)}, u32[]{:S(2)}) collective-permute-start(bf16[128,384]{1,0:T(8,128)(2,1)S(1)} %broadcast_select_fusion), channel_id=1, source_target_pairs={{0,4},{1,5},{8,12},{9,13},{16,20},{17,21},{24,28},{25,29},{32,36},... | collective-permute-start | bytes 294920 | tf_op jit(solution)/shard_map/ppermute | solution.py:233
  9.5 5.3 %collective-permute-start.1 = (bf16[128,384]{1,0:T(8,128)(2,1)S(1)}, bf16[128,384]{1,0:T(8,128)(2,1)S(1)}, u32[]{:S(2)}, u32[]{:S(2)}) collective-permute-start(bf16[128,384]{1,0:T(8,128)(2,1)S(1)} %broadcast_select_fusion), channel_id=1, source_target_pairs={{0,2},{1,3},{8,10},{9,11},{16,18},{17,19},{24,26},{25,27},{32,34},... | collective-permute-start | bytes 294920 | tf_op jit(solution)/shard_map/ppermute | solution.py:233
  14.9 4.4 %collective-permute-start.4 = (bf16[128,384]{1,0:T(8,128)(2,1)S(1)}, bf16[128,384]{1,0:T(8,128)(2,1)S(1)}, u32[]{:S(2)}, u32[]{:S(2)}) collective-permute-start(bf16[128,384]{1,0:T(8,128)(2,1)S(1)} %add_select_fusion.1.own_ref.o3), channel_id=1, source_target_pairs={{0,1},{1,0},{2,3},{3,2},{4,5},{5,4},{6,7},{7,6},{8,9},{9,8},{10,11... | collective-permute-start | bytes 294920 | tf_op jit(solution)/shard_map/ppermute | solution.py:240
  24.0 31.8 %all-to-all-start = ((bf16[8,128,384]{2,1,0:T(8,128)(2,1)}), bf16[8,128,384]{2,1,0:T(8,128)(2,1)S(1)}, u32[]{:S(2)}, u32[]{:S(2)}) async-start(bf16[8,128,384]{2,1,0:T(8,128)(2,1)} %back.3), calls=%async_computation | async-start | bytes 1572864 | tf_op jit(solution)/shard_map/all_to_all | solution.py:257
  36.0 2.2 %collective-permute-start.10 = (bf16[3,128,384]{2,1,0:T(8,128)(2,1)}, bf16[3,128,384]{2,1,0:T(8,128)(2,1)}, u32[]{:S(2)}, u32[]{:S(2)}) collective-permute-start(bf16[3,128,384]{2,1,0:T(8,128)(2,1)} %bitcast.23), channel_id=1, source_target_pairs={{0,1},{1,0},{2,3},{3,2},{4,5},{5,4},{6,7},{7,6},{8,9},{9,8},{10,11... | collective-permute-start | bytes 884744 | tf_op jit(solution)/shard_map/ppermute | solution.py:230
  40.0 19.7 %collective-permute-start.13 = (bf16[3,128,384]{2,1,0:T(8,128)(2,1)}, bf16[3,128,384]{2,1,0:T(8,128)(2,1)}, u32[]{:S(2)}, u32[]{:S(2)}) collective-permute-start(bf16[3,128,384]{2,1,0:T(8,128)(2,1)} %bitcast_select_fusion), channel_id=1, source_target_pairs={{0,6},{1,7},{8,14},{9,15},{16,22},{17,23},{24,30},{25,31},{32,38},... | collective-permute-start | bytes 884744 | tf_op jit(solution)/shard_map/ppermute | solution.py:233
  41.3 21.6 %collective-permute-start.12 = (bf16[3,128,384]{2,1,0:T(8,128)(2,1)}, bf16[3,128,384]{2,1,0:T(8,128)(2,1)}, u32[]{:S(2)}, u32[]{:S(2)}) collective-permute-start(bf16[3,128,384]{2,1,0:T(8,128)(2,1)} %bitcast_select_fusion), channel_id=1, source_target_pairs={{0,4},{1,5},{8,12},{9,13},{16,20},{17,21},{24,28},{25,29},{32,36},... | collective-permute-start | bytes 884744 | tf_op jit(solution)/shard_map/ppermute | solution.py:233
  42.7 25.6 %collective-permute-start.11 = (bf16[3,128,384]{2,1,0:T(8,128)(2,1)}, bf16[3,128,384]{2,1,0:T(8,128)(2,1)}, u32[]{:S(2)}, u32[]{:S(2)}) collective-permute-start(bf16[3,128,384]{2,1,0:T(8,128)(2,1)} %bitcast_select_fusion), channel_id=1, source_target_pairs={{0,2},{1,3},{8,10},{9,11},{16,18},{17,19},{24,26},{25,27},{32,34},... | collective-permute-start | bytes 884744 | tf_op jit(solution)/shard_map/ppermute | solution.py:233
  56.0 13.6 %collective-permute-start.9 = (bf16[128,384]{1,0:T(8,128)(2,1)S(1)}, bf16[128,384]{1,0:T(8,128)(2,1)S(1)}, u32[]{:S(2)}, u32[]{:S(2)}) collective-permute-start(bf16[128,384]{1,0:T(8,128)(2,1)S(1)} %reduce_sum.36), channel_id=1, source_target_pairs={{0,6},{1,7},{2,70},{3,71},{4,134},{5,135},{6,198},{7,199},{8,14},{... | collective-permute-start | bytes 294920 | tf_op jit(solution)/shard_map/ppermute | solution.py:262
  58.5 11.1 %collective-permute-start.8 = (bf16[128,384]{1,0:T(8,128)(2,1)S(1)}, bf16[128,384]{1,0:T(8,128)(2,1)S(1)}, u32[]{:S(2)}, u32[]{:S(2)}) collective-permute-start(bf16[128,384]{1,0:T(8,128)(2,1)S(1)} %reduce_sum.36), channel_id=1, source_target_pairs={{0,4},{1,5},{2,68},{3,69},{4,132},{5,133},{6,196},{7,197},{8,12},{... | collective-permute-start | bytes 294920 | tf_op jit(solution)/shard_map/ppermute | solution.py:262
  59.7 9.9 %collective-permute-start.7 = (bf16[128,384]{1,0:T(8,128)(2,1)S(1)}, bf16[128,384]{1,0:T(8,128)(2,1)S(1)}, u32[]{:S(2)}, u32[]{:S(2)}) collective-permute-start(bf16[128,384]{1,0:T(8,128)(2,1)S(1)} %reduce_sum.36), channel_id=1, source_target_pairs={{0,2},{1,3},{2,66},{3,67},{4,130},{5,131},{6,194},{7,195},{8,10},{... | collective-permute-start | bytes 294920 | tf_op jit(solution)/shard_map/ppermute | solution.py:262
  62.9 11.3 %collective-permute-start.6 = (bf16[128,384]{1,0:T(8,128)(2,1)S(1)}, bf16[128,384]{1,0:T(8,128)(2,1)S(1)}, u32[]{:S(2)}, u32[]{:S(2)}) collective-permute-start(bf16[128,384]{1,0:T(8,128)(2,1)S(1)} %reduce_sum.36), channel_id=1, source_target_pairs={{0,0},{1,1},{2,64},{3,65},{4,128},{5,129},{6,192},{7,193},{8,8},{9... | collective-permute-start | bytes 294920 | tf_op jit(solution)/shard_map/ppermute | solution.py:262
  106.5 7.8 %collective-permute-start.18 = (bf16[128,384]{1,0:T(8,128)(2,1)}, bf16[128,384]{1,0:T(8,128)(2,1)S(1)}, u32[]{:S(2)}, u32[]{:S(2)}) collective-permute-start(bf16[128,384]{1,0:T(8,128)(2,1)} %reduce_sum.37), channel_id=1, source_target_pairs={{0,6},{1,7},{2,70},{3,71},{4,134},{5,135},{6,198},{7,199},{8,14},{... | collective-permute-start | bytes 294920 | tf_op jit(solution)/shard_map/ppermute | solution.py:262
  106.5 7.8 %collective-permute-start.17 = (bf16[128,384]{1,0:T(8,128)(2,1)}, bf16[128,384]{1,0:T(8,128)(2,1)S(1)}, u32[]{:S(2)}, u32[]{:S(2)}) collective-permute-start(bf16[128,384]{1,0:T(8,128)(2,1)} %reduce_sum.37), channel_id=1, source_target_pairs={{0,4},{1,5},{2,68},{3,69},{4,132},{5,133},{6,196},{7,197},{8,12},{... | collective-permute-start | bytes 294920 | tf_op jit(solution)/shard_map/ppermute | solution.py:262
  106.5 7.8 %collective-permute-start.16 = (bf16[128,384]{1,0:T(8,128)(2,1)}, bf16[128,384]{1,0:T(8,128)(2,1)S(1)}, u32[]{:S(2)}, u32[]{:S(2)}) collective-permute-start(bf16[128,384]{1,0:T(8,128)(2,1)} %reduce_sum.37), channel_id=1, source_target_pairs={{0,2},{1,3},{2,66},{3,67},{4,130},{5,131},{6,194},{7,195},{8,10},{... | collective-permute-start | bytes 294920 | tf_op jit(solution)/shard_map/ppermute | solution.py:262
  109.6 11.6 %collective-permute-start.15 = (bf16[128,384]{1,0:T(8,128)(2,1)}, bf16[128,384]{1,0:T(8,128)(2,1)S(1)}, u32[]{:S(2)}, u32[]{:S(2)}) collective-permute-start(bf16[128,384]{1,0:T(8,128)(2,1)} %reduce_sum.37), channel_id=1, source_target_pairs={{0,0},{1,1},{2,64},{3,65},{4,128},{5,129},{6,192},{7,193},{8,8},{9... | collective-permute-start | bytes 294920 | tf_op jit(solution)/shard_map/ppermute | solution.py:262
  122.2 2.2 %collective-permute-start.19 = (bf16[128,384]{1,0:T(8,128)(2,1)S(1)}, bf16[128,384]{1,0:T(8,128)(2,1)S(1)}, u32[]{:S(2)}, u32[]{:S(2)}) collective-permute-start(bf16[128,384]{1,0:T(8,128)(2,1)S(1)} %fusion.1.own_ref.o1), channel_id=1, source_target_pairs={{0,1},{1,0},{2,3},{3,2},{4,5},{5,4},{6,7},{7,6},{8,9},{9,8},{10,11... | collective-permute-start | bytes 294920 | tf_op jit(solution)/shard_map/ppermute | solution.py:266
  129.1 27.1 %all-to-all-start.2 = ((bf16[8,128,384]{2,1,0:T(8,128)(2,1)}), bf16[8,128,384]{2,1,0:T(8,128)(2,1)S(1)}, u32[]{:S(2)}, u32[]{:S(2)}) async-start(bf16[8,128,384]{2,1,0:T(8,128)(2,1)} %back.5), calls=%async_computation.2 | async-start | bytes 1572864 | tf_op jit(solution)/shard_map/all_to_all | solution.py:257
  156.3 7.7 %collective-permute-start.23 = (bf16[128,384]{1,0:T(8,128)(2,1)S(1)}, bf16[128,384]{1,0:T(8,128)(2,1)S(1)}, u32[]{:S(2)}, u32[]{:S(2)}) collective-permute-start(bf16[128,384]{1,0:T(8,128)(2,1)S(1)} %reduce_sum.38), channel_id=1, source_target_pairs={{0,6},{1,7},{2,70},{3,71},{4,134},{5,135},{6,198},{7,199},{8,14},{... | collective-permute-start | bytes 294920 | tf_op jit(solution)/shard_map/ppermute | solution.py:262
  156.4 7.6 %collective-permute-start.22 = (bf16[128,384]{1,0:T(8,128)(2,1)S(1)}, bf16[128,384]{1,0:T(8,128)(2,1)S(1)}, u32[]{:S(2)}, u32[]{:S(2)}) collective-permute-start(bf16[128,384]{1,0:T(8,128)(2,1)S(1)} %reduce_sum.38), channel_id=1, source_target_pairs={{0,4},{1,5},{2,68},{3,69},{4,132},{5,133},{6,196},{7,197},{8,12},{... | collective-permute-start | bytes 294920 | tf_op jit(solution)/shard_map/ppermute | solution.py:262
  156.5 7.5 %collective-permute-start.21 = (bf16[128,384]{1,0:T(8,128)(2,1)S(1)}, bf16[128,384]{1,0:T(8,128)(2,1)S(1)}, u32[]{:S(2)}, u32[]{:S(2)}) collective-permute-start(bf16[128,384]{1,0:T(8,128)(2,1)S(1)} %reduce_sum.38), channel_id=1, source_target_pairs={{0,2},{1,3},{2,66},{3,67},{4,130},{5,131},{6,194},{7,195},{8,10},{... | collective-permute-start | bytes 294920 | tf_op jit(solution)/shard_map/ppermute | solution.py:262
  159.9 11.2 %collective-permute-start.20 = (bf16[128,384]{1,0:T(8,128)(2,1)S(1)}, bf16[128,384]{1,0:T(8,128)(2,1)S(1)}, u32[]{:S(2)}, u32[]{:S(2)}) collective-permute-start(bf16[128,384]{1,0:T(8,128)(2,1)S(1)} %reduce_sum.38), channel_id=1, source_target_pairs={{0,0},{1,1},{2,64},{3,65},{4,128},{5,129},{6,192},{7,193},{8,8},{9... | collective-permute-start | bytes 294920 | tf_op jit(solution)/shard_map/ppermute | solution.py:262
  (4 other events, 10.5 us)
where the time goes:
time: 182 us; the launch traced here: 181 us
  waiting for transfers between devices  56.7 us (31%)
  starting transfers between devices  50.3 us (28%)
  Pallas kernels  32.6 us (18%)
  blocking collectives  26 us (14%)
  local copies, waits for them, and re-layouts  8.97 us (5%)
  other arithmetic  6.16 us (3%)
    all_to_all x2, waiting for transfers between devices, whole(): parts = lax.all_to_all(shares, 'z', 0, 0, tiled=True)  28.3 us
    ppermute x12, starting transfers between devices, whole(): lax.ppermute(summed, EVERY, across(shift)).astype(jnp.float32)  26.5 us
    all_to_all x1, blocking collectives, whole(): parts = lax.all_to_all(shares, 'z', 0, 0, tiled=True)  26 us
    ppermute x12, waiting for transfers between devices, whole(): lax.ppermute(summed, EVERY, across(shift)).astype(jnp.float32)  20 us
    pallas_call x3, Pallas kernels, back(): pl.pallas_call(back_kernel, in_specs=[SMEM, VMEM, VMEM, HBM, HBM], out_sp...  13.3 us
    all_to_all x2, starting transfers between devices, whole(): parts = lax.all_to_all(shares, 'z', 0, 0, tiled=True)  11.8 us
    pallas_call x1, Pallas kernels, early(): pl.pallas_call(early_kernel, grid_spec=pltpu.PrefetchScalarGridSpec(num_s...  7.02 us
    pallas_call x1, Pallas kernels, final(): pl.pallas_call(final_kernel, grid_spec=pltpu.PrefetchScalarGridSpec(num_s...  6.95 us
  transfers between devices with their start and end apart: 27, of which 12 were waited for; matrix products, arithmetic and copies ran while one was open for 7% of the time, Pallas kernels for 4%

commit v1 on v0

v1 whole, which is shorter than its diff:
```python
import jax
import jax.numpy as jnp
from jax import lax
from jax.experimental import pallas as pl
from jax.experimental.pallas import tpu as pltpu
from jax.sharding import Mesh, PartitionSpec as P

STEPS = 4
Y, Z, X, C = 4, 8, 4, 2
EVERY = ("y", "z", "x", "core")
SWAP = [(0, 1), (1, 0)]
HALF = 384
QUARTER = 768
TRIALS = 128
SLICE = 32
SPLIT, ROWS, BACK, OUTER = 16, 16, 8, 52
COLS = 3072
VMEM = pl.BlockSpec(memory_space=pltpu.VMEM)
SMEM = pl.BlockSpec(memory_space=pltpu.SMEM)
HBM = pl.BlockSpec(memory_space=pltpu.HBM)


def flat(y, z, x, core):
    return ((y % Y * Z + z) * X + x % X) * C + core


def across(shift):
    return [
        (flat(y, z, x, core), flat(x, z, y + shift, core))
        for y in range(Y) for z in range(Z) for x in range(X) for core in range(C)
    ]


def from_root(shift):
    return [
        (flat(y, z, y, core), flat(y, z, y + shift, core))
        for y in range(Y) for z in range(Z) for core in range(C)
    ]


def params(mib):
    return pltpu.CompilerParams(vmem_limit_bytes=mib << 20)


def cost(flops, moved):
    return pl.CostEstimate(flops=flops, bytes_accessed=moved, transcendentals=0)


def half(core):
    return pl.ds(pl.multiple_of(core * HALF, 128), HALF)


def first_kernel(at_ref, rates_ref, mine_ref, theirs_ref, last_ref, zero_ref, sems):
    core = at_ref[1]
    rows = pl.ds(pl.multiple_of(at_ref[0] * QUARTER, 16), QUARTER)
    copies = [
        pltpu.make_async_copy(rates_ref.at[STEPS, rows], last_ref, sems.at[0]),
        pltpu.make_async_copy(rates_ref.at[0, rows], zero_ref, sems.at[1]),
    ]
    for copy in copies:
        copy.start()
    for copy in copies:
        copy.wait()
    for out_ref, part in ((theirs_ref, 1 - core), (mine_ref, core)):
        part = pl.ds(pl.multiple_of(part * HALF, 16), HALF)
        last = last_ref[part, :].astype(jnp.float32)
        zero = zero_ref[part, :].astype(jnp.float32)
        out_ref[...] = ((last - zero) * (1.0 - last * last)).astype(jnp.bfloat16).T


def first(at, rates):
    shape = jax.ShapeDtypeStruct((TRIALS, HALF), jnp.bfloat16)
    return pl.pallas_call(
        first_kernel,
        in_specs=[SMEM, HBM],
        out_specs=[VMEM, VMEM],
        out_shape=[shape, shape],
        scratch_shapes=[
            pltpu.VMEM((QUARTER, TRIALS), jnp.bfloat16),
            pltpu.VMEM((QUARTER, TRIALS), jnp.bfloat16),
            pltpu.SemaphoreType.DMA((2,)),
        ],
        compiler_params=params(52),
        name="first",
    )(at, rates)


def split_kernel(at_ref, w_ref, mine_ref, theirs_ref, sems):
    core = at_ref[1]
    copies = []
    for out_ref, part in ((theirs_ref, 1 - core), (mine_ref, core)):
        for q in range(4):
            columns = pl.ds(pl.multiple_of((2 * q + part) * HALF, 128), HALF)
            copies.append(
                pltpu.make_async_copy(w_ref.at[:, columns], out_ref.at[q], sems.at[len(copies)])
            )
    for copy in copies:
        copy.start()
    for copy in copies:
        copy.wait()


def split(at, weights):
    shape = jax.ShapeDtypeStruct((4, QUARTER, HALF), jnp.bfloat16)
    return pl.pallas_call(
        split_kernel,
        in_specs=[SMEM, HBM],
        out_specs=[VMEM, VMEM],
        out_shape=[shape, shape],
        scratch_shapes=[pltpu.SemaphoreType.DMA((8,))],
        cost_estimate=cost(0, 9_437_184),
        compiler_params=params(SPLIT),
        name="split",
    )(at, weights)


def rows_kernel(at_ref, rates_ref, mine_ref, theirs_ref, held_ref, turned_ref, sem):
    core = at_ref[1]
    rows = pl.ds(pl.multiple_of(at_ref[0] * QUARTER, 16), QUARTER)
    copy = pltpu.make_async_copy(rates_ref.at[1:STEPS, rows], held_ref, sem)
    copy.start()
    copy.wait()
    slot = pl.ds(pl.multiple_of(at_ref[2] * SLICE, SLICE), SLICE)
    for t in range(STEPS - 1):
        for out_ref, part in ((theirs_ref, 1 - core), (mine_ref, core)):
            turned_ref[...] = held_ref[t, pl.ds(pl.multiple_of(part * HALF, 16), HALF), :].T
            out_ref[t] = turned_ref[slot, :]


def rows(at, rates):
    shape = jax.ShapeDtypeStruct((STEPS - 1, SLICE, HALF), jnp.bfloat16)
    return pl.pallas_call(
        rows_kernel,
        in_specs=[SMEM, HBM],
        out_specs=[VMEM, VMEM],
        out_shape=[shape, shape],
        scratch_shapes=[
            pltpu.VMEM((STEPS - 1, QUARTER, TRIALS), jnp.bfloat16),
            pltpu.VMEM((TRIALS, HALF), jnp.bfloat16),
            pltpu.SemaphoreType.DMA,
        ],
        cost_estimate=cost(0, 600_000),
        compiler_params=params(ROWS),
        name="rows",
    )(at, rates)


def back_kernel(at_ref, own_ref, oth_ref, mine_ref, theirs_ref, out_ref, g_ref):
    core = at_ref[1]
    g_ref[:, half(core)] = own_ref[...]
    g_ref[:, half(1 - core)] = oth_ref[...]
    for ref, block in ((mine_ref, core), (theirs_ref, 1 - core)):
        for q in range(4):
            got = jnp.dot(g_ref[...], ref[q], preferred_element_type=jnp.float32)
            got = got.astype(jnp.bfloat16)
            for part in range(Y):
                out_ref[part, block * 4 + q] = got[part * SLICE : (part + 1) * SLICE]


def back(at, own, oth, mine, theirs):
    return pl.pallas_call(
        back_kernel,
        in_specs=[SMEM, VMEM, VMEM, VMEM, VMEM],
        out_specs=VMEM,
        out_shape=jax.ShapeDtypeStruct((Y, 8, SLICE, HALF), jnp.bfloat16),
        scratch_shapes=[pltpu.VMEM((TRIALS, QUARTER), jnp.bfloat16)],
        cost_estimate=cost(2 * TRIALS * QUARTER * COLS, 6_000_000),
        compiler_params=params(BACK),
        name="back",
    )(at, own, oth, mine, theirs)


TILE = 1024


def gather_rows(core, pairs, g_ref):
    for t, (own_ref, oth_ref) in enumerate(pairs):
        for ref, part in ((own_ref, core), (oth_ref, 1 - core)):
            rows = pl.ds(pl.multiple_of(part * HALF, 16), HALF)
            g_ref[rows, t * TRIALS : (t + 1) * TRIALS] = ref[...].T


def outer_kernel(at_ref, *refs):
    owns, oths, rates_ref, out_ref, g_ref = refs[:4], refs[4:8], *refs[8:]

    @pl.when(pl.program_id(0) == 0)
    def _():
        gather_rows(at_ref[1], tuple(zip(owns, oths)), g_ref)

    before = jnp.concatenate([rates_ref[t] for t in range(STEPS)], axis=1)
    out_ref[...] = lax.dot_general(
        g_ref[...], before, (((1,), (1,)), ((), ())), preferred_element_type=jnp.float32
    ).astype(jnp.bfloat16)


def outer(at, owns, oths, rates):
    return pl.pallas_call(
        outer_kernel,
        grid_spec=pltpu.PrefetchScalarGridSpec(
            num_scalar_prefetch=1,
            grid=(COLS // TILE,),
            in_specs=[VMEM] * 8 + [pl.BlockSpec((STEPS, TILE, TRIALS), lambda j, at: (0, j, 0))],
            out_specs=pl.BlockSpec((QUARTER, TILE), lambda j, at: (0, j)),
            scratch_shapes=[pltpu.VMEM((QUARTER, STEPS * TRIALS), jnp.bfloat16)],
        ),
        out_shape=jax.ShapeDtypeStruct((QUARTER, COLS), jnp.bfloat16),
        cost_estimate=cost(2 * STEPS * TRIALS * QUARTER * COLS, 8_000_000),
        compiler_params=params(OUTER),
        name="outer",
    )(at, *owns, *oths, rates)


def whole(weights, rates):
    y, z, x, core = (lax.axis_index(a) for a in EVERY)
    at = jnp.stack([z % 4, core, y]).astype(jnp.int32)

    def of_root_core(mine, theirs):
        return jnp.where(core == z // 4, mine, lax.ppermute(theirs, "core", SWAP))

    root = of_root_core(*first(at, rates))
    parts = [lax.ppermute(root, EVERY, from_root(shift)) for shift in (1, 2, 3)]
    own = jnp.where(x == y, root, parts[0] + parts[1] + parts[2])
    late_weights, late_rates, _ = lax.optimization_barrier((weights, rates, root))
    mine, theirs = split(at, late_weights)
    theirs = lax.ppermute(theirs, "core", SWAP)
    before = of_root_core(*rows(at, late_rates))
    oth = lax.ppermute(own, "core", SWAP)
    owns, oths = [own], [oth]
    for step in range(STEPS - 1, 0, -1):
        sums = back(at, own, oth, mine, theirs)
        for axis in ("y", "z"):
            sums = lax.all_to_all(sums, axis, 0, 0, tiled=True)
            sums = jnp.sum(sums.astype(jnp.float32), axis=0)
            if axis == "y":
                sums = sums.astype(jnp.bfloat16)
        rate = before[step - 1].astype(jnp.float32)
        share = (sums * (1.0 - rate * rate)).astype(jnp.bfloat16)
        slices = [lax.ppermute(share, EVERY, across(shift)) for shift in range(X)]
        turned = jnp.concatenate([slices[-s % X] for s in range(X)] * 2)
        own = lax.dynamic_slice_in_dim(turned, (X - x) % X * SLICE, TRIALS, 0)
        oth = lax.ppermute(own, "core", SWAP)
        owns.append(own)
        oths.append(oth)
    return outer(at, owns[::-1], oths[::-1], rates)


def solution(mesh):
    fine = Mesh(mesh.devices.reshape(Y, Z, X, C), EVERY)
    in_specs = (P(("y", "z"), ("x", "core")), P(None, ("x", "core"), None))
    out_specs = P(("y", "z"), ("x", "core"))
    return jax.shard_map(whole, mesh=fine, in_specs=in_specs, out_specs=out_specs, check_vma=False)
```

time: 182 us -> 177 us (0.973)
  the two profiles are of different devices: /device:TPU:7 before, /device:TPU:1 now
where the time goes in v1:
time: 177 us; the launch traced here: 176 us
  blocking collectives  72.3 us (41%)
  starting transfers between devices  55.5 us (31%)
  Pallas kernels  20.2 us (11%)
  waiting for transfers between devices  19.2 us (11%)
  local copies, waits for them, and re-layouts  4.73 us (3%)
  other arithmetic  3.51 us (2%)
    all_to_all x5, blocking collectives, whole(): sums = lax.all_to_all(sums, axis, 0, 0, tiled=True)  72.3 us
    ppermute x12, starting transfers between devices, whole(): slices = [lax.ppermute(share, EVERY, across(shift)) for shift in range(X)]  20.9 us
    ppermute x4, starting transfers between devices, whole(): oth = lax.ppermute(own, 'core', SWAP)  15.7 us
    ppermute x12, waiting for transfers between devices, whole(): slices = [lax.ppermute(share, EVERY, across(shift)) for shift in range(X)]  8.91 us
    all_to_all x1, starting transfers between devices, whole(): sums = lax.all_to_all(sums, axis, 0, 0, tiled=True)  8.16 us
    pallas_call x3, Pallas kernels, back(): pl.pallas_call(back_kernel, in_specs=[SMEM, VMEM, VMEM, VMEM, VMEM], out_...  8 us
    pallas_call x1, Pallas kernels, outer(): pl.pallas_call(outer_kernel, grid_spec=pltpu.PrefetchScalarGridSpec(num_s...  7.02 us
    ppermute x2, starting transfers between devices, of_root_core(): return jnp.where(core == z // 4, mine, lax.ppermute(theirs, 'core', SWAP))  5.45 us
  transfers between devices with their start and end apart: 23, of which 16 were waited for; matrix products, arithmetic and copies ran while one was open for 0% of the time, Pallas kernels for 0%

profile of v1, /device:TPU:1, one launch (start us, length us, event | category | flops | bytes accessed | tf_op | source)
XLA Modules:
  0.0 175.6 jit_solution(8413500987723041408)
XLA Ops:
  1.8 3.3 %collective-permute-start = (bf16[128,384]{1,0:T(8,128)(2,1)S(1)}, bf16[128,384]{1,0:T(8,128)(2,1)S(1)}, u32[]{:S(2)}, u32[]{:S(2)}) collective-permute-start(bf16[128,384]{1,0:T(8,128)(2,1)S(1)} %get-tuple-element.14), channel_id=1, source_target_pairs={{0,1},{1,0},{2,3},{3,2},{4,5},{5,4},{6,7},{7,6},{8,9},{9,8},{10,11... | collective-permute-start | bytes 294920 | tf_op jit(solution)/shard_map/ppermute | solution.py:218
  6.1 2.3 %copy-done.1 = bf16[768,3072]{1,0:T(8,128)(2,1)S(1)} copy-done((bf16[768,3072]{1,0:T(8,128)(2,1)S(1)}, bf16[768,3072]{1,0:T(8,128)(2,1)}, u32[]{:S(2)}) %copy-start.1) | copy-done | bytes 4718616
  8.4 2.7 %split.1 = (bf16[4,768,384]{2,1,0:T(8,128)(2,1)S(1)}, bf16[4,768,384]{2,1,0:T(8,128)(2,1)}) custom-call(s32[3]{0:T(128)S(1)} %pad_add_fusion.at_ref, bf16[768,3072]{1,0:T(8,128)(2,1)S(1)} %copy-done.1), custom_call_target="tpu_custom_call" | custom-call | bytes 9437184 | tf_op jit(solution)/shard_map/split/pallas_call | solution.py:105
  12.9 2.2 %collective-permute-start.2 = (bf16[128,384]{1,0:T(8,128)(2,1)S(1)}, bf16[128,384]{1,0:T(8,128)(2,1)S(1)}, u32[]{:S(2)}, u32[]{:S(2)}) collective-permute-start(bf16[128,384]{1,0:T(8,128)(2,1)S(1)} %broadcast_select_fusion), channel_id=1, source_target_pairs={{0,4},{1,5},{8,12},{9,13},{16,20},{17,21},{24,28},{25,29},{32,36},... | collective-permute-start | bytes 294920 | tf_op jit(solution)/shard_map/ppermute | solution.py:221
  20.5 2.7 %back.3 = bf16[4,8,32,384]{3,2,1,0:T(8,128)(2,1)S(1)} custom-call(s32[3]{0:T(128)S(1)} %pad_add_fusion.at_ref, bf16[128,384]{1,0:T(8,128)(2,1)S(1)} %add_select_fusion.own_ref.refs_3_, bf16[128,384]{1,0:T(8,128)(2,1)S(1)} %collective-permute-done.4.oth_ref.refs_7_, bf16[4,768,384]{2,1,0:T(8,128)(2,1)S(1)} %get-tuple-element.16.mine_ref, ...), custom_call_target="tpu_custom_call" | custom-call | flops 603979776 | bytes 6000000 | tf_op jit(solution)/shard_map/back/pallas_call | solution.py:161
  23.2 17.2 %all_to_all.30 = bf16[4,8,32,384]{3,2,1,0:T(8,128)(2,1)S(1)} all-to-all(bf16[4,8,32,384]{3,2,1,0:T(8,128)(2,1)S(1)} %back.3), channel_id=1, replica_groups=mesh['y'=4,'z'=8,'x'=4,'core'=2] {'y'}, dimensions={0} | all-to-all | bytes 1572864 | tf_op jit(solution)/shard_map/all_to_all | solution.py:232
  41.2 8.2 %all-to-all-start.1 = ((bf16[8,32,384]{2,1,0:T(8,128)(2,1)}), bf16[8,32,384]{2,1,0:T(8,128)(2,1)S(1)}, u32[]{:S(2)}, u32[]{:S(2)}) async-start(bf16[8,32,384]{2,1,0:T(8,128)(2,1)} %reduce_sum.63), calls=%async_computation.1 | async-start | bytes 393216 | tf_op jit(solution)/shard_map/all_to_all | solution.py:232
  52.3 2.2 %collective-permute-start.6 = (bf16[3,32,384]{2,1,0:T(8,128)(2,1)S(1)}, bf16[3,32,384]{2,1,0:T(8,128)(2,1)S(1)}, u32[]{:S(2)}, u32[]{:S(2)}) collective-permute-start(bf16[3,32,384]{2,1,0:T(8,128)(2,1)S(1)} %get-tuple-element.20), channel_id=1, source_target_pairs={{0,1},{1,0},{2,3},{3,2},{4,5},{5,4},{6,7},{7,6},{8,9},{9,8},{10,11... | collective-permute-start | bytes 221192 | tf_op jit(solution)/shard_map/ppermute | solution.py:218
  55.4 2.7 %all-to-all-done.1 = bf16[8,32,384]{2,1,0:T(8,128)(2,1)S(1)} async-done(((bf16[8,32,384]{2,1,0:T(8,128)(2,1)}), bf16[8,32,384]{2,1,0:T(8,128)(2,1)S(1)}, u32[]{:S(2)}, u32[]{:S(2)}) %all-to-all-start.1) | async-done | bytes 196640 | tf_op jit(solution)/shard_map/all_to_all | solution.py:232
  58.8 4.6 %collective-permute-start.8 = (bf16[32,384]{1,0:T(8,128)(2,1)S(1)}, bf16[32,384]{1,0:T(8,128)(2,1)S(1)}, u32[]{:S(2)}, u32[]{:S(2)}) collective-permute-start(bf16[32,384]{1,0:T(8,128)(2,1)S(1)} %fusion.2), channel_id=1, source_target_pairs={{0,6},{1,7},{2,70},{3,71},{4,134},{5,135},{6,198},{7,199},{8,14},{... | collective-permute-start | bytes 73736 | tf_op jit(solution)/shard_map/ppermute | solution.py:238
  68.7 5.2 %collective-permute-start.11 = (bf16[128,384]{1,0:T(8,128)(2,1)S(1)}, bf16[128,384]{1,0:T(8,128)(2,1)S(1)}, u32[]{:S(2)}, u32[]{:S(2)}) collective-permute-start(bf16[128,384]{1,0:T(8,128)(2,1)S(1)} %constant_dynamic-slice_fusion.2.own_ref.refs_2_), channel_id=1, source_target_pairs={{0,1},{1,0},{2,3},{3,2},{4,5},{5,4},{6,7},{7,6},{8,9},{9,8},{10,11... | collective-permute-start | bytes 294920 | tf_op jit(solution)/shard_map/ppermute | solution.py:241
  74.9 2.7 %back.4 = bf16[4,8,32,384]{3,2,1,0:T(8,128)(2,1)S(1)} custom-call(s32[3]{0:T(128)S(1)} %pad_add_fusion.at_ref, bf16[128,384]{1,0:T(8,128)(2,1)S(1)} %constant_dynamic-slice_fusion.2.own_ref.refs_2_, bf16[128,384]{1,0:T(8,128)(2,1)S(1)} %collective-permute-done.11.oth_ref.refs_6_, bf16[4,768,384]{2,1,0:T(8,128)(2,1)S(1)} %get-tuple-element.16.mine_ref, ...), custom_call_target="tpu_custom_call" | custom-call | flops 603979776 | bytes 6000000 | tf_op jit(solution)/shard_map/back/pallas_call | solution.py:161
  77.6 15.5 %all_to_all.31 = bf16[4,8,32,384]{3,2,1,0:T(8,128)(2,1)S(1)} all-to-all(bf16[4,8,32,384]{3,2,1,0:T(8,128)(2,1)S(1)} %back.4), channel_id=1, replica_groups=mesh['y'=4,'z'=8,'x'=4,'core'=2] {'y'}, dimensions={0} | all-to-all | bytes 1572864 | tf_op jit(solution)/shard_map/all_to_all | solution.py:232
  93.9 12.0 %all_to_all.32 = bf16[8,32,384]{2,1,0:T(8,128)(2,1)S(1)} all-to-all(bf16[8,32,384]{2,1,0:T(8,128)(2,1)} %reduce_sum.65), channel_id=1, replica_groups=mesh['y'=4,'z'=8,'x'=4,'core'=2] {'z'}, dimensions={0} | all-to-all | bytes 393216 | tf_op jit(solution)/shard_map/all_to_all | solution.py:232
  107.3 4.6 %collective-permute-start.13 = (bf16[32,384]{1,0:T(8,128)(2,1)S(1)}, bf16[32,384]{1,0:T(8,128)(2,1)S(1)}, u32[]{:S(2)}, u32[]{:S(2)}) collective-permute-start(bf16[32,384]{1,0:T(8,128)(2,1)S(1)} %fusion.1), channel_id=1, source_target_pairs={{0,6},{1,7},{2,70},{3,71},{4,134},{5,135},{6,198},{7,199},{8,14},{... | collective-permute-start | bytes 73736 | tf_op jit(solution)/shard_map/ppermute | solution.py:238
  113.4 2.7 %collective-permute-done.14 = bf16[32,384]{1,0:T(8,128)(2,1)S(1)} collective-permute-done((bf16[32,384]{1,0:T(8,128)(2,1)S(1)}, bf16[32,384]{1,0:T(8,128)(2,1)S(1)}, u32[]{:S(2)}, u32[]{:S(2)}) %collective-permute-start.14) | collective-permute-done | bytes 24608 | tf_op jit(solution)/shard_map/ppermute | solution.py:238
  116.4 4.7 %collective-permute-start.16 = (bf16[128,384]{1,0:T(8,128)(2,1)S(1)}, bf16[128,384]{1,0:T(8,128)(2,1)S(1)}, u32[]{:S(2)}, u32[]{:S(2)}) collective-permute-start(bf16[128,384]{1,0:T(8,128)(2,1)S(1)} %constant_dynamic-slice_fusion.1.own_ref.refs_1_), channel_id=1, source_target_pairs={{0,1},{1,0},{2,3},{3,2},{4,5},{5,4},{6,7},{7,6},{8,9},{9,8},{10,11... | collective-permute-start | bytes 294920 | tf_op jit(solution)/shard_map/ppermute | solution.py:241
  122.0 2.7 %back.5 = bf16[4,8,32,384]{3,2,1,0:T(8,128)(2,1)S(1)} custom-call(s32[3]{0:T(128)S(1)} %pad_add_fusion.at_ref, bf16[128,384]{1,0:T(8,128)(2,1)S(1)} %constant_dynamic-slice_fusion.1.own_ref.refs_1_, bf16[128,384]{1,0:T(8,128)(2,1)S(1)} %collective-permute-done.16.oth_ref.refs_5_, bf16[4,768,384]{2,1,0:T(8,128)(2,1)S(1)} %get-tuple-element.16.mine_ref, ...), custom_call_target="tpu_custom_call" | custom-call | flops 603979776 | bytes 6000000 | tf_op jit(solution)/shard_map/back/pallas_call | solution.py:161
  124.7 16.5 %all_to_all.33 = bf16[4,8,32,384]{3,2,1,0:T(8,128)(2,1)S(1)} all-to-all(bf16[4,8,32,384]{3,2,1,0:T(8,128)(2,1)S(1)} %back.5), channel_id=1, replica_groups=mesh['y'=4,'z'=8,'x'=4,'core'=2] {'y'}, dimensions={0} | all-to-all | bytes 1572864 | tf_op jit(solution)/shard_map/all_to_all | solution.py:232
  141.3 11.1 %all_to_all.34 = bf16[8,32,384]{2,1,0:T(8,128)(2,1)S(1)} all-to-all(bf16[8,32,384]{2,1,0:T(8,128)(2,1)S(1)} %reduce_sum.67), channel_id=1, replica_groups=mesh['y'=4,'z'=8,'x'=4,'core'=2] {'z'}, dimensions={0} | all-to-all | bytes 393216 | tf_op jit(solution)/shard_map/all_to_all | solution.py:232
  153.9 4.6 %collective-permute-start.18 = (bf16[32,384]{1,0:T(8,128)(2,1)S(1)}, bf16[32,384]{1,0:T(8,128)(2,1)S(1)}, u32[]{:S(2)}, u32[]{:S(2)}) collective-permute-start(bf16[32,384]{1,0:T(8,128)(2,1)S(1)} %fusion), channel_id=1, source_target_pairs={{0,6},{1,7},{2,70},{3,71},{4,134},{5,135},{6,198},{7,199},{8,14},{... | collective-permute-start | bytes 73736 | tf_op jit(solution)/shard_map/ppermute | solution.py:238
  159.4 3.2 %collective-permute-done.19 = bf16[32,384]{1,0:T(8,128)(2,1)S(1)} collective-permute-done((bf16[32,384]{1,0:T(8,128)(2,1)S(1)}, bf16[32,384]{1,0:T(8,128)(2,1)S(1)}, u32[]{:S(2)}, u32[]{:S(2)}) %collective-permute-start.19) | collective-permute-done | bytes 24608 | tf_op jit(solution)/shard_map/ppermute | solution.py:238
  163.0 4.7 %collective-permute-start.21 = (bf16[128,384]{1,0:T(8,128)(2,1)S(1)}, bf16[128,384]{1,0:T(8,128)(2,1)S(1)}, u32[]{:S(2)}, u32[]{:S(2)}) collective-permute-start(bf16[128,384]{1,0:T(8,128)(2,1)S(1)} %constant_dynamic-slice_fusion.refs_0_), channel_id=1, source_target_pairs={{0,1},{1,0},{2,3},{3,2},{4,5},{5,4},{6,7},{7,6},{8,9},{9,8},{10,11... | collective-permute-start | bytes 294920 | tf_op jit(solution)/shard_map/ppermute | solution.py:241
  168.6 7.0 %outer.1 = bf16[768,3072]{1,0:T(8,128)(2,1)} custom-call(s32[3]{0:T(128)S(1)} %pad_add_fusion.at_ref, bf16[128,384]{1,0:T(8,128)(2,1)S(1)} %constant_dynamic-slice_fusion.refs_0_, bf16[128,384]{1,0:T(8,128)(2,1)S(1)} %constant_dynamic-slice_fusion.1.own_ref.refs_1_, bf16[128,384]{1,0:T(8,128)(2,1)S(1)} %constant_dynamic-slice_fusion.2.own_ref.refs_2_, ...), custom_call_target="tpu_custom_call" | custom-call | flops 2415919104 | bytes 8000000 | tf_op jit(solution)/shard_map/outer/pallas_call | solution.py:197
  (80 shorter events, 30.3 us)
Async XLA Ops:
  1.8 4.2 %collective-permute-start = (bf16[128,384]{1,0:T(8,128)(2,1)S(1)}, bf16[128,384]{1,0:T(8,128)(2,1)S(1)}, u32[]{:S(2)}, u32[]{:S(2)}) collective-permute-start(bf16[128,384]{1,0:T(8,128)(2,1)S(1)} %get-tuple-element.14), channel_id=1, source_target_pairs={{0,1},{1,0},{2,3},{3,2},{4,5},{5,4},{6,7},{7,6},{8,9},{9,8},{10,11... | collective-permute-start | bytes 294920 | tf_op jit(solution)/shard_map/ppermute | solution.py:218
  11.1 9.4 %collective-permute-start.5 = (bf16[4,768,384]{2,1,0:T(8,128)(2,1)}, bf16[4,768,384]{2,1,0:T(8,128)(2,1)}, u32[]{:S(2)}, u32[]{:S(2)}) collective-permute-start(bf16[4,768,384]{2,1,0:T(8,128)(2,1)} %get-tuple-element.17), channel_id=1, source_target_pairs={{0,1},{1,0},{2,3},{3,2},{4,5},{5,4},{6,7},{7,6},{8,9},{9,8},{10,11... | collective-permute-start | bytes 7077896 | tf_op jit(solution)/shard_map/ppermute | solution.py:225
  11.5 4.9 %collective-permute-start.1 = (bf16[128,384]{1,0:T(8,128)(2,1)S(1)}, bf16[128,384]{1,0:T(8,128)(2,1)S(1)}, u32[]{:S(2)}, u32[]{:S(2)}) collective-permute-start(bf16[128,384]{1,0:T(8,128)(2,1)S(1)} %broadcast_select_fusion), channel_id=1, source_target_pairs={{0,2},{1,3},{8,10},{9,11},{16,18},{17,19},{24,26},{25,27},{32,34},... | collective-permute-start | bytes 294920 | tf_op jit(solution)/shard_map/ppermute | solution.py:221
  12.9 4.2 %collective-permute-start.2 = (bf16[128,384]{1,0:T(8,128)(2,1)S(1)}, bf16[128,384]{1,0:T(8,128)(2,1)S(1)}, u32[]{:S(2)}, u32[]{:S(2)}) collective-permute-start(bf16[128,384]{1,0:T(8,128)(2,1)S(1)} %broadcast_select_fusion), channel_id=1, source_target_pairs={{0,4},{1,5},{8,12},{9,13},{16,20},{17,21},{24,28},{25,29},{32,36},... | collective-permute-start | bytes 294920 | tf_op jit(solution)/shard_map/ppermute | solution.py:221
  15.1 3.3 %collective-permute-start.3 = (bf16[128,384]{1,0:T(8,128)(2,1)S(1)}, bf16[128,384]{1,0:T(8,128)(2,1)S(1)}, u32[]{:S(2)}, u32[]{:S(2)}) collective-permute-start(bf16[128,384]{1,0:T(8,128)(2,1)S(1)} %broadcast_select_fusion), channel_id=1, source_target_pairs={{0,6},{1,7},{8,14},{9,15},{16,22},{17,23},{24,30},{25,31},{32,38},... | collective-permute-start | bytes 294920 | tf_op jit(solution)/shard_map/ppermute | solution.py:221
  18.4 2.0 %collective-permute-start.4 = (bf16[128,384]{1,0:T(8,128)(2,1)S(1)}, bf16[128,384]{1,0:T(8,128)(2,1)S(1)}, u32[]{:S(2)}, u32[]{:S(2)}) collective-permute-start(bf16[128,384]{1,0:T(8,128)(2,1)S(1)} %add_select_fusion.own_ref.refs_3_), channel_id=1, source_target_pairs={{0,1},{1,0},{2,3},{3,2},{4,5},{5,4},{6,7},{7,6},{8,9},{9,8},{10,11... | collective-permute-start | bytes 294920 | tf_op jit(solution)/shard_map/ppermute | solution.py:227
  41.2 16.8 %all-to-all-start.1 = ((bf16[8,32,384]{2,1,0:T(8,128)(2,1)}), bf16[8,32,384]{2,1,0:T(8,128)(2,1)S(1)}, u32[]{:S(2)}, u32[]{:S(2)}) async-start(bf16[8,32,384]{2,1,0:T(8,128)(2,1)} %reduce_sum.63), calls=%async_computation.1 | async-start | bytes 393216 | tf_op jit(solution)/shard_map/all_to_all | solution.py:232
  52.3 3.1 %collective-permute-start.6 = (bf16[3,32,384]{2,1,0:T(8,128)(2,1)S(1)}, bf16[3,32,384]{2,1,0:T(8,128)(2,1)S(1)}, u32[]{:S(2)}, u32[]{:S(2)}) collective-permute-start(bf16[3,32,384]{2,1,0:T(8,128)(2,1)S(1)} %get-tuple-element.20), channel_id=1, source_target_pairs={{0,1},{1,0},{2,3},{3,2},{4,5},{5,4},{6,7},{7,6},{8,9},{9,8},{10,11... | collective-permute-start | bytes 221192 | tf_op jit(solution)/shard_map/ppermute | solution.py:218
  55.4 19.5 %copy-start.2 = (bf16[3,32,384]{2,1,0:T(8,128)(2,1)}, bf16[3,32,384]{2,1,0:T(8,128)(2,1)S(1)}, u32[]{:S(2)}) copy-start(bf16[3,32,384]{2,1,0:T(8,128)(2,1)S(1)} %broadcast_select_fusion.1) | copy-start | bytes 221188
  58.1 8.1 %collective-permute-start.7 = (bf16[32,384]{1,0:T(8,128)(2,1)S(1)}, bf16[32,384]{1,0:T(8,128)(2,1)S(1)}, u32[]{:S(2)}, u32[]{:S(2)}) collective-permute-start(bf16[32,384]{1,0:T(8,128)(2,1)S(1)} %fusion.2), channel_id=1, source_target_pairs={{0,0},{1,1},{2,64},{3,65},{4,128},{5,129},{6,192},{7,193},{8,8},{9... | collective-permute-start | bytes 73736 | tf_op jit(solution)/shard_map/ppermute | solution.py:238
  58.8 7.4 %collective-permute-start.8 = (bf16[32,384]{1,0:T(8,128)(2,1)S(1)}, bf16[32,384]{1,0:T(8,128)(2,1)S(1)}, u32[]{:S(2)}, u32[]{:S(2)}) collective-permute-start(bf16[32,384]{1,0:T(8,128)(2,1)S(1)} %fusion.2), channel_id=1, source_target_pairs={{0,6},{1,7},{2,70},{3,71},{4,134},{5,135},{6,198},{7,199},{8,14},{... | collective-permute-start | bytes 73736 | tf_op jit(solution)/shard_map/ppermute | solution.py:238
  63.4 4.2 %collective-permute-start.9 = (bf16[32,384]{1,0:T(8,128)(2,1)S(1)}, bf16[32,384]{1,0:T(8,128)(2,1)S(1)}, u32[]{:S(2)}, u32[]{:S(2)}) collective-permute-start(bf16[32,384]{1,0:T(8,128)(2,1)S(1)} %fusion.2), channel_id=1, source_target_pairs={{0,4},{1,5},{2,68},{3,69},{4,132},{5,133},{6,196},{7,197},{8,12},{... | collective-permute-start | bytes 73736 | tf_op jit(solution)/shard_map/ppermute | solution.py:238
  64.7 3.9 %collective-permute-start.10 = (bf16[32,384]{1,0:T(8,128)(2,1)S(1)}, bf16[32,384]{1,0:T(8,128)(2,1)S(1)}, u32[]{:S(2)}, u32[]{:S(2)}) collective-permute-start(bf16[32,384]{1,0:T(8,128)(2,1)S(1)} %fusion.2), channel_id=1, source_target_pairs={{0,2},{1,3},{2,66},{3,67},{4,130},{5,131},{6,194},{7,195},{8,10},{... | collective-permute-start | bytes 73736 | tf_op jit(solution)/shard_map/ppermute | solution.py:238
  68.7 6.2 %collective-permute-start.11 = (bf16[128,384]{1,0:T(8,128)(2,1)S(1)}, bf16[128,384]{1,0:T(8,128)(2,1)S(1)}, u32[]{:S(2)}, u32[]{:S(2)}) collective-permute-start(bf16[128,384]{1,0:T(8,128)(2,1)S(1)} %constant_dynamic-slice_fusion.2.own_ref.refs_2_), channel_id=1, source_target_pairs={{0,1},{1,0},{2,3},{3,2},{4,5},{5,4},{6,7},{7,6},{8,9},{9,8},{10,11... | collective-permute-start | bytes 294920 | tf_op jit(solution)/shard_map/ppermute | solution.py:241
  106.6 6.8 %collective-permute-start.12 = (bf16[32,384]{1,0:T(8,128)(2,1)S(1)}, bf16[32,384]{1,0:T(8,128)(2,1)S(1)}, u32[]{:S(2)}, u32[]{:S(2)}) collective-permute-start(bf16[32,384]{1,0:T(8,128)(2,1)S(1)} %fusion.1), channel_id=1, source_target_pairs={{0,0},{1,1},{2,64},{3,65},{4,128},{5,129},{6,192},{7,193},{8,8},{9... | collective-permute-start | bytes 73736 | tf_op jit(solution)/shard_map/ppermute | solution.py:238
  107.3 6.1 %collective-permute-start.13 = (bf16[32,384]{1,0:T(8,128)(2,1)S(1)}, bf16[32,384]{1,0:T(8,128)(2,1)S(1)}, u32[]{:S(2)}, u32[]{:S(2)}) collective-permute-start(bf16[32,384]{1,0:T(8,128)(2,1)S(1)} %fusion.1), channel_id=1, source_target_pairs={{0,6},{1,7},{2,70},{3,71},{4,134},{5,135},{6,198},{7,199},{8,14},{... | collective-permute-start | bytes 73736 | tf_op jit(solution)/shard_map/ppermute | solution.py:238
  111.9 4.2 %collective-permute-start.14 = (bf16[32,384]{1,0:T(8,128)(2,1)S(1)}, bf16[32,384]{1,0:T(8,128)(2,1)S(1)}, u32[]{:S(2)}, u32[]{:S(2)}) collective-permute-start(bf16[32,384]{1,0:T(8,128)(2,1)S(1)} %fusion.1), channel_id=1, source_target_pairs={{0,4},{1,5},{2,68},{3,69},{4,132},{5,133},{6,196},{7,197},{8,12},{... | collective-permute-start | bytes 73736 | tf_op jit(solution)/shard_map/ppermute | solution.py:238
  111.9 4.4 %collective-permute-start.15 = (bf16[32,384]{1,0:T(8,128)(2,1)S(1)}, bf16[32,384]{1,0:T(8,128)(2,1)S(1)}, u32[]{:S(2)}, u32[]{:S(2)}) collective-permute-start(bf16[32,384]{1,0:T(8,128)(2,1)S(1)} %fusion.1), channel_id=1, source_target_pairs={{0,2},{1,3},{2,66},{3,67},{4,130},{5,131},{6,194},{7,195},{8,10},{... | collective-permute-start | bytes 73736 | tf_op jit(solution)/shard_map/ppermute | solution.py:238
  116.4 5.6 %collective-permute-start.16 = (bf16[128,384]{1,0:T(8,128)(2,1)S(1)}, bf16[128,384]{1,0:T(8,128)(2,1)S(1)}, u32[]{:S(2)}, u32[]{:S(2)}) collective-permute-start(bf16[128,384]{1,0:T(8,128)(2,1)S(1)} %constant_dynamic-slice_fusion.1.own_ref.refs_1_), channel_id=1, source_target_pairs={{0,1},{1,0},{2,3},{3,2},{4,5},{5,4},{6,7},{7,6},{8,9},{9,8},{10,11... | collective-permute-start | bytes 294920 | tf_op jit(solution)/shard_map/ppermute | solution.py:241
  153.2 6.1 %collective-permute-start.17 = (bf16[32,384]{1,0:T(8,128)(2,1)S(1)}, bf16[32,384]{1,0:T(8,128)(2,1)S(1)}, u32[]{:S(2)}, u32[]{:S(2)}) collective-permute-start(bf16[32,384]{1,0:T(8,128)(2,1)S(1)} %fusion), channel_id=1, source_target_pairs={{0,0},{1,1},{2,64},{3,65},{4,128},{5,129},{6,192},{7,193},{8,8},{9... | collective-permute-start | bytes 73736 | tf_op jit(solution)/shard_map/ppermute | solution.py:238
  153.9 5.6 %collective-permute-start.18 = (bf16[32,384]{1,0:T(8,128)(2,1)S(1)}, bf16[32,384]{1,0:T(8,128)(2,1)S(1)}, u32[]{:S(2)}, u32[]{:S(2)}) collective-permute-start(bf16[32,384]{1,0:T(8,128)(2,1)S(1)} %fusion), channel_id=1, source_target_pairs={{0,6},{1,7},{2,70},{3,71},{4,134},{5,135},{6,198},{7,199},{8,14},{... | collective-permute-start | bytes 73736 | tf_op jit(solution)/shard_map/ppermute | solution.py:238
  158.5 4.2 %collective-permute-start.19 = (bf16[32,384]{1,0:T(8,128)(2,1)S(1)}, bf16[32,384]{1,0:T(8,128)(2,1)S(1)}, u32[]{:S(2)}, u32[]{:S(2)}) collective-permute-start(bf16[32,384]{1,0:T(8,128)(2,1)S(1)} %fusion), channel_id=1, source_target_pairs={{0,4},{1,5},{2,68},{3,69},{4,132},{5,133},{6,196},{7,197},{8,12},{... | collective-permute-start | bytes 73736 | tf_op jit(solution)/shard_map/ppermute | solution.py:238
  158.5 4.4 %collective-permute-start.20 = (bf16[32,384]{1,0:T(8,128)(2,1)S(1)}, bf16[32,384]{1,0:T(8,128)(2,1)S(1)}, u32[]{:S(2)}, u32[]{:S(2)}) collective-permute-start(bf16[32,384]{1,0:T(8,128)(2,1)S(1)} %fusion), channel_id=1, source_target_pairs={{0,2},{1,3},{2,66},{3,67},{4,130},{5,131},{6,194},{7,195},{8,10},{... | collective-permute-start | bytes 73736 | tf_op jit(solution)/shard_map/ppermute | solution.py:238
  163.0 5.6 %collective-permute-start.21 = (bf16[128,384]{1,0:T(8,128)(2,1)S(1)}, bf16[128,384]{1,0:T(8,128)(2,1)S(1)}, u32[]{:S(2)}, u32[]{:S(2)}) collective-permute-start(bf16[128,384]{1,0:T(8,128)(2,1)S(1)} %constant_dynamic-slice_fusion.refs_0_), channel_id=1, source_target_pairs={{0,1},{1,0},{2,3},{3,2},{4,5},{5,4},{6,7},{7,6},{8,9},{9,8},{10,11... | collective-permute-start | bytes 294920 | tf_op jit(solution)/shard_map/ppermute | solution.py:241
  (2 other events, 4.5 us)

commit v2 on v1

v2 whole, which is shorter than its diff:
```python
import functools

import jax
import jax.numpy as jnp
from jax import lax
from jax.experimental import pallas as pl
from jax.experimental.pallas import tpu as pltpu
from jax.sharding import Mesh, PartitionSpec as P

STEPS = 4
Y, Z, X, C = 4, 8, 4, 2
EVERY = ("y", "z", "x", "core")
SWAP = [(0, 1), (1, 0)]
HALF = 384
QUARTER = 768
TRIALS = 128
SLICE = 32
SPLIT, ROWS, BACK, OUTER, KEEP = 52, 52, 8, 52, 48
COLS = 3072
VMEM = pl.BlockSpec(memory_space=pltpu.VMEM)
SMEM = pl.BlockSpec(memory_space=pltpu.SMEM)
HBM = pl.BlockSpec(memory_space=pltpu.HBM)


def flat(y, z, x, core):
    return ((y % Y * Z + z) * X + x % X) * C + core


def across(j):
    return [
        (flat(y, z, x, core), flat(x, z, y + j + 2 * core, core))
        for y in range(Y) for z in range(Z) for x in range(X) for core in range(C)
    ]


def from_root(shift):
    return [
        (flat(y, z, y, core), flat(y, z, y + shift, core))
        for y in range(Y) for z in range(Z) for core in range(C)
    ]


def params(mib):
    return pltpu.CompilerParams(vmem_limit_bytes=mib << 20)


def cost(flops, moved):
    return pl.CostEstimate(flops=flops, bytes_accessed=moved, transcendentals=0)


def half(core):
    return pl.ds(pl.multiple_of(core * HALF, 128), HALF)


def first_kernel(at_ref, rates_ref, mine_ref, theirs_ref, last_ref, zero_ref, sems):
    core = at_ref[1]
    rows = pl.ds(pl.multiple_of(at_ref[0] * QUARTER, 16), QUARTER)
    copies = [
        pltpu.make_async_copy(rates_ref.at[STEPS, rows], last_ref, sems.at[0]),
        pltpu.make_async_copy(rates_ref.at[0, rows], zero_ref, sems.at[1]),
    ]
    for copy in copies:
        copy.start()
    for copy in copies:
        copy.wait()
    for out_ref, part in ((theirs_ref, 1 - core), (mine_ref, core)):
        part = pl.ds(pl.multiple_of(part * HALF, 16), HALF)
        last = last_ref[part, :].astype(jnp.float32)
        zero = zero_ref[part, :].astype(jnp.float32)
        out_ref[...] = ((last - zero) * (1.0 - last * last)).astype(jnp.bfloat16).T


def first(at, rates):
    shape = jax.ShapeDtypeStruct((TRIALS, HALF), jnp.bfloat16)
    return pl.pallas_call(
        first_kernel,
        in_specs=[SMEM, HBM],
        out_specs=[VMEM, VMEM],
        out_shape=[shape, shape],
        scratch_shapes=[
            pltpu.VMEM((QUARTER, TRIALS), jnp.bfloat16),
            pltpu.VMEM((QUARTER, TRIALS), jnp.bfloat16),
            pltpu.SemaphoreType.DMA((2,)),
        ],
        compiler_params=params(52),
        name="first",
    )(at, rates)


def split_kernel(at_ref, w_ref, out_ref, sems, *, partner):
    part = 1 - at_ref[1] if partner else at_ref[1]
    copies = []
    for q in range(4):
        columns = pl.ds(pl.multiple_of((2 * q + part) * HALF, 128), HALF)
        copies.append(pltpu.make_async_copy(w_ref.at[:, columns], out_ref.at[q], sems.at[q]))
    for copy in copies:
        copy.start()
    for copy in copies:
        copy.wait()


def split(at, weights, partner):
    return pl.pallas_call(
        functools.partial(split_kernel, partner=partner),
        in_specs=[SMEM, HBM],
        out_specs=VMEM,
        out_shape=jax.ShapeDtypeStruct((4, QUARTER, HALF), jnp.bfloat16),
        scratch_shapes=[pltpu.SemaphoreType.DMA((4,))],
        cost_estimate=cost(0, 4_718_592),
        compiler_params=params(SPLIT if partner else KEEP),
        name="split",
    )(at, weights)


def rows_kernel(at_ref, rates_ref, mine_ref, theirs_ref, held_ref, turned_ref, sem):
    core = at_ref[1]
    rows = pl.ds(pl.multiple_of(at_ref[0] * QUARTER, 16), QUARTER)
    copy = pltpu.make_async_copy(rates_ref.at[1:STEPS, rows], held_ref, sem)
    copy.start()
    copy.wait()
    slot = pl.ds(pl.multiple_of(at_ref[2] * SLICE, SLICE), SLICE)
    for t in range(STEPS - 1):
        for out_ref, part in ((theirs_ref, 1 - core), (mine_ref, core)):
            turned_ref[...] = held_ref[t, pl.ds(pl.multiple_of(part * HALF, 16), HALF), :].T
            out_ref[t] = turned_ref[slot, :]


def rows(at, rates):
    shape = jax.ShapeDtypeStruct((STEPS - 1, SLICE, HALF), jnp.bfloat16)
    return pl.pallas_call(
        rows_kernel,
        in_specs=[SMEM, HBM],
        out_specs=[VMEM, VMEM],
        out_shape=[shape, shape],
        scratch_shapes=[
            pltpu.VMEM((STEPS - 1, QUARTER, TRIALS), jnp.bfloat16),
            pltpu.VMEM((TRIALS, HALF), jnp.bfloat16),
            pltpu.SemaphoreType.DMA,
        ],
        cost_estimate=cost(0, 600_000),
        compiler_params=params(ROWS),
        name="rows",
    )(at, rates)


def fill(at_ref, first_ref, second_ref, g_ref):
    core, x = at_ref[1], at_ref[3]
    for ref, part in ((first_ref, core), (second_ref, 1 - core)):
        if ref.shape == (TRIALS, HALF):
            g_ref[:, half(part)] = ref[...]
        else:
            for j in range(2):
                slot = (x + 2 * X - j - 2 * part) % X
                g_ref[pl.ds(pl.multiple_of(slot * SLICE, SLICE), SLICE), :] = ref[j]


def back_kernel(at_ref, first_ref, second_ref, mine_ref, theirs_ref, out_ref, g_ref, held_ref, sems):
    core = at_ref[1]
    copies = [
        pltpu.make_async_copy(theirs_ref.at[q], held_ref.at[q], sems.at[q]) for q in range(4)
    ]
    for copy in copies:
        copy.start()
    fill(at_ref, first_ref, second_ref, g_ref)
    for ref, block in ((mine_ref, core), (held_ref, 1 - core)):
        for q in range(4):
            if ref is held_ref:
                copies[q].wait()
            got = jnp.dot(g_ref[...], ref[q], preferred_element_type=jnp.float32)
            got = got.astype(jnp.bfloat16)
            for part in range(Y):
                out_ref[part, block * 4 + q] = got[part * SLICE : (part + 1) * SLICE]


def back(at, pair, mine, theirs):
    return pl.pallas_call(
        back_kernel,
        in_specs=[SMEM, VMEM, VMEM, VMEM, HBM],
        out_specs=[VMEM, VMEM],
        out_shape=[
            jax.ShapeDtypeStruct((Y, 8, SLICE, HALF), jnp.bfloat16),
            jax.ShapeDtypeStruct((TRIALS, QUARTER), jnp.bfloat16),
        ],
        scratch_shapes=[
            pltpu.VMEM((4, QUARTER, HALF), jnp.bfloat16),
            pltpu.SemaphoreType.DMA((4,)),
        ],
        cost_estimate=cost(2 * TRIALS * QUARTER * COLS, 6_000_000),
        compiler_params=params(BACK),
        name="back",
    )(at, *pair, mine, theirs)


TILE = 512
TILES = COLS // TILE


def outer_kernel(
    at_ref, g4, g3, g2, first_ref, second_ref, rates_ref, out_ref, g_ref, turned_ref, held_ref, done_ref, sems
):
    def came(j):
        columns = pl.ds(j * TILE, TILE)
        return pltpu.make_async_copy(rates_ref.at[0:STEPS, columns], held_ref.at[:, columns], sems.at[0, j])

    def went(j):
        columns = pl.ds(j * TILE, TILE)
        return pltpu.make_async_copy(done_ref.at[j], out_ref.at[:, columns], sems.at[1, j])

    for j in range(TILES):
        came(j).start()
    for t, ref in ((3, g4), (2, g3), (1, g2)):
        turned_ref[:, t * TRIALS : (t + 1) * TRIALS] = ref[...].T
    fill(at_ref, first_ref, second_ref, g_ref)
    turned_ref[:, :TRIALS] = g_ref[...].T
    for j in range(TILES):
        came(j).wait()
        columns = slice(j * TILE, (j + 1) * TILE)
        before = jnp.concatenate([held_ref[t, columns, :] for t in range(STEPS)], axis=1)
        done_ref[j] = lax.dot_general(
            turned_ref[...], before, (((1,), (1,)), ((), ())), preferred_element_type=jnp.float32
        ).astype(jnp.bfloat16)
        went(j).start()
    for j in range(TILES):
        went(j).wait()


def outer(at, full, pair, rates):
    return pl.pallas_call(
        outer_kernel,
        in_specs=[SMEM] + [VMEM] * 5 + [HBM],
        out_specs=HBM,
        out_shape=jax.ShapeDtypeStruct((QUARTER, COLS), jnp.bfloat16),
        scratch_shapes=[
            pltpu.VMEM((TRIALS, QUARTER), jnp.bfloat16),
            pltpu.VMEM((QUARTER, STEPS * TRIALS), jnp.bfloat16),
            pltpu.VMEM((STEPS, COLS, TRIALS), jnp.bfloat16),
            pltpu.VMEM((TILES, QUARTER, TILE), jnp.bfloat16),
            pltpu.SemaphoreType.DMA((2, TILES)),
        ],
        cost_estimate=cost(2 * STEPS * TRIALS * QUARTER * COLS, 8_000_000),
        compiler_params=params(OUTER),
        name="outer",
    )(at, *full, *pair, rates)


def whole(weights, rates):
    y, z, x, core = (lax.axis_index(a) for a in EVERY)
    at = jnp.stack([z % 4, core, y, x]).astype(jnp.int32)

    def swapped(array):
        return lax.ppermute(array, "core", SWAP)

    def of_root_core(mine, theirs):
        return jnp.where(core == z // 4, mine, swapped(theirs))

    root = of_root_core(*first(at, rates))
    parts = [lax.ppermute(root, EVERY, from_root(shift)) for shift in (1, 2, 3)]
    own = jnp.where(x == y, root, parts[0] + parts[1] + parts[2])
    late_weights, late_rates, _ = lax.optimization_barrier((weights, rates, root))
    theirs = swapped(split(at, late_weights, True))
    mine = split(at, late_weights, False)
    before = of_root_core(*rows(at, late_rates))
    pair = (own, swapped(own))
    full = []
    for step in range(STEPS - 1, 0, -1):
        sums, whole_grad = back(at, pair, mine, theirs)
        full.append(whole_grad)
        for axis in ("y", "z"):
            sums = lax.all_to_all(sums, axis, 0, 0, tiled=True)
            sums = jnp.sum(sums.astype(jnp.float32), axis=0)
            if axis == "y":
                sums = sums.astype(jnp.bfloat16)
        rate = before[step - 1].astype(jnp.float32)
        share = (sums * (1.0 - rate * rate)).astype(jnp.bfloat16)
        other = swapped(share)
        share = jnp.where(
            core == 0, jnp.concatenate([share, other], 1), jnp.concatenate([other, share], 1)
        )
        slices = jnp.stack([lax.ppermute(share, EVERY, across(j)) for j in range(2)])
        pair = (slices, swapped(slices))
    return outer(at, full, pair, rates)


def solution(mesh):
    fine = Mesh(mesh.devices.reshape(Y, Z, X, C), EVERY)
    in_specs = (P(("y", "z"), ("x", "core")), P(None, ("x", "core"), None))
    out_specs = P(("y", "z"), ("x", "core"))
    return jax.shard_map(whole, mesh=fine, in_specs=in_specs, out_specs=out_specs, check_vma=False)
```

time: 177 us -> 174 us (0.983)
  starting transfers between devices: 55.5 us -> 48.5 us
  local copies, waits for them, and re-layouts: 4.73 us -> 0.01 us
  Pallas kernels: 20.2 us -> 24 us
  blocking collectives: 72.3 us -> 74.8 us
  waiting for transfers between devices: 19.2 us -> 21 us
    ppermute x19 -> x16, starting transfers between devices: 42.5 us -> 35.4 us  [the longest x10 21.7 us: swapped(): return lax.ppermute(array, 'core', SWAP)]
    unnamed x27 -> x2, local copies, waits for them, and re-layouts: 4.63 us -> 0.01 us
    pallas_call x5 -> x6, Pallas kernels: 17.7 us -> 20.5 us  [the longest x3 8.32 us: back(): pl.pallas_call(back_kernel, in_specs=[SMEM, VMEM, VMEM, VMEM, HBM], out_s...]
    all_to_all x5, blocking collectives: 72.3 us -> 74.8 us  [whole(): sums = lax.all_to_all(sums, axis, 0, 0, tiled=True)]
    ppermute x19 -> x16, waiting for transfers between devices: 14.5 us -> 14.9 us  [the longest x6 7.64 us: whole(): lax.ppermute(share, EVERY, across(j))]
  transfers between devices with their start and end apart: 23 -> 20, of which waited for: 16 -> 17; matrix products, arithmetic and copies ran while one was open for 0% -> 0% of each run, Pallas kernels for 0% -> 2%
where the time goes in v2:
time: 174 us; the launch traced here: 172 us
  blocking collectives  74.8 us (43%)
  starting transfers between devices  48.5 us (28%)
  Pallas kernels  24 us (14%)
  waiting for transfers between devices  21 us (12%)
  other arithmetic  3.58 us (2%)
    all_to_all x5, blocking collectives, whole(): sums = lax.all_to_all(sums, axis, 0, 0, tiled=True)  74.8 us
    ppermute x10, starting transfers between devices, swapped(): return lax.ppermute(array, 'core', SWAP)  21.7 us
    ppermute x6, starting transfers between devices, whole(): lax.ppermute(share, EVERY, across(j))  13.7 us
    pallas_call x3, Pallas kernels, back(): pl.pallas_call(back_kernel, in_specs=[SMEM, VMEM, VMEM, VMEM, HBM], out_s...  8.32 us
    all_to_all x1, starting transfers between devices, whole(): sums = lax.all_to_all(sums, axis, 0, 0, tiled=True)  8.18 us
    ppermute x6, waiting for transfers between devices, whole(): lax.ppermute(share, EVERY, across(j))  7.64 us
    ppermute x10, waiting for transfers between devices, swapped(): return lax.ppermute(array, 'core', SWAP)  7.24 us
    pallas_call x1, Pallas kernels, outer(): pl.pallas_call(outer_kernel, in_specs=[SMEM] + [VMEM] * 5 + [HBM], out_sp...  6.33 us
  transfers between devices with their start and end apart: 20, of which 17 were waited for; matrix products, arithmetic and copies ran while one was open for 0% of the time, Pallas kernels for 2%

profile of v2, /device:TPU:1, one launch (start us, length us, event | category | flops | bytes accessed | tf_op | source)
XLA Modules:
  0.0 172.3 jit_solution(17208420523334945526)
XLA Ops:
  1.8 3.3 %collective-permute-start = (bf16[128,384]{1,0:T(8,128)(2,1)S(1)}, bf16[128,384]{1,0:T(8,128)(2,1)S(1)}, u32[]{:S(2)}, u32[]{:S(2)}) collective-permute-start(bf16[128,384]{1,0:T(8,128)(2,1)S(1)} %get-tuple-element.18), channel_id=1, source_target_pairs={{0,1},{1,0},{2,3},{3,2},{4,5},{5,4},{6,7},{7,6},{8,9},{9,8},{10,11... | collective-permute-start | bytes 294920 | tf_op jit(solution)/shard_map/ppermute | solution.py:251
  6.1 3.6 %split.3 = bf16[4,768,384]{2,1,0:T(8,128)(2,1)} custom-call(s32[4]{0:T(128)S(1)} %pad_add_fusion.at_ref, bf16[768,3072]{1,0:T(8,128)(2,1)} %w_ref.1), custom_call_target="tpu_custom_call" | custom-call | bytes 4718592 | tf_op jit(solution)/shard_map/split/pallas_call | solution.py:103
  11.5 2.2 %collective-permute-start.2 = (bf16[128,384]{1,0:T(8,128)(2,1)S(1)}, bf16[128,384]{1,0:T(8,128)(2,1)S(1)}, u32[]{:S(2)}, u32[]{:S(2)}) collective-permute-start(bf16[128,384]{1,0:T(8,128)(2,1)S(1)} %broadcast_select_fusion), channel_id=1, source_target_pairs={{0,4},{1,5},{8,12},{9,13},{16,20},{17,21},{24,28},{25,29},{32,36},... | collective-permute-start | bytes 294920 | tf_op jit(solution)/shard_map/ppermute | solution.py:257
  18.1 2.2 %split.2.mine_ref = bf16[4,768,384]{2,1,0:T(8,128)(2,1)S(1)} custom-call(s32[4]{0:T(128)S(1)} %pad_add_fusion.at_ref, bf16[768,3072]{1,0:T(8,128)(2,1)} %w_ref.1), custom_call_target="tpu_custom_call" | custom-call | bytes 4718592 | tf_op jit(solution)/shard_map/split/pallas_call | solution.py:103
  20.4 2.8 %back.3 = (bf16[4,8,32,384]{3,2,1,0:T(8,128)(2,1)S(1)}, bf16[128,768]{1,0:T(8,128)(2,1)S(1)}) custom-call(s32[4]{0:T(128)S(1)} %pad_add_fusion.at_ref, bf16[128,384]{1,0:T(8,128)(2,1)S(1)} %add_select_fusion.first_ref, bf16[128,384]{1,0:T(8,128)(2,1)S(1)} %collective-permute-done.4.second_ref, bf16[4,768,384]{2,1,0:T(8,128)(2,1)S(1)} %split.2.mine_ref, ...), custom_call_target="tpu_custom_call" | custom-call | flops 603979776 | bytes 6000000 | tf_op jit(solution)/shard_map/back/pallas_call | solution.py:176
  23.1 17.9 %all_to_all.30 = bf16[4,8,32,384]{3,2,1,0:T(8,128)(2,1)S(1)} all-to-all(bf16[4,8,32,384]{3,2,1,0:T(8,128)(2,1)S(1)} %get-tuple-element.21), channel_id=1, replica_groups=mesh['y'=4,'z'=8,'x'=4,'core'=2] {'y'}, dimensions={0} | all-to-all | bytes 1572864 | tf_op jit(solution)/shard_map/all_to_all | solution.py:269
  41.8 8.2 %all-to-all-start.1 = ((bf16[8,32,384]{2,1,0:T(8,128)(2,1)}), bf16[8,32,384]{2,1,0:T(8,128)(2,1)S(1)}, u32[]{:S(2)}, u32[]{:S(2)}) async-start(bf16[8,32,384]{2,1,0:T(8,128)(2,1)} %reduce_sum.63), calls=%async_computation.1 | async-start | bytes 393216 | tf_op jit(solution)/shard_map/all_to_all | solution.py:269
  54.3 4.2 %all-to-all-done.1 = bf16[8,32,384]{2,1,0:T(8,128)(2,1)S(1)} async-done(((bf16[8,32,384]{2,1,0:T(8,128)(2,1)}), bf16[8,32,384]{2,1,0:T(8,128)(2,1)S(1)}, u32[]{:S(2)}, u32[]{:S(2)}) %all-to-all-start.1) | async-done | bytes 196640 | tf_op jit(solution)/shard_map/all_to_all | solution.py:269
  58.5 3.0 %collective-permute-start.7 = (bf16[32,384]{1,0:T(8,128)(2,1)S(1)}, bf16[32,384]{1,0:T(8,128)(2,1)S(1)}, u32[]{:S(2)}, u32[]{:S(2)}) collective-permute-start(bf16[32,384]{1,0:T(8,128)(2,1)S(1)} %fusion.2), channel_id=1, source_target_pairs={{0,1},{1,0},{2,3},{3,2},{4,5},{5,4},{6,7},{7,6},{8,9},{9,8},{10,11... | collective-permute-start | bytes 73736 | tf_op jit(solution)/shard_map/ppermute | solution.py:251
  62.4 3.5 %collective-permute-start.8 = (bf16[32,768]{1,0:T(8,128)(2,1)S(1)}, bf16[32,768]{1,0:T(8,128)(2,1)S(1)}, u32[]{:S(2)}, u32[]{:S(2)}) collective-permute-start(bf16[32,768]{1,0:T(8,128)(2,1)S(1)} %maximum_select_fusion), channel_id=1, source_target_pairs={{0,0},{1,5},{2,64},{3,69},{4,128},{5,133},{6,192},{7,197},{8,8},{9... | collective-permute-start | bytes 147464 | tf_op jit(solution)/shard_map/ppermute | solution.py:279
  71.0 2.8 %back.4 = (bf16[4,8,32,384]{3,2,1,0:T(8,128)(2,1)S(1)}, bf16[128,768]{1,0:T(8,128)(2,1)S(1)}) custom-call(s32[4]{0:T(128)S(1)} %pad_add_fusion.at_ref, bf16[2,32,768]{2,1,0:T(8,128)(2,1)S(1)} %pad_maximum_fusion.first_ref, bf16[2,32,768]{2,1,0:T(8,128)(2,1)S(1)} %collective-permute-done.10.second_ref, bf16[4,768,384]{2,1,0:T(8,128)(2,1)S(1)} %split.2.mine_ref, ...), custom_call_target="tpu_custom_call" | custom-call | flops 603979776 | bytes 6000000 | tf_op jit(solution)/shard_map/back/pallas_call | solution.py:176
  73.8 18.4 %all_to_all.31 = bf16[4,8,32,384]{3,2,1,0:T(8,128)(2,1)S(1)} all-to-all(bf16[4,8,32,384]{3,2,1,0:T(8,128)(2,1)S(1)} %get-tuple-element.26), channel_id=1, replica_groups=mesh['y'=4,'z'=8,'x'=4,'core'=2] {'y'}, dimensions={0} | all-to-all | bytes 1572864 | tf_op jit(solution)/shard_map/all_to_all | solution.py:269
  93.0 12.0 %all_to_all.32 = bf16[8,32,384]{2,1,0:T(8,128)(2,1)S(1)} all-to-all(bf16[8,32,384]{2,1,0:T(8,128)(2,1)} %reduce_sum.65), channel_id=1, replica_groups=mesh['y'=4,'z'=8,'x'=4,'core'=2] {'z'}, dimensions={0} | all-to-all | bytes 393216 | tf_op jit(solution)/shard_map/all_to_all | solution.py:269
  105.8 3.0 %collective-permute-start.11 = (bf16[32,384]{1,0:T(8,128)(2,1)S(1)}, bf16[32,384]{1,0:T(8,128)(2,1)S(1)}, u32[]{:S(2)}, u32[]{:S(2)}) collective-permute-start(bf16[32,384]{1,0:T(8,128)(2,1)S(1)} %fusion.1), channel_id=1, source_target_pairs={{0,1},{1,0},{2,3},{3,2},{4,5},{5,4},{6,7},{7,6},{8,9},{9,8},{10,11... | collective-permute-start | bytes 73736 | tf_op jit(solution)/shard_map/ppermute | solution.py:251
  109.6 2.4 %collective-permute-start.12 = (bf16[32,768]{1,0:T(8,128)(2,1)S(1)}, bf16[32,768]{1,0:T(8,128)(2,1)S(1)}, u32[]{:S(2)}, u32[]{:S(2)}) collective-permute-start(bf16[32,768]{1,0:T(8,128)(2,1)S(1)} %maximum_select_fusion.1), channel_id=1, source_target_pairs={{0,0},{1,5},{2,64},{3,69},{4,128},{5,133},{6,192},{7,197},{8,8},{9... | collective-permute-start | bytes 147464 | tf_op jit(solution)/shard_map/ppermute | solution.py:279
  113.7 2.3 %collective-permute-done.12 = bf16[32,768]{1,0:T(8,128)(2,1)S(1)} collective-permute-done((bf16[32,768]{1,0:T(8,128)(2,1)S(1)}, bf16[32,768]{1,0:T(8,128)(2,1)S(1)}, u32[]{:S(2)}, u32[]{:S(2)}) %collective-permute-start.12) | collective-permute-done | bytes 49184 | tf_op jit(solution)/shard_map/ppermute | solution.py:279
  116.4 2.8 %collective-permute-start.14 = (bf16[2,32,768]{2,1,0:T(8,128)(2,1)S(1)}, bf16[2,32,768]{2,1,0:T(8,128)(2,1)S(1)}, u32[]{:S(2)}, u32[]{:S(2)}) collective-permute-start(bf16[2,32,768]{2,1,0:T(8,128)(2,1)S(1)} %pad_maximum_fusion.1.first_ref), channel_id=1, source_target_pairs={{0,1},{1,0},{2,3},{3,2},{4,5},{5,4},{6,7},{7,6},{8,9},{9,8},{10,11... | collective-permute-start | bytes 294920 | tf_op jit(solution)/shard_map/ppermute | solution.py:251
  120.1 2.8 %back.5 = (bf16[4,8,32,384]{3,2,1,0:T(8,128)(2,1)S(1)}, bf16[128,768]{1,0:T(8,128)(2,1)S(1)}) custom-call(s32[4]{0:T(128)S(1)} %pad_add_fusion.at_ref, bf16[2,32,768]{2,1,0:T(8,128)(2,1)S(1)} %pad_maximum_fusion.1.first_ref, bf16[2,32,768]{2,1,0:T(8,128)(2,1)S(1)} %collective-permute-done.14.second_ref, bf16[4,768,384]{2,1,0:T(8,128)(2,1)S(1)} %split.2.mine_ref, ...), custom_call_target="tpu_custom_call" | custom-call | flops 603979776 | bytes 6000000 | tf_op jit(solution)/shard_map/back/pallas_call | solution.py:176
  122.9 15.5 %all_to_all.33 = bf16[4,8,32,384]{3,2,1,0:T(8,128)(2,1)S(1)} all-to-all(bf16[4,8,32,384]{3,2,1,0:T(8,128)(2,1)S(1)} %get-tuple-element.28), channel_id=1, replica_groups=mesh['y'=4,'z'=8,'x'=4,'core'=2] {'y'}, dimensions={0} | all-to-all | bytes 1572864 | tf_op jit(solution)/shard_map/all_to_all | solution.py:269
  138.5 11.1 %all_to_all.34 = bf16[8,32,384]{2,1,0:T(8,128)(2,1)S(1)} all-to-all(bf16[8,32,384]{2,1,0:T(8,128)(2,1)S(1)} %reduce_sum.67), channel_id=1, replica_groups=mesh['y'=4,'z'=8,'x'=4,'core'=2] {'z'}, dimensions={0} | all-to-all | bytes 393216 | tf_op jit(solution)/shard_map/all_to_all | solution.py:269
  150.4 3.0 %collective-permute-start.15 = (bf16[32,384]{1,0:T(8,128)(2,1)S(1)}, bf16[32,384]{1,0:T(8,128)(2,1)S(1)}, u32[]{:S(2)}, u32[]{:S(2)}) collective-permute-start(bf16[32,384]{1,0:T(8,128)(2,1)S(1)} %fusion), channel_id=1, source_target_pairs={{0,1},{1,0},{2,3},{3,2},{4,5},{5,4},{6,7},{7,6},{8,9},{9,8},{10,11... | collective-permute-start | bytes 73736 | tf_op jit(solution)/shard_map/ppermute | solution.py:251
  154.2 3.8 %collective-permute-start.16 = (bf16[32,768]{1,0:T(8,128)(2,1)S(1)}, bf16[32,768]{1,0:T(8,128)(2,1)S(1)}, u32[]{:S(2)}, u32[]{:S(2)}) collective-permute-start(bf16[32,768]{1,0:T(8,128)(2,1)S(1)} %maximum_select_fusion.2), channel_id=1, source_target_pairs={{0,0},{1,5},{2,64},{3,69},{4,128},{5,133},{6,192},{7,197},{8,8},{9... | collective-permute-start | bytes 147464 | tf_op jit(solution)/shard_map/ppermute | solution.py:279
  162.1 2.8 %collective-permute-start.18 = (bf16[2,32,768]{2,1,0:T(8,128)(2,1)S(1)}, bf16[2,32,768]{2,1,0:T(8,128)(2,1)S(1)}, u32[]{:S(2)}, u32[]{:S(2)}) collective-permute-start(bf16[2,32,768]{2,1,0:T(8,128)(2,1)S(1)} %pad_maximum_fusion.2.first_ref), channel_id=1, source_target_pairs={{0,1},{1,0},{2,3},{3,2},{4,5},{5,4},{6,7},{7,6},{8,9},{9,8},{10,11... | collective-permute-start | bytes 294920 | tf_op jit(solution)/shard_map/ppermute | solution.py:251
  165.8 6.3 %outer.1 = bf16[768,3072]{1,0:T(8,128)(2,1)} custom-call(s32[4]{0:T(128)S(1)} %pad_add_fusion.at_ref, bf16[128,768]{1,0:T(8,128)(2,1)S(1)} %get-tuple-element.20.g4, bf16[128,768]{1,0:T(8,128)(2,1)S(1)} %get-tuple-element.25.g3, bf16[128,768]{1,0:T(8,128)(2,1)S(1)} %get-tuple-element.27.g2, bf16[2,32,768]{2,1,0:T(8,128)(2,1)S(1)} %pad_maximum_fusion.2.first_ref, ...), custom_call_target="tpu_custom_call" | custom-call | flops 2415919104 | bytes 8000000 | tf_op jit(solution)/shard_map/outer/pallas_call | solution.py:228
  (50 shorter events, 32.3 us)
Async XLA Ops:
  1.8 4.2 %collective-permute-start = (bf16[128,384]{1,0:T(8,128)(2,1)S(1)}, bf16[128,384]{1,0:T(8,128)(2,1)S(1)}, u32[]{:S(2)}, u32[]{:S(2)}) collective-permute-start(bf16[128,384]{1,0:T(8,128)(2,1)S(1)} %get-tuple-element.18), channel_id=1, source_target_pairs={{0,1},{1,0},{2,3},{3,2},{4,5},{5,4},{6,7},{7,6},{8,9},{9,8},{10,11... | collective-permute-start | bytes 294920 | tf_op jit(solution)/shard_map/ppermute | solution.py:251
  9.7 10.7 %collective-permute-start.5 = (bf16[4,768,384]{2,1,0:T(8,128)(2,1)}, bf16[4,768,384]{2,1,0:T(8,128)(2,1)}, u32[]{:S(2)}, u32[]{:S(2)}) collective-permute-start(bf16[4,768,384]{2,1,0:T(8,128)(2,1)} %split.3), channel_id=1, source_target_pairs={{0,1},{1,0},{2,3},{3,2},{4,5},{5,4},{6,7},{7,6},{8,9},{9,8},{10,11... | collective-permute-start | bytes 7077896 | tf_op jit(solution)/shard_map/ppermute | solution.py:251
  10.1 4.9 %collective-permute-start.1 = (bf16[128,384]{1,0:T(8,128)(2,1)S(1)}, bf16[128,384]{1,0:T(8,128)(2,1)S(1)}, u32[]{:S(2)}, u32[]{:S(2)}) collective-permute-start(bf16[128,384]{1,0:T(8,128)(2,1)S(1)} %broadcast_select_fusion), channel_id=1, source_target_pairs={{0,2},{1,3},{8,10},{9,11},{16,18},{17,19},{24,26},{25,27},{32,34},... | collective-permute-start | bytes 294920 | tf_op jit(solution)/shard_map/ppermute | solution.py:257
  11.5 4.2 %collective-permute-start.2 = (bf16[128,384]{1,0:T(8,128)(2,1)S(1)}, bf16[128,384]{1,0:T(8,128)(2,1)S(1)}, u32[]{:S(2)}, u32[]{:S(2)}) collective-permute-start(bf16[128,384]{1,0:T(8,128)(2,1)S(1)} %broadcast_select_fusion), channel_id=1, source_target_pairs={{0,4},{1,5},{8,12},{9,13},{16,20},{17,21},{24,28},{25,29},{32,36},... | collective-permute-start | bytes 294920 | tf_op jit(solution)/shard_map/ppermute | solution.py:257
  13.7 3.3 %collective-permute-start.3 = (bf16[128,384]{1,0:T(8,128)(2,1)S(1)}, bf16[128,384]{1,0:T(8,128)(2,1)S(1)}, u32[]{:S(2)}, u32[]{:S(2)}) collective-permute-start(bf16[128,384]{1,0:T(8,128)(2,1)S(1)} %broadcast_select_fusion), channel_id=1, source_target_pairs={{0,6},{1,7},{8,14},{9,15},{16,22},{17,23},{24,30},{25,31},{32,38},... | collective-permute-start | bytes 294920 | tf_op jit(solution)/shard_map/ppermute | solution.py:257
  17.0 3.3 %collective-permute-start.4 = (bf16[128,384]{1,0:T(8,128)(2,1)S(1)}, bf16[128,384]{1,0:T(8,128)(2,1)S(1)}, u32[]{:S(2)}, u32[]{:S(2)}) collective-permute-start(bf16[128,384]{1,0:T(8,128)(2,1)S(1)} %add_select_fusion.first_ref), channel_id=1, source_target_pairs={{0,1},{1,0},{2,3},{3,2},{4,5},{5,4},{6,7},{7,6},{8,9},{9,8},{10,11... | collective-permute-start | bytes 294920 | tf_op jit(solution)/shard_map/ppermute | solution.py:251
  41.8 16.7 %all-to-all-start.1 = ((bf16[8,32,384]{2,1,0:T(8,128)(2,1)}), bf16[8,32,384]{2,1,0:T(8,128)(2,1)S(1)}, u32[]{:S(2)}, u32[]{:S(2)}) async-start(bf16[8,32,384]{2,1,0:T(8,128)(2,1)} %reduce_sum.63), calls=%async_computation.1 | async-start | bytes 393216 | tf_op jit(solution)/shard_map/all_to_all | solution.py:269
  51.8 2.4 %collective-permute-start.6 = (bf16[3,32,384]{2,1,0:T(8,128)(2,1)S(1)}, bf16[3,32,384]{2,1,0:T(8,128)(2,1)S(1)}, u32[]{:S(2)}, u32[]{:S(2)}) collective-permute-start(bf16[3,32,384]{2,1,0:T(8,128)(2,1)S(1)} %get-tuple-element.24), channel_id=1, source_target_pairs={{0,1},{1,0},{2,3},{3,2},{4,5},{5,4},{6,7},{7,6},{8,9},{9,8},{10,11... | collective-permute-start | bytes 221192 | tf_op jit(solution)/shard_map/ppermute | solution.py:251
  54.3 19.5 %copy-start = (bf16[3,32,384]{2,1,0:T(8,128)(2,1)}, bf16[3,32,384]{2,1,0:T(8,128)(2,1)S(1)}, u32[]{:S(2)}) copy-start(bf16[3,32,384]{2,1,0:T(8,128)(2,1)S(1)} %broadcast_select_fusion.1) | copy-start | bytes 221188
  58.5 3.9 %collective-permute-start.7 = (bf16[32,384]{1,0:T(8,128)(2,1)S(1)}, bf16[32,384]{1,0:T(8,128)(2,1)S(1)}, u32[]{:S(2)}, u32[]{:S(2)}) collective-permute-start(bf16[32,384]{1,0:T(8,128)(2,1)S(1)} %fusion.2), channel_id=1, source_target_pairs={{0,1},{1,0},{2,3},{3,2},{4,5},{5,4},{6,7},{7,6},{8,9},{9,8},{10,11... | collective-permute-start | bytes 73736 | tf_op jit(solution)/shard_map/ppermute | solution.py:251
  62.4 6.3 %collective-permute-start.8 = (bf16[32,768]{1,0:T(8,128)(2,1)S(1)}, bf16[32,768]{1,0:T(8,128)(2,1)S(1)}, u32[]{:S(2)}, u32[]{:S(2)}) collective-permute-start(bf16[32,768]{1,0:T(8,128)(2,1)S(1)} %maximum_select_fusion), channel_id=1, source_target_pairs={{0,0},{1,5},{2,64},{3,69},{4,128},{5,133},{6,192},{7,197},{8,8},{9... | collective-permute-start | bytes 147464 | tf_op jit(solution)/shard_map/ppermute | solution.py:279
  66.0 3.3 %collective-permute-start.9 = (bf16[32,768]{1,0:T(8,128)(2,1)S(1)}, bf16[32,768]{1,0:T(8,128)(2,1)S(1)}, u32[]{:S(2)}, u32[]{:S(2)}) collective-permute-start(bf16[32,768]{1,0:T(8,128)(2,1)S(1)} %maximum_select_fusion), channel_id=1, source_target_pairs={{0,2},{1,7},{2,66},{3,71},{4,130},{5,135},{6,194},{7,199},{8,10},{... | collective-permute-start | bytes 147464 | tf_op jit(solution)/shard_map/ppermute | solution.py:279
  69.3 1.7 %collective-permute-start.10 = (bf16[2,32,768]{2,1,0:T(8,128)(2,1)S(1)}, bf16[2,32,768]{2,1,0:T(8,128)(2,1)S(1)}, u32[]{:S(2)}, u32[]{:S(2)}) collective-permute-start(bf16[2,32,768]{2,1,0:T(8,128)(2,1)S(1)} %pad_maximum_fusion.first_ref), channel_id=1, source_target_pairs={{0,1},{1,0},{2,3},{3,2},{4,5},{5,4},{6,7},{7,6},{8,9},{9,8},{10,11... | collective-permute-start | bytes 294920 | tf_op jit(solution)/shard_map/ppermute | solution.py:251
  105.8 3.8 %collective-permute-start.11 = (bf16[32,384]{1,0:T(8,128)(2,1)S(1)}, bf16[32,384]{1,0:T(8,128)(2,1)S(1)}, u32[]{:S(2)}, u32[]{:S(2)}) collective-permute-start(bf16[32,384]{1,0:T(8,128)(2,1)S(1)} %fusion.1), channel_id=1, source_target_pairs={{0,1},{1,0},{2,3},{3,2},{4,5},{5,4},{6,7},{7,6},{8,9},{9,8},{10,11... | collective-permute-start | bytes 73736 | tf_op jit(solution)/shard_map/ppermute | solution.py:251
  109.6 6.3 %collective-permute-start.12 = (bf16[32,768]{1,0:T(8,128)(2,1)S(1)}, bf16[32,768]{1,0:T(8,128)(2,1)S(1)}, u32[]{:S(2)}, u32[]{:S(2)}) collective-permute-start(bf16[32,768]{1,0:T(8,128)(2,1)S(1)} %maximum_select_fusion.1), channel_id=1, source_target_pairs={{0,0},{1,5},{2,64},{3,69},{4,128},{5,133},{6,192},{7,197},{8,8},{9... | collective-permute-start | bytes 147464 | tf_op jit(solution)/shard_map/ppermute | solution.py:279
  112.0 4.3 %collective-permute-start.13 = (bf16[32,768]{1,0:T(8,128)(2,1)S(1)}, bf16[32,768]{1,0:T(8,128)(2,1)S(1)}, u32[]{:S(2)}, u32[]{:S(2)}) collective-permute-start(bf16[32,768]{1,0:T(8,128)(2,1)S(1)} %maximum_select_fusion.1), channel_id=1, source_target_pairs={{0,2},{1,7},{2,66},{3,71},{4,130},{5,135},{6,194},{7,199},{8,10},{... | collective-permute-start | bytes 147464 | tf_op jit(solution)/shard_map/ppermute | solution.py:279
  116.4 3.7 %collective-permute-start.14 = (bf16[2,32,768]{2,1,0:T(8,128)(2,1)S(1)}, bf16[2,32,768]{2,1,0:T(8,128)(2,1)S(1)}, u32[]{:S(2)}, u32[]{:S(2)}) collective-permute-start(bf16[2,32,768]{2,1,0:T(8,128)(2,1)S(1)} %pad_maximum_fusion.1.first_ref), channel_id=1, source_target_pairs={{0,1},{1,0},{2,3},{3,2},{4,5},{5,4},{6,7},{7,6},{8,9},{9,8},{10,11... | collective-permute-start | bytes 294920 | tf_op jit(solution)/shard_map/ppermute | solution.py:251
  150.4 3.8 %collective-permute-start.15 = (bf16[32,384]{1,0:T(8,128)(2,1)S(1)}, bf16[32,384]{1,0:T(8,128)(2,1)S(1)}, u32[]{:S(2)}, u32[]{:S(2)}) collective-permute-start(bf16[32,384]{1,0:T(8,128)(2,1)S(1)} %fusion), channel_id=1, source_target_pairs={{0,1},{1,0},{2,3},{3,2},{4,5},{5,4},{6,7},{7,6},{8,9},{9,8},{10,11... | collective-permute-start | bytes 73736 | tf_op jit(solution)/shard_map/ppermute | solution.py:251
  154.2 6.3 %collective-permute-start.16 = (bf16[32,768]{1,0:T(8,128)(2,1)S(1)}, bf16[32,768]{1,0:T(8,128)(2,1)S(1)}, u32[]{:S(2)}, u32[]{:S(2)}) collective-permute-start(bf16[32,768]{1,0:T(8,128)(2,1)S(1)} %maximum_select_fusion.2), channel_id=1, source_target_pairs={{0,0},{1,5},{2,64},{3,69},{4,128},{5,133},{6,192},{7,197},{8,8},{9... | collective-permute-start | bytes 147464 | tf_op jit(solution)/shard_map/ppermute | solution.py:279
  158.0 4.0 %collective-permute-start.17 = (bf16[32,768]{1,0:T(8,128)(2,1)S(1)}, bf16[32,768]{1,0:T(8,128)(2,1)S(1)}, u32[]{:S(2)}, u32[]{:S(2)}) collective-permute-start(bf16[32,768]{1,0:T(8,128)(2,1)S(1)} %maximum_select_fusion.2), channel_id=1, source_target_pairs={{0,2},{1,7},{2,66},{3,71},{4,130},{5,135},{6,194},{7,199},{8,10},{... | collective-permute-start | bytes 147464 | tf_op jit(solution)/shard_map/ppermute | solution.py:279
  162.1 3.7 %collective-permute-start.18 = (bf16[2,32,768]{2,1,0:T(8,128)(2,1)S(1)}, bf16[2,32,768]{2,1,0:T(8,128)(2,1)S(1)}, u32[]{:S(2)}, u32[]{:S(2)}) collective-permute-start(bf16[2,32,768]{2,1,0:T(8,128)(2,1)S(1)} %pad_maximum_fusion.2.first_ref), channel_id=1, source_target_pairs={{0,1},{1,0},{2,3},{3,2},{4,5},{5,4},{6,7},{7,6},{8,9},{9,8},{10,11... | collective-permute-start | bytes 294920 | tf_op jit(solution)/shard_map/ppermute | solution.py:251

commit v3 on v2

--- a/solution.py
+++ b/solution.py
@@ -15,7 +15,7 @@
 QUARTER = 768
 TRIALS = 128
 SLICE = 32
-SPLIT, ROWS, BACK, OUTER, KEEP = 52, 52, 8, 52, 48
+SPLIT, ROWS, BACK, OUTER, KEEP = 48, 52, 8, 52, 48
 COLS = 3072
 VMEM = pl.BlockSpec(memory_space=pltpu.VMEM)
 SMEM = pl.BlockSpec(memory_space=pltpu.SMEM)
@@ -265,11 +265,8 @@
     for step in range(STEPS - 1, 0, -1):
         sums, whole_grad = back(at, pair, mine, theirs)
         full.append(whole_grad)
-        for axis in ("y", "z"):
-            sums = lax.all_to_all(sums, axis, 0, 0, tiled=True)
-            sums = jnp.sum(sums.astype(jnp.float32), axis=0)
-            if axis == "y":
-                sums = sums.astype(jnp.bfloat16)
+        sums = lax.all_to_all(sums.reshape(Y * Z, SLICE, HALF), ("y", "z"), 0, 0, tiled=True)
+        sums = jnp.sum(sums.astype(jnp.float32), axis=0)
         rate = before[step - 1].astype(jnp.float32)
         share = (sums * (1.0 - rate * rate)).astype(jnp.bfloat16)
         other = swapped(share)

time: 174 us -> 171 us (0.983)
  blocking collectives: 74.8 us -> 55.1 us
  waiting for transfers between devices: 21 us -> 35.3 us
  starting transfers between devices: 48.5 us -> 52.3 us
  other arithmetic: 3.58 us -> 0.59 us
    all_to_all x5 -> x2, blocking collectives: 74.8 us -> 55.1 us  [whole(): lax.all_to_all(sums.reshape(Y * Z, SLICE, HALF), ('y', 'z'), 0, 0, tiled=...]
    all_to_all x1, waiting for transfers between devices: 4.18 us -> 16.9 us  [whole(): lax.all_to_all(sums.reshape(Y * Z, SLICE, HALF), ('y', 'z'), 0, 0, tiled=...]
    all_to_all x1, starting transfers between devices: 8.18 us -> 13 us  [whole(): lax.all_to_all(sums.reshape(Y * Z, SLICE, HALF), ('y', 'z'), 0, 0, tiled=...]
    ppermute x6, starting transfers between devices: 13.7 us -> 10.8 us  [whole(): lax.ppermute(share, EVERY, across(j))]
    ppermute x10, starting transfers between devices: 21.7 us -> 23.6 us  [swapped(): return lax.ppermute(array, 'core', SWAP)]
  transfers between devices with their start and end apart: 20 -> 20, of which waited for: 17 -> 16; matrix products, arithmetic and copies ran while one was open for 0% -> 0% of each run, Pallas kernels for 2% -> 2%
where the time goes in v3:
time: 171 us; the launch traced here: 169 us
  blocking collectives  55.1 us (32%)
  starting transfers between devices  52.3 us (31%)
  waiting for transfers between devices  35.3 us (21%)
  Pallas kernels  24.9 us (15%)
    all_to_all x2, blocking collectives, whole(): lax.all_to_all(sums.reshape(Y * Z, SLICE, HALF), ('y', 'z'), 0, 0, tiled=...  55.1 us
    ppermute x10, starting transfers between devices, swapped(): return lax.ppermute(array, 'core', SWAP)  23.6 us
    all_to_all x1, waiting for transfers between devices, whole(): lax.all_to_all(sums.reshape(Y * Z, SLICE, HALF), ('y', 'z'), 0, 0, tiled=...  16.9 us
    all_to_all x1, starting transfers between devices, whole(): lax.all_to_all(sums.reshape(Y * Z, SLICE, HALF), ('y', 'z'), 0, 0, tiled=...  13 us
    ppermute x6, starting transfers between devices, whole(): lax.ppermute(share, EVERY, across(j))  10.8 us
    pallas_call x3, Pallas kernels, back(): pl.pallas_call(back_kernel, in_specs=[SMEM, VMEM, VMEM, VMEM, HBM], out_s...  9.18 us
    ppermute x6, waiting for transfers between devices, whole(): lax.ppermute(share, EVERY, across(j))  9.12 us
    ppermute x10, waiting for transfers between devices, swapped(): return lax.ppermute(array, 'core', SWAP)  7.31 us
  transfers between devices with their start and end apart: 20, of which 16 were waited for; matrix products, arithmetic and copies ran while one was open for 0% of the time, Pallas kernels for 2%

profile of v3, /device:TPU:1, one launch (start us, length us, event | category | flops | bytes accessed | tf_op | source)
XLA Modules:
  0.0 168.5 jit_solution(655157946882761300)
XLA Ops:
  1.8 3.3 %collective-permute-start = (bf16[128,384]{1,0:T(8,128)(2,1)S(1)}, bf16[128,384]{1,0:T(8,128)(2,1)S(1)}, u32[]{:S(2)}, u32[]{:S(2)}) collective-permute-start(bf16[128,384]{1,0:T(8,128)(2,1)S(1)} %get-tuple-element.18), channel_id=1, source_target_pairs={{0,1},{1,0},{2,3},{3,2},{4,5},{5,4},{6,7},{7,6},{8,9},{9,8},{10,11... | collective-permute-start | bytes 294920 | tf_op jit(solution)/shard_map/ppermute | solution.py:251
  6.1 3.6 %split.3 = bf16[4,768,384]{2,1,0:T(8,128)(2,1)} custom-call(s32[4]{0:T(128)S(1)} %pad_add_fusion.at_ref, bf16[768,3072]{1,0:T(8,128)(2,1)} %w_ref.1), custom_call_target="tpu_custom_call" | custom-call | bytes 4718592 | tf_op jit(solution)/shard_map/split/pallas_call | solution.py:103
  11.5 2.2 %collective-permute-start.2 = (bf16[128,384]{1,0:T(8,128)(2,1)S(1)}, bf16[128,384]{1,0:T(8,128)(2,1)S(1)}, u32[]{:S(2)}, u32[]{:S(2)}) collective-permute-start(bf16[128,384]{1,0:T(8,128)(2,1)S(1)} %broadcast_select_fusion), channel_id=1, source_target_pairs={{0,4},{1,5},{8,12},{9,13},{16,20},{17,21},{24,28},{25,29},{32,36},... | collective-permute-start | bytes 294920 | tf_op jit(solution)/shard_map/ppermute | solution.py:257
  18.1 2.2 %split.2.mine_ref = bf16[4,768,384]{2,1,0:T(8,128)(2,1)S(1)} custom-call(s32[4]{0:T(128)S(1)} %pad_add_fusion.at_ref, bf16[768,3072]{1,0:T(8,128)(2,1)} %w_ref.1), custom_call_target="tpu_custom_call" | custom-call | bytes 4718592 | tf_op jit(solution)/shard_map/split/pallas_call | solution.py:103
  20.4 3.6 %back.3 = (bf16[4,8,32,384]{3,2,1,0:T(8,128)(2,1)}, bf16[128,768]{1,0:T(8,128)(2,1)S(1)}) custom-call(s32[4]{0:T(128)S(1)} %pad_add_fusion.at_ref, bf16[128,384]{1,0:T(8,128)(2,1)S(1)} %add_select_fusion.first_ref, bf16[128,384]{1,0:T(8,128)(2,1)S(1)} %collective-permute-done.4.second_ref, bf16[4,768,384]{2,1,0:T(8,128)(2,1)S(1)} %split.2.mine_ref, ...), custom_call_target="tpu_custom_call" | custom-call | flops 603979776 | bytes 6000000 | tf_op jit(solution)/shard_map/back/pallas_call | solution.py:176
  24.0 13.0 %all-to-all-start = ((bf16[32,32,384]{2,1,0:T(8,128)(2,1)}), bf16[32,32,384]{2,1,0:T(8,128)(2,1)S(1)}, u32[]{:S(2)}, u32[]{:S(2)}) async-start(bf16[32,32,384]{2,1,0:T(8,128)(2,1)} %bitcast.4), calls=%async_computation | async-start | bytes 1572864 | tf_op jit(solution)/shard_map/all_to_all | solution.py:268
  37.0 1.8 %rows.1 = (bf16[3,32,384]{2,1,0:T(8,128)(2,1)S(1)}, bf16[3,32,384]{2,1,0:T(8,128)(2,1)S(1)}) custom-call(s32[4]{0:T(128)S(1)} %pad_add_fusion.at_ref, bf16[5,3072,128]{2,1,0:T(8,128)(2,1)} %rates_ref.4), custom_call_target="tpu_custom_call" | custom-call | bytes 600000 | tf_op jit(solution)/shard_map/rows/pallas_call | solution.py:130
  40.2 16.9 %all-to-all-done = bf16[32,32,384]{2,1,0:T(8,128)(2,1)S(1)} async-done(((bf16[32,32,384]{2,1,0:T(8,128)(2,1)}), bf16[32,32,384]{2,1,0:T(8,128)(2,1)S(1)}, u32[]{:S(2)}, u32[]{:S(2)}) %all-to-all-start) | async-done | bytes 786464 | tf_op jit(solution)/shard_map/all_to_all | solution.py:268
  57.2 3.3 %collective-permute-start.7 = (bf16[32,384]{1,0:T(8,128)(2,1)S(1)}, bf16[32,384]{1,0:T(8,128)(2,1)S(1)}, u32[]{:S(2)}, u32[]{:S(2)}) collective-permute-start(bf16[32,384]{1,0:T(8,128)(2,1)S(1)} %fusion.2), channel_id=1, source_target_pairs={{0,1},{1,0},{2,3},{3,2},{4,5},{5,4},{6,7},{7,6},{8,9},{9,8},{10,11... | collective-permute-start | bytes 73736 | tf_op jit(solution)/shard_map/ppermute | solution.py:251
  61.5 3.5 %collective-permute-start.8 = (bf16[32,768]{1,0:T(8,128)(2,1)S(1)}, bf16[32,768]{1,0:T(8,128)(2,1)S(1)}, u32[]{:S(2)}, u32[]{:S(2)}) collective-permute-start(bf16[32,768]{1,0:T(8,128)(2,1)S(1)} %maximum_select_fusion), channel_id=1, source_target_pairs={{0,0},{1,5},{2,64},{3,69},{4,128},{5,133},{6,192},{7,197},{8,8},{9... | collective-permute-start | bytes 147464 | tf_op jit(solution)/shard_map/ppermute | solution.py:276
  65.6 2.3 %collective-permute-done.8 = bf16[32,768]{1,0:T(8,128)(2,1)S(1)} collective-permute-done((bf16[32,768]{1,0:T(8,128)(2,1)S(1)}, bf16[32,768]{1,0:T(8,128)(2,1)S(1)}, u32[]{:S(2)}, u32[]{:S(2)}) %collective-permute-start.8) | collective-permute-done | bytes 49184 | tf_op jit(solution)/shard_map/ppermute | solution.py:276
  70.1 2.8 %back.4 = (bf16[4,8,32,384]{3,2,1,0:T(8,128)(2,1)S(1)}, bf16[128,768]{1,0:T(8,128)(2,1)S(1)}) custom-call(s32[4]{0:T(128)S(1)} %pad_add_fusion.at_ref, bf16[2,32,768]{2,1,0:T(8,128)(2,1)S(1)} %pad_maximum_fusion.first_ref, bf16[2,32,768]{2,1,0:T(8,128)(2,1)S(1)} %collective-permute-done.10.second_ref, bf16[4,768,384]{2,1,0:T(8,128)(2,1)S(1)} %split.2.mine_ref, ...), custom_call_target="tpu_custom_call" | custom-call | flops 603979776 | bytes 6000000 | tf_op jit(solution)/shard_map/back/pallas_call | solution.py:176
  72.8 28.7 %all_to_all.15 = bf16[32,32,384]{2,1,0:T(8,128)(2,1)S(1)} all-to-all(bf16[32,32,384]{2,1,0:T(8,128)(2,1)S(1)} %bitcast.26), channel_id=1, replica_groups=mesh['y'=4,'z'=8,'x'=4,'core'=2] {'y','z'}, dimensions={0} | all-to-all | bytes 1572864 | tf_op jit(solution)/shard_map/all_to_all | solution.py:268
  101.6 4.8 %collective-permute-start.11 = (bf16[32,384]{1,0:T(8,128)(2,1)S(1)}, bf16[32,384]{1,0:T(8,128)(2,1)S(1)}, u32[]{:S(2)}, u32[]{:S(2)}) collective-permute-start(bf16[32,384]{1,0:T(8,128)(2,1)S(1)} %fusion.1), channel_id=1, source_target_pairs={{0,1},{1,0},{2,3},{3,2},{4,5},{5,4},{6,7},{7,6},{8,9},{9,8},{10,11... | collective-permute-start | bytes 73736 | tf_op jit(solution)/shard_map/ppermute | solution.py:251
  107.3 1.9 %collective-permute-start.12 = (bf16[32,768]{1,0:T(8,128)(2,1)S(1)}, bf16[32,768]{1,0:T(8,128)(2,1)S(1)}, u32[]{:S(2)}, u32[]{:S(2)}) collective-permute-start(bf16[32,768]{1,0:T(8,128)(2,1)S(1)} %maximum_select_fusion.1), channel_id=1, source_target_pairs={{0,0},{1,5},{2,64},{3,69},{4,128},{5,133},{6,192},{7,197},{8,8},{9... | collective-permute-start | bytes 147464 | tf_op jit(solution)/shard_map/ppermute | solution.py:276
  109.9 3.8 %collective-permute-done.12 = bf16[32,768]{1,0:T(8,128)(2,1)S(1)} collective-permute-done((bf16[32,768]{1,0:T(8,128)(2,1)S(1)}, bf16[32,768]{1,0:T(8,128)(2,1)S(1)}, u32[]{:S(2)}, u32[]{:S(2)}) %collective-permute-start.12) | collective-permute-done | bytes 49184 | tf_op jit(solution)/shard_map/ppermute | solution.py:276
  113.7 1.9 %collective-permute-start.14 = (bf16[2,32,768]{2,1,0:T(8,128)(2,1)S(1)}, bf16[2,32,768]{2,1,0:T(8,128)(2,1)S(1)}, u32[]{:S(2)}, u32[]{:S(2)}) collective-permute-start(bf16[2,32,768]{2,1,0:T(8,128)(2,1)S(1)} %pad_maximum_fusion.1.first_ref), channel_id=1, source_target_pairs={{0,1},{1,0},{2,3},{3,2},{4,5},{5,4},{6,7},{7,6},{8,9},{9,8},{10,11... | collective-permute-start | bytes 294920 | tf_op jit(solution)/shard_map/ppermute | solution.py:251
  116.5 2.8 %back.5 = (bf16[4,8,32,384]{3,2,1,0:T(8,128)(2,1)S(1)}, bf16[128,768]{1,0:T(8,128)(2,1)S(1)}) custom-call(s32[4]{0:T(128)S(1)} %pad_add_fusion.at_ref, bf16[2,32,768]{2,1,0:T(8,128)(2,1)S(1)} %pad_maximum_fusion.1.first_ref, bf16[2,32,768]{2,1,0:T(8,128)(2,1)S(1)} %collective-permute-done.14.second_ref, bf16[4,768,384]{2,1,0:T(8,128)(2,1)S(1)} %split.2.mine_ref, ...), custom_call_target="tpu_custom_call" | custom-call | flops 603979776 | bytes 6000000 | tf_op jit(solution)/shard_map/back/pallas_call | solution.py:176
  119.2 26.5 %all_to_all.16 = bf16[32,32,384]{2,1,0:T(8,128)(2,1)S(1)} all-to-all(bf16[32,32,384]{2,1,0:T(8,128)(2,1)S(1)} %bitcast.25), channel_id=1, replica_groups=mesh['y'=4,'z'=8,'x'=4,'core'=2] {'y','z'}, dimensions={0} | all-to-all | bytes 1572864 | tf_op jit(solution)/shard_map/all_to_all | solution.py:268
  145.8 4.8 %collective-permute-start.15 = (bf16[32,384]{1,0:T(8,128)(2,1)S(1)}, bf16[32,384]{1,0:T(8,128)(2,1)S(1)}, u32[]{:S(2)}, u32[]{:S(2)}) collective-permute-start(bf16[32,384]{1,0:T(8,128)(2,1)S(1)} %fusion), channel_id=1, source_target_pairs={{0,1},{1,0},{2,3},{3,2},{4,5},{5,4},{6,7},{7,6},{8,9},{9,8},{10,11... | collective-permute-start | bytes 73736 | tf_op jit(solution)/shard_map/ppermute | solution.py:251
  151.5 3.4 %collective-permute-start.16 = (bf16[32,768]{1,0:T(8,128)(2,1)S(1)}, bf16[32,768]{1,0:T(8,128)(2,1)S(1)}, u32[]{:S(2)}, u32[]{:S(2)}) collective-permute-start(bf16[32,768]{1,0:T(8,128)(2,1)S(1)} %maximum_select_fusion.2), channel_id=1, source_target_pairs={{0,0},{1,5},{2,64},{3,69},{4,128},{5,133},{6,192},{7,197},{8,8},{9... | collective-permute-start | bytes 147464 | tf_op jit(solution)/shard_map/ppermute | solution.py:276
  155.6 2.2 %collective-permute-done.16 = bf16[32,768]{1,0:T(8,128)(2,1)S(1)} collective-permute-done((bf16[32,768]{1,0:T(8,128)(2,1)S(1)}, bf16[32,768]{1,0:T(8,128)(2,1)S(1)}, u32[]{:S(2)}, u32[]{:S(2)}) %collective-permute-start.16) | collective-permute-done | bytes 49184 | tf_op jit(solution)/shard_map/ppermute | solution.py:276
  158.3 2.8 %collective-permute-start.18 = (bf16[2,32,768]{2,1,0:T(8,128)(2,1)S(1)}, bf16[2,32,768]{2,1,0:T(8,128)(2,1)S(1)}, u32[]{:S(2)}, u32[]{:S(2)}) collective-permute-start(bf16[2,32,768]{2,1,0:T(8,128)(2,1)S(1)} %pad_maximum_fusion.2.first_ref), channel_id=1, source_target_pairs={{0,1},{1,0},{2,3},{3,2},{4,5},{5,4},{6,7},{7,6},{8,9},{9,8},{10,11... | collective-permute-start | bytes 294920 | tf_op jit(solution)/shard_map/ppermute | solution.py:251
  162.0 6.3 %outer.1 = bf16[768,3072]{1,0:T(8,128)(2,1)} custom-call(s32[4]{0:T(128)S(1)} %pad_add_fusion.at_ref, bf16[128,768]{1,0:T(8,128)(2,1)S(1)} %get-tuple-element.20.g4, bf16[128,768]{1,0:T(8,128)(2,1)S(1)} %get-tuple-element.25.g3, bf16[128,768]{1,0:T(8,128)(2,1)S(1)} %get-tuple-element.27.g2, bf16[2,32,768]{2,1,0:T(8,128)(2,1)S(1)} %pad_maximum_fusion.2.first_ref, ...), custom_call_target="tpu_custom_call" | custom-call | flops 2415919104 | bytes 8000000 | tf_op jit(solution)/shard_map/outer/pallas_call | solution.py:228
  (42 shorter events, 19.8 us)
Async XLA Ops:
  1.8 4.2 %collective-permute-start = (bf16[128,384]{1,0:T(8,128)(2,1)S(1)}, bf16[128,384]{1,0:T(8,128)(2,1)S(1)}, u32[]{:S(2)}, u32[]{:S(2)}) collective-permute-start(bf16[128,384]{1,0:T(8,128)(2,1)S(1)} %get-tuple-element.18), channel_id=1, source_target_pairs={{0,1},{1,0},{2,3},{3,2},{4,5},{5,4},{6,7},{7,6},{8,9},{9,8},{10,11... | collective-permute-start | bytes 294920 | tf_op jit(solution)/shard_map/ppermute | solution.py:251
  9.7 10.7 %collective-permute-start.5 = (bf16[4,768,384]{2,1,0:T(8,128)(2,1)}, bf16[4,768,384]{2,1,0:T(8,128)(2,1)}, u32[]{:S(2)}, u32[]{:S(2)}) collective-permute-start(bf16[4,768,384]{2,1,0:T(8,128)(2,1)} %split.3), channel_id=1, source_target_pairs={{0,1},{1,0},{2,3},{3,2},{4,5},{5,4},{6,7},{7,6},{8,9},{9,8},{10,11... | collective-permute-start | bytes 7077896 | tf_op jit(solution)/shard_map/ppermute | solution.py:251
  10.1 4.9 %collective-permute-start.1 = (bf16[128,384]{1,0:T(8,128)(2,1)S(1)}, bf16[128,384]{1,0:T(8,128)(2,1)S(1)}, u32[]{:S(2)}, u32[]{:S(2)}) collective-permute-start(bf16[128,384]{1,0:T(8,128)(2,1)S(1)} %broadcast_select_fusion), channel_id=1, source_target_pairs={{0,2},{1,3},{8,10},{9,11},{16,18},{17,19},{24,26},{25,27},{32,34},... | collective-permute-start | bytes 294920 | tf_op jit(solution)/shard_map/ppermute | solution.py:257
  11.5 4.2 %collective-permute-start.2 = (bf16[128,384]{1,0:T(8,128)(2,1)S(1)}, bf16[128,384]{1,0:T(8,128)(2,1)S(1)}, u32[]{:S(2)}, u32[]{:S(2)}) collective-permute-start(bf16[128,384]{1,0:T(8,128)(2,1)S(1)} %broadcast_select_fusion), channel_id=1, source_target_pairs={{0,4},{1,5},{8,12},{9,13},{16,20},{17,21},{24,28},{25,29},{32,36},... | collective-permute-start | bytes 294920 | tf_op jit(solution)/shard_map/ppermute | solution.py:257
  13.7 3.3 %collective-permute-start.3 = (bf16[128,384]{1,0:T(8,128)(2,1)S(1)}, bf16[128,384]{1,0:T(8,128)(2,1)S(1)}, u32[]{:S(2)}, u32[]{:S(2)}) collective-permute-start(bf16[128,384]{1,0:T(8,128)(2,1)S(1)} %broadcast_select_fusion), channel_id=1, source_target_pairs={{0,6},{1,7},{8,14},{9,15},{16,22},{17,23},{24,30},{25,31},{32,38},... | collective-permute-start | bytes 294920 | tf_op jit(solution)/shard_map/ppermute | solution.py:257
  17.0 3.3 %collective-permute-start.4 = (bf16[128,384]{1,0:T(8,128)(2,1)S(1)}, bf16[128,384]{1,0:T(8,128)(2,1)S(1)}, u32[]{:S(2)}, u32[]{:S(2)}) collective-permute-start(bf16[128,384]{1,0:T(8,128)(2,1)S(1)} %add_select_fusion.first_ref), channel_id=1, source_target_pairs={{0,1},{1,0},{2,3},{3,2},{4,5},{5,4},{6,7},{7,6},{8,9},{9,8},{10,11... | collective-permute-start | bytes 294920 | tf_op jit(solution)/shard_map/ppermute | solution.py:251
  24.0 33.1 %all-to-all-start = ((bf16[32,32,384]{2,1,0:T(8,128)(2,1)}), bf16[32,32,384]{2,1,0:T(8,128)(2,1)S(1)}, u32[]{:S(2)}, u32[]{:S(2)}) async-start(bf16[32,32,384]{2,1,0:T(8,128)(2,1)} %bitcast.4), calls=%async_computation | async-start | bytes 1572864 | tf_op jit(solution)/shard_map/all_to_all | solution.py:268
  38.9 1.4 collective-permute-start.6
  57.2 4.2 %collective-permute-start.7 = (bf16[32,384]{1,0:T(8,128)(2,1)S(1)}, bf16[32,384]{1,0:T(8,128)(2,1)S(1)}, u32[]{:S(2)}, u32[]{:S(2)}) collective-permute-start(bf16[32,384]{1,0:T(8,128)(2,1)S(1)} %fusion.2), channel_id=1, source_target_pairs={{0,1},{1,0},{2,3},{3,2},{4,5},{5,4},{6,7},{7,6},{8,9},{9,8},{10,11... | collective-permute-start | bytes 73736 | tf_op jit(solution)/shard_map/ppermute | solution.py:251
  61.5 6.4 %collective-permute-start.8 = (bf16[32,768]{1,0:T(8,128)(2,1)S(1)}, bf16[32,768]{1,0:T(8,128)(2,1)S(1)}, u32[]{:S(2)}, u32[]{:S(2)}) collective-permute-start(bf16[32,768]{1,0:T(8,128)(2,1)S(1)} %maximum_select_fusion), channel_id=1, source_target_pairs={{0,0},{1,5},{2,64},{3,69},{4,128},{5,133},{6,192},{7,197},{8,8},{9... | collective-permute-start | bytes 147464 | tf_op jit(solution)/shard_map/ppermute | solution.py:276
  65.0 3.3 %collective-permute-start.9 = (bf16[32,768]{1,0:T(8,128)(2,1)S(1)}, bf16[32,768]{1,0:T(8,128)(2,1)S(1)}, u32[]{:S(2)}, u32[]{:S(2)}) collective-permute-start(bf16[32,768]{1,0:T(8,128)(2,1)S(1)} %maximum_select_fusion), channel_id=1, source_target_pairs={{0,2},{1,7},{2,66},{3,71},{4,130},{5,135},{6,194},{7,199},{8,10},{... | collective-permute-start | bytes 147464 | tf_op jit(solution)/shard_map/ppermute | solution.py:276
  68.3 1.7 %collective-permute-start.10 = (bf16[2,32,768]{2,1,0:T(8,128)(2,1)S(1)}, bf16[2,32,768]{2,1,0:T(8,128)(2,1)S(1)}, u32[]{:S(2)}, u32[]{:S(2)}) collective-permute-start(bf16[2,32,768]{2,1,0:T(8,128)(2,1)S(1)} %pad_maximum_fusion.first_ref), channel_id=1, source_target_pairs={{0,1},{1,0},{2,3},{3,2},{4,5},{5,4},{6,7},{7,6},{8,9},{9,8},{10,11... | collective-permute-start | bytes 294920 | tf_op jit(solution)/shard_map/ppermute | solution.py:251
  101.6 5.7 %collective-permute-start.11 = (bf16[32,384]{1,0:T(8,128)(2,1)S(1)}, bf16[32,384]{1,0:T(8,128)(2,1)S(1)}, u32[]{:S(2)}, u32[]{:S(2)}) collective-permute-start(bf16[32,384]{1,0:T(8,128)(2,1)S(1)} %fusion.1), channel_id=1, source_target_pairs={{0,1},{1,0},{2,3},{3,2},{4,5},{5,4},{6,7},{7,6},{8,9},{9,8},{10,11... | collective-permute-start | bytes 73736 | tf_op jit(solution)/shard_map/ppermute | solution.py:251
  107.3 6.3 %collective-permute-start.12 = (bf16[32,768]{1,0:T(8,128)(2,1)S(1)}, bf16[32,768]{1,0:T(8,128)(2,1)S(1)}, u32[]{:S(2)}, u32[]{:S(2)}) collective-permute-start(bf16[32,768]{1,0:T(8,128)(2,1)S(1)} %maximum_select_fusion.1), channel_id=1, source_target_pairs={{0,0},{1,5},{2,64},{3,69},{4,128},{5,133},{6,192},{7,197},{8,8},{9... | collective-permute-start | bytes 147464 | tf_op jit(solution)/shard_map/ppermute | solution.py:276
  109.2 4.4 %collective-permute-start.13 = (bf16[32,768]{1,0:T(8,128)(2,1)S(1)}, bf16[32,768]{1,0:T(8,128)(2,1)S(1)}, u32[]{:S(2)}, u32[]{:S(2)}) collective-permute-start(bf16[32,768]{1,0:T(8,128)(2,1)S(1)} %maximum_select_fusion.1), channel_id=1, source_target_pairs={{0,2},{1,7},{2,66},{3,71},{4,130},{5,135},{6,194},{7,199},{8,10},{... | collective-permute-start | bytes 147464 | tf_op jit(solution)/shard_map/ppermute | solution.py:276
  113.7 2.8 %collective-permute-start.14 = (bf16[2,32,768]{2,1,0:T(8,128)(2,1)S(1)}, bf16[2,32,768]{2,1,0:T(8,128)(2,1)S(1)}, u32[]{:S(2)}, u32[]{:S(2)}) collective-permute-start(bf16[2,32,768]{2,1,0:T(8,128)(2,1)S(1)} %pad_maximum_fusion.1.first_ref), channel_id=1, source_target_pairs={{0,1},{1,0},{2,3},{3,2},{4,5},{5,4},{6,7},{7,6},{8,9},{9,8},{10,11... | collective-permute-start | bytes 294920 | tf_op jit(solution)/shard_map/ppermute | solution.py:251
  145.8 5.6 %collective-permute-start.15 = (bf16[32,384]{1,0:T(8,128)(2,1)S(1)}, bf16[32,384]{1,0:T(8,128)(2,1)S(1)}, u32[]{:S(2)}, u32[]{:S(2)}) collective-permute-start(bf16[32,384]{1,0:T(8,128)(2,1)S(1)} %fusion), channel_id=1, source_target_pairs={{0,1},{1,0},{2,3},{3,2},{4,5},{5,4},{6,7},{7,6},{8,9},{9,8},{10,11... | collective-permute-start | bytes 73736 | tf_op jit(solution)/shard_map/ppermute | solution.py:251
  151.5 6.3 %collective-permute-start.16 = (bf16[32,768]{1,0:T(8,128)(2,1)S(1)}, bf16[32,768]{1,0:T(8,128)(2,1)S(1)}, u32[]{:S(2)}, u32[]{:S(2)}) collective-permute-start(bf16[32,768]{1,0:T(8,128)(2,1)S(1)} %maximum_select_fusion.2), channel_id=1, source_target_pairs={{0,0},{1,5},{2,64},{3,69},{4,128},{5,133},{6,192},{7,197},{8,8},{9... | collective-permute-start | bytes 147464 | tf_op jit(solution)/shard_map/ppermute | solution.py:276
  155.0 3.3 %collective-permute-start.17 = (bf16[32,768]{1,0:T(8,128)(2,1)S(1)}, bf16[32,768]{1,0:T(8,128)(2,1)S(1)}, u32[]{:S(2)}, u32[]{:S(2)}) collective-permute-start(bf16[32,768]{1,0:T(8,128)(2,1)S(1)} %maximum_select_fusion.2), channel_id=1, source_target_pairs={{0,2},{1,7},{2,66},{3,71},{4,130},{5,135},{6,194},{7,199},{8,10},{... | collective-permute-start | bytes 147464 | tf_op jit(solution)/shard_map/ppermute | solution.py:276
  158.3 3.7 %collective-permute-start.18 = (bf16[2,32,768]{2,1,0:T(8,128)(2,1)S(1)}, bf16[2,32,768]{2,1,0:T(8,128)(2,1)S(1)}, u32[]{:S(2)}, u32[]{:S(2)}) collective-permute-start(bf16[2,32,768]{2,1,0:T(8,128)(2,1)S(1)} %pad_maximum_fusion.2.first_ref), channel_id=1, source_target_pairs={{0,1},{1,0},{2,3},{3,2},{4,5},{5,4},{6,7},{7,6},{8,9},{9,8},{10,11... | collective-permute-start | bytes 294920 | tf_op jit(solution)/shard_map/ppermute | solution.py:251

commit v4 on v3

--- a/solution.py
+++ b/solution.py
@@ -28,16 +28,13 @@
 
 def across(j):
     return [
-        (flat(y, z, x, core), flat(x, z, y + j + 2 * core, core))
+        (flat(y, z, x, core), flat(x, z, y + 2 * j + core, core))
         for y in range(Y) for z in range(Z) for x in range(X) for core in range(C)
     ]
 
 
 def from_root(shift):
-    return [
-        (flat(y, z, y, core), flat(y, z, y + shift, core))
-        for y in range(Y) for z in range(Z) for core in range(C)
-    ]
+    return [(flat(y, z, y, z // 4), flat(y, z, y + shift, z // 4)) for y in range(Y) for z in range(Z)]
 
 
 def params(mib):
@@ -48,12 +45,7 @@
     return pl.CostEstimate(flops=flops, bytes_accessed=moved, transcendentals=0)
 
 
-def half(core):
-    return pl.ds(pl.multiple_of(core * HALF, 128), HALF)
-
-
-def first_kernel(at_ref, rates_ref, mine_ref, theirs_ref, last_ref, zero_ref, sems):
-    core = at_ref[1]
+def first_kernel(at_ref, rates_ref, out_ref, last_ref, zero_ref, sems):
     rows = pl.ds(pl.multiple_of(at_ref[0] * QUARTER, 16), QUARTER)
     copies = [
         pltpu.make_async_copy(rates_ref.at[STEPS, rows], last_ref, sems.at[0]),
@@ -63,20 +55,17 @@
         copy.start()
     for copy in copies:
         copy.wait()
-    for out_ref, part in ((theirs_ref, 1 - core), (mine_ref, core)):
-        part = pl.ds(pl.multiple_of(part * HALF, 16), HALF)
-        last = last_ref[part, :].astype(jnp.float32)
-        zero = zero_ref[part, :].astype(jnp.float32)
-        out_ref[...] = ((last - zero) * (1.0 - last * last)).astype(jnp.bfloat16).T
+    last = last_ref[...].astype(jnp.float32)
+    zero = zero_ref[...].astype(jnp.float32)
+    out_ref[...] = ((last - zero) * (1.0 - last * last)).astype(jnp.bfloat16).T
 
 
 def first(at, rates):
-    shape = jax.ShapeDtypeStruct((TRIALS, HALF), jnp.bfloat16)
     return pl.pallas_call(
         first_kernel,
         in_specs=[SMEM, HBM],
-        out_specs=[VMEM, VMEM],
-        out_shape=[shape, shape],
+        out_specs=VMEM,
+        out_shape=jax.ShapeDtypeStruct((TRIALS, QUARTER), jnp.bfloat16),
         scratch_shapes=[
             pltpu.VMEM((QUARTER, TRIALS), jnp.bfloat16),
             pltpu.VMEM((QUARTER, TRIALS), jnp.bfloat16),
@@ -143,25 +132,26 @@
     )(at, rates)
 
 
-def fill(at_ref, first_ref, second_ref, g_ref):
+def fill(at_ref, pair_refs, g_ref):
     core, x = at_ref[1], at_ref[3]
-    for ref, part in ((first_ref, core), (second_ref, 1 - core)):
-        if ref.shape == (TRIALS, HALF):
-            g_ref[:, half(part)] = ref[...]
-        else:
-            for j in range(2):
-                slot = (x + 2 * X - j - 2 * part) % X
-                g_ref[pl.ds(pl.multiple_of(slot * SLICE, SLICE), SLICE), :] = ref[j]
-
-
-def back_kernel(at_ref, first_ref, second_ref, mine_ref, theirs_ref, out_ref, g_ref, held_ref, sems):
+    if len(pair_refs) == 1:
+        g_ref[...] = pair_refs[0][...]
+        return
+    for ref, part in zip(pair_refs, (core, 1 - core)):
+        for j in range(2):
+            slot = (x + 2 * X - 2 * j - part) % X
+            g_ref[pl.ds(pl.multiple_of(slot * SLICE, SLICE), SLICE), :] = ref[j]
+
+
+def back_kernel(at_ref, *refs):
+    *pair_refs, mine_ref, theirs_ref, out_ref, g_ref, held_ref, sems = refs
     core = at_ref[1]
     copies = [
         pltpu.make_async_copy(theirs_ref.at[q], held_ref.at[q], sems.at[q]) for q in range(4)
     ]
     for copy in copies:
         copy.start()
-    fill(at_ref, first_ref, second_ref, g_ref)
+    fill(at_ref, pair_refs, g_ref)
     for ref, block in ((mine_ref, core), (held_ref, 1 - core)):
         for q in range(4):
             if ref is held_ref:
@@ -175,7 +165,7 @@
 def back(at, pair, mine, theirs):
     return pl.pallas_call(
         back_kernel,
-        in_specs=[SMEM, VMEM, VMEM, VMEM, HBM],
+        in_specs=[SMEM] + [VMEM] * len(pair) + [VMEM, HBM],
         out_specs=[VMEM, VMEM],
         out_shape=[
             jax.ShapeDtypeStruct((Y, 8, SLICE, HALF), jnp.bfloat16),
@@ -210,7 +200,7 @@
         came(j).start()
     for t, ref in ((3, g4), (2, g3), (1, g2)):
         turned_ref[:, t * TRIALS : (t + 1) * TRIALS] = ref[...].T
-    fill(at_ref, first_ref, second_ref, g_ref)
+    fill(at_ref, (first_ref, second_ref), g_ref)
     turned_ref[:, :TRIALS] = g_ref[...].T
     for j in range(TILES):
         came(j).wait()
@@ -250,17 +240,19 @@
     def swapped(array):
         return lax.ppermute(array, "core", SWAP)
 
-    def of_root_core(mine, theirs):
-        return jnp.where(core == z // 4, mine, swapped(theirs))
-
-    root = of_root_core(*first(at, rates))
+    is_root_core = core == z // 4
+    root = first(at, rates)
     parts = [lax.ppermute(root, EVERY, from_root(shift)) for shift in (1, 2, 3)]
-    own = jnp.where(x == y, root, parts[0] + parts[1] + parts[2])
     late_weights, late_rates, _ = lax.optimization_barrier((weights, rates, root))
     theirs = swapped(split(at, late_weights, True))
     mine = split(at, late_weights, False)
-    before = of_root_core(*rows(at, late_rates))
-    pair = (own, swapped(own))
+    before, other = rows(at, late_rates)
+    before = jnp.where(is_root_core, before, swapped(other))
+    came = jnp.where(x == y, root, parts[0] + parts[1] + parts[2])
+    grad, before = lax.optimization_barrier(
+        (jnp.where(is_root_core, came, swapped(came)), before)
+    )
+    pair = (grad,)
     full = []
     for step in range(STEPS - 1, 0, -1):
         sums, whole_grad = back(at, pair, mine, theirs)

time: 171 us -> 164 us (0.959)
  blocking collectives: 55.1 us -> 83.1 us
  waiting for transfers between devices: 35.3 us -> 12.2 us
  starting transfers between devices: 52.3 us -> 42.3 us
    all_to_all x2 -> x3, blocking collectives: 55.1 us -> 83.1 us  [whole(): lax.all_to_all(sums.reshape(Y * Z, SLICE, HALF), ('y', 'z'), 0, 0, tiled=...]
    all_to_all x1 -> x0, waiting for transfers between devices: 16.9 us -> none  [whole(): lax.all_to_all(sums.reshape(Y * Z, SLICE, HALF), ('y', 'z'), 0, 0, tiled=...]
    all_to_all x1 -> x0, starting transfers between devices: 13 us -> none  [whole(): lax.all_to_all(sums.reshape(Y * Z, SLICE, HALF), ('y', 'z'), 0, 0, tiled=...]
    ppermute x6, waiting for transfers between devices: 9.12 us -> 5.39 us  [whole(): lax.ppermute(share, EVERY, across(j))]
    ppermute x10 -> x9, starting transfers between devices: 23.6 us -> 26.9 us  [swapped(): return lax.ppermute(array, 'core', SWAP)]
    ppermute x3, starting transfers between devices: 4.9 us -> 2.01 us  [whole(): parts = [lax.ppermute(root, EVERY, from_root(shift)) for shift in (1, 2, 3)]]
    ppermute x6, starting transfers between devices: 10.8 us -> 13.4 us  [whole(): lax.ppermute(share, EVERY, across(j))]
    ppermute x3, waiting for transfers between devices: 1.96 us -> 0.01 us  [whole(): parts = [lax.ppermute(root, EVERY, from_root(shift)) for shift in (1, 2, 3)]]
  transfers between devices with their start and end apart: 20 -> 18, of which waited for: 16 -> 11; matrix products, arithmetic and copies ran while one was open for 0% -> 0% of each run, Pallas kernels for 2% -> 2%
where the time goes in v4:
time: 164 us; the launch traced here: 163 us
  blocking collectives  83.1 us (51%)
  starting transfers between devices  42.3 us (26%)
  Pallas kernels  24 us (15%)
  waiting for transfers between devices  12.2 us (7%)
    all_to_all x3, blocking collectives, whole(): lax.all_to_all(sums.reshape(Y * Z, SLICE, HALF), ('y', 'z'), 0, 0, tiled=...  83.1 us
    ppermute x9, starting transfers between devices, swapped(): return lax.ppermute(array, 'core', SWAP)  26.9 us
    ppermute x6, starting transfers between devices, whole(): lax.ppermute(share, EVERY, across(j))  13.4 us
    pallas_call x3, Pallas kernels, back(): pl.pallas_call(back_kernel, in_specs=[SMEM] + [VMEM] * len(pair) + [VMEM,...  8.29 us
    ppermute x9, waiting for transfers between devices, swapped(): return lax.ppermute(array, 'core', SWAP)  6.78 us
    pallas_call x1, Pallas kernels, outer(): pl.pallas_call(outer_kernel, in_specs=[SMEM] + [VMEM] * 5 + [HBM], out_sp...  6.33 us
    pallas_call x2, Pallas kernels, split(): pl.pallas_call(functools.partial(split_kernel, partner=partner), in_specs...  5.8 us
    ppermute x6, waiting for transfers between devices, whole(): lax.ppermute(share, EVERY, across(j))  5.39 us
  transfers between devices with their start and end apart: 18, of which 11 were waited for; matrix products, arithmetic and copies ran while one was open for 0% of the time, Pallas kernels for 2%

profile of v4, /device:TPU:1, one launch (start us, length us, event | category | flops | bytes accessed | tf_op | source)
XLA Modules:
  0.0 162.6 jit_solution(17250056428510781709)
XLA Ops:
  1.8 3.6 %split.3 = bf16[4,768,384]{2,1,0:T(8,128)(2,1)} custom-call(s32[4]{0:T(128)S(1)} %pad_add_fusion.at_ref, bf16[768,3072]{1,0:T(8,128)(2,1)} %w_ref.1), custom_call_target="tpu_custom_call" | custom-call | bytes 4718592 | tf_op jit(solution)/shard_map/split/pallas_call | solution.py:92
  5.4 3.3 %collective-permute-start.5 = (bf16[4,768,384]{2,1,0:T(8,128)(2,1)}, bf16[4,768,384]{2,1,0:T(8,128)(2,1)}, u32[]{:S(2)}, u32[]{:S(2)}) collective-permute-start(bf16[4,768,384]{2,1,0:T(8,128)(2,1)} %split.3), channel_id=1, source_target_pairs={{0,1},{1,0},{2,3},{3,2},{4,5},{5,4},{6,7},{7,6},{8,9},{9,8},{10,11... | collective-permute-start | bytes 7077896 | tf_op jit(solution)/shard_map/ppermute | solution.py:241
  12.6 3.3 %collective-permute-start.4 = (bf16[3,32,384]{2,1,0:T(8,128)(2,1)S(1)}, bf16[3,32,384]{2,1,0:T(8,128)(2,1)S(1)}, u32[]{:S(2)}, u32[]{:S(2)}) collective-permute-start(bf16[3,32,384]{2,1,0:T(8,128)(2,1)S(1)} %get-tuple-element.19), channel_id=1, source_target_pairs={{0,1},{1,0},{2,3},{3,2},{4,5},{5,4},{6,7},{7,6},{8,9},{9,8},{10,11... | collective-permute-start | bytes 221192 | tf_op jit(solution)/shard_map/ppermute | solution.py:241
  15.9 2.2 %split.2.refs_1_.refs_2_ = bf16[4,768,384]{2,1,0:T(8,128)(2,1)S(1)} custom-call(s32[4]{0:T(128)S(1)} %pad_add_fusion.at_ref, bf16[768,3072]{1,0:T(8,128)(2,1)} %w_ref.1), custom_call_target="tpu_custom_call" | custom-call | bytes 4718592 | tf_op jit(solution)/shard_map/split/pallas_call | solution.py:92
  19.7 2.7 %back.3 = (bf16[4,8,32,384]{3,2,1,0:T(8,128)(2,1)S(1)}, bf16[128,768]{1,0:T(8,128)(2,1)S(1)}) custom-call(s32[4]{0:T(128)S(1)} %pad_add_fusion.at_ref, bf16[128,768]{1,0:T(8,128)(2,1)S(1)} %broadcast_select_fusion.refs_0_, bf16[4,768,384]{2,1,0:T(8,128)(2,1)S(1)} %split.2.refs_1_.refs_2_, bf16[4,768,384]{2,1,0:T(8,128)(2,1)} %collective-permute-done.5.refs_2_.refs_3_), custom_call_target="tpu_custom_call" | custom-call | flops 603979776 | bytes 6000000 | tf_op jit(solution)/shard_map/back/pallas_call | solution.py:166
  22.5 30.4 %all_to_all.15 = bf16[32,32,384]{2,1,0:T(8,128)(2,1)S(1)} all-to-all(bf16[32,32,384]{2,1,0:T(8,128)(2,1)S(1)} %bitcast.27), channel_id=1, replica_groups=mesh['y'=4,'z'=8,'x'=4,'core'=2] {'y','z'}, dimensions={0} | all-to-all | bytes 1572864 | tf_op jit(solution)/shard_map/all_to_all | solution.py:260
  53.0 3.5 %collective-permute-start.6 = (bf16[32,384]{1,0:T(8,128)(2,1)S(1)}, bf16[32,384]{1,0:T(8,128)(2,1)S(1)}, u32[]{:S(2)}, u32[]{:S(2)}) collective-permute-start(bf16[32,384]{1,0:T(8,128)(2,1)S(1)} %fusion.2), channel_id=1, source_target_pairs={{0,1},{1,0},{2,3},{3,2},{4,5},{5,4},{6,7},{7,6},{8,9},{9,8},{10,11... | collective-permute-start | bytes 73736 | tf_op jit(solution)/shard_map/ppermute | solution.py:241
  57.4 2.1 %collective-permute-start.7 = (bf16[32,768]{1,0:T(8,128)(2,1)S(1)}, bf16[32,768]{1,0:T(8,128)(2,1)S(1)}, u32[]{:S(2)}, u32[]{:S(2)}) collective-permute-start(bf16[32,768]{1,0:T(8,128)(2,1)S(1)} %maximum_select_fusion), channel_id=1, source_target_pairs={{0,0},{1,3},{2,64},{3,67},{4,128},{5,131},{6,192},{7,195},{8,8},{9... | collective-permute-start | bytes 147464 | tf_op jit(solution)/shard_map/ppermute | solution.py:268
  59.5 2.7 %collective-permute-start.8 = (bf16[32,768]{1,0:T(8,128)(2,1)S(1)}, bf16[32,768]{1,0:T(8,128)(2,1)S(1)}, u32[]{:S(2)}, u32[]{:S(2)}) collective-permute-start(bf16[32,768]{1,0:T(8,128)(2,1)S(1)} %maximum_select_fusion), channel_id=1, source_target_pairs={{0,4},{1,7},{2,68},{3,71},{4,132},{5,135},{6,196},{7,199},{8,12},{... | collective-permute-start | bytes 147464 | tf_op jit(solution)/shard_map/ppermute | solution.py:268
  64.2 3.1 %collective-permute-start.9 = (bf16[2,32,768]{2,1,0:T(8,128)(2,1)S(1)}, bf16[2,32,768]{2,1,0:T(8,128)(2,1)S(1)}, u32[]{:S(2)}, u32[]{:S(2)}) collective-permute-start(bf16[2,32,768]{2,1,0:T(8,128)(2,1)S(1)} %pad_maximum_fusion.refs_0_), channel_id=1, source_target_pairs={{0,1},{1,0},{2,3},{3,2},{4,5},{5,4},{6,7},{7,6},{8,9},{9,8},{10,11... | collective-permute-start | bytes 294920 | tf_op jit(solution)/shard_map/ppermute | solution.py:241
  68.2 2.8 %back.4 = (bf16[4,8,32,384]{3,2,1,0:T(8,128)(2,1)S(1)}, bf16[128,768]{1,0:T(8,128)(2,1)S(1)}) custom-call(s32[4]{0:T(128)S(1)} %pad_add_fusion.at_ref, bf16[2,32,768]{2,1,0:T(8,128)(2,1)S(1)} %pad_maximum_fusion.refs_0_, bf16[2,32,768]{2,1,0:T(8,128)(2,1)S(1)} %collective-permute-done.9.refs_1_, bf16[4,768,384]{2,1,0:T(8,128)(2,1)S(1)} %split.2.refs_1_.refs_2_, ...), custom_call_target="tpu_custom_call" | custom-call | flops 603979776 | bytes 6000000 | tf_op jit(solution)/shard_map/back/pallas_call | solution.py:166
  71.0 25.9 %all_to_all.16 = bf16[32,32,384]{2,1,0:T(8,128)(2,1)S(1)} all-to-all(bf16[32,32,384]{2,1,0:T(8,128)(2,1)S(1)} %bitcast.26), channel_id=1, replica_groups=mesh['y'=4,'z'=8,'x'=4,'core'=2] {'y','z'}, dimensions={0} | all-to-all | bytes 1572864 | tf_op jit(solution)/shard_map/all_to_all | solution.py:260
  97.0 4.8 %collective-permute-start.10 = (bf16[32,384]{1,0:T(8,128)(2,1)S(1)}, bf16[32,384]{1,0:T(8,128)(2,1)S(1)}, u32[]{:S(2)}, u32[]{:S(2)}) collective-permute-start(bf16[32,384]{1,0:T(8,128)(2,1)S(1)} %fusion.1), channel_id=1, source_target_pairs={{0,1},{1,0},{2,3},{3,2},{4,5},{5,4},{6,7},{7,6},{8,9},{9,8},{10,11... | collective-permute-start | bytes 73736 | tf_op jit(solution)/shard_map/ppermute | solution.py:241
  102.7 1.9 %collective-permute-start.11 = (bf16[32,768]{1,0:T(8,128)(2,1)S(1)}, bf16[32,768]{1,0:T(8,128)(2,1)S(1)}, u32[]{:S(2)}, u32[]{:S(2)}) collective-permute-start(bf16[32,768]{1,0:T(8,128)(2,1)S(1)} %maximum_select_fusion.1), channel_id=1, source_target_pairs={{0,0},{1,3},{2,64},{3,67},{4,128},{5,131},{6,192},{7,195},{8,8},{9... | collective-permute-start | bytes 147464 | tf_op jit(solution)/shard_map/ppermute | solution.py:268
  104.6 2.1 %collective-permute-start.12 = (bf16[32,768]{1,0:T(8,128)(2,1)S(1)}, bf16[32,768]{1,0:T(8,128)(2,1)S(1)}, u32[]{:S(2)}, u32[]{:S(2)}) collective-permute-start(bf16[32,768]{1,0:T(8,128)(2,1)S(1)} %maximum_select_fusion.1), channel_id=1, source_target_pairs={{0,4},{1,7},{2,68},{3,71},{4,132},{5,135},{6,196},{7,199},{8,12},{... | collective-permute-start | bytes 147464 | tf_op jit(solution)/shard_map/ppermute | solution.py:268
  106.8 2.0 %collective-permute-done.11 = bf16[32,768]{1,0:T(8,128)(2,1)S(1)} collective-permute-done((bf16[32,768]{1,0:T(8,128)(2,1)S(1)}, bf16[32,768]{1,0:T(8,128)(2,1)S(1)}, u32[]{:S(2)}, u32[]{:S(2)}) %collective-permute-start.11) | collective-permute-done | bytes 49184 | tf_op jit(solution)/shard_map/ppermute | solution.py:268
  108.7 1.9 %collective-permute-start.13 = (bf16[2,32,768]{2,1,0:T(8,128)(2,1)S(1)}, bf16[2,32,768]{2,1,0:T(8,128)(2,1)S(1)}, u32[]{:S(2)}, u32[]{:S(2)}) collective-permute-start(bf16[2,32,768]{2,1,0:T(8,128)(2,1)S(1)} %pad_maximum_fusion.1.refs_0_), channel_id=1, source_target_pairs={{0,1},{1,0},{2,3},{3,2},{4,5},{5,4},{6,7},{7,6},{8,9},{9,8},{10,11... | collective-permute-start | bytes 294920 | tf_op jit(solution)/shard_map/ppermute | solution.py:241
  111.6 2.8 %back.5 = (bf16[4,8,32,384]{3,2,1,0:T(8,128)(2,1)S(1)}, bf16[128,768]{1,0:T(8,128)(2,1)S(1)}) custom-call(s32[4]{0:T(128)S(1)} %pad_add_fusion.at_ref, bf16[2,32,768]{2,1,0:T(8,128)(2,1)S(1)} %pad_maximum_fusion.1.refs_0_, bf16[2,32,768]{2,1,0:T(8,128)(2,1)S(1)} %collective-permute-done.13.refs_1_, bf16[4,768,384]{2,1,0:T(8,128)(2,1)S(1)} %split.2.refs_1_.refs_2_, ...), custom_call_target="tpu_custom_call" | custom-call | flops 603979776 | bytes 6000000 | tf_op jit(solution)/shard_map/back/pallas_call | solution.py:166
  114.4 26.8 %all_to_all.17 = bf16[32,32,384]{2,1,0:T(8,128)(2,1)S(1)} all-to-all(bf16[32,32,384]{2,1,0:T(8,128)(2,1)S(1)} %bitcast.25), channel_id=1, replica_groups=mesh['y'=4,'z'=8,'x'=4,'core'=2] {'y','z'}, dimensions={0} | all-to-all | bytes 1572864 | tf_op jit(solution)/shard_map/all_to_all | solution.py:260
  141.3 4.2 %collective-permute-start.14 = (bf16[32,384]{1,0:T(8,128)(2,1)S(1)}, bf16[32,384]{1,0:T(8,128)(2,1)S(1)}, u32[]{:S(2)}, u32[]{:S(2)}) collective-permute-start(bf16[32,384]{1,0:T(8,128)(2,1)S(1)} %fusion), channel_id=1, source_target_pairs={{0,1},{1,0},{2,3},{3,2},{4,5},{5,4},{6,7},{7,6},{8,9},{9,8},{10,11... | collective-permute-start | bytes 73736 | tf_op jit(solution)/shard_map/ppermute | solution.py:241
  146.4 1.9 %collective-permute-start.15 = (bf16[32,768]{1,0:T(8,128)(2,1)S(1)}, bf16[32,768]{1,0:T(8,128)(2,1)S(1)}, u32[]{:S(2)}, u32[]{:S(2)}) collective-permute-start(bf16[32,768]{1,0:T(8,128)(2,1)S(1)} %maximum_select_fusion.2), channel_id=1, source_target_pairs={{0,0},{1,3},{2,64},{3,67},{4,128},{5,131},{6,192},{7,195},{8,8},{9... | collective-permute-start | bytes 147464 | tf_op jit(solution)/shard_map/ppermute | solution.py:268
  148.3 2.6 %collective-permute-start.16 = (bf16[32,768]{1,0:T(8,128)(2,1)S(1)}, bf16[32,768]{1,0:T(8,128)(2,1)S(1)}, u32[]{:S(2)}, u32[]{:S(2)}) collective-permute-start(bf16[32,768]{1,0:T(8,128)(2,1)S(1)} %maximum_select_fusion.2), channel_id=1, source_target_pairs={{0,4},{1,7},{2,68},{3,71},{4,132},{5,135},{6,196},{7,199},{8,12},{... | collective-permute-start | bytes 147464 | tf_op jit(solution)/shard_map/ppermute | solution.py:268
  152.5 2.7 %collective-permute-start.17 = (bf16[2,32,768]{2,1,0:T(8,128)(2,1)S(1)}, bf16[2,32,768]{2,1,0:T(8,128)(2,1)S(1)}, u32[]{:S(2)}, u32[]{:S(2)}) collective-permute-start(bf16[2,32,768]{2,1,0:T(8,128)(2,1)S(1)} %pad_maximum_fusion.2.first_ref), channel_id=1, source_target_pairs={{0,1},{1,0},{2,3},{3,2},{4,5},{5,4},{6,7},{7,6},{8,9},{9,8},{10,11... | collective-permute-start | bytes 294920 | tf_op jit(solution)/shard_map/ppermute | solution.py:241
  156.1 6.3 %outer.1 = bf16[768,3072]{1,0:T(8,128)(2,1)} custom-call(s32[4]{0:T(128)S(1)} %pad_add_fusion.at_ref, bf16[128,768]{1,0:T(8,128)(2,1)S(1)} %get-tuple-element.22.g4, bf16[128,768]{1,0:T(8,128)(2,1)S(1)} %get-tuple-element.25.g3, bf16[128,768]{1,0:T(8,128)(2,1)S(1)} %get-tuple-element.27.g2, bf16[2,32,768]{2,1,0:T(8,128)(2,1)S(1)} %pad_maximum_fusion.2.first_ref, ...), custom_call_target="tpu_custom_call" | custom-call | flops 2415919104 | bytes 8000000 | tf_op jit(solution)/shard_map/outer/pallas_call | solution.py:218
  (39 shorter events, 16.5 us)
Async XLA Ops:
  5.4 14.3 %collective-permute-start.5 = (bf16[4,768,384]{2,1,0:T(8,128)(2,1)}, bf16[4,768,384]{2,1,0:T(8,128)(2,1)}, u32[]{:S(2)}, u32[]{:S(2)}) collective-permute-start(bf16[4,768,384]{2,1,0:T(8,128)(2,1)} %split.3), channel_id=1, source_target_pairs={{0,1},{1,0},{2,3},{3,2},{4,5},{5,4},{6,7},{7,6},{8,9},{9,8},{10,11... | collective-permute-start | bytes 7077896 | tf_op jit(solution)/shard_map/ppermute | solution.py:241
  8.7 9.4 %collective-permute-start = (bf16[128,768]{1,0:T(8,128)(2,1)S(1)}, bf16[128,768]{1,0:T(8,128)(2,1)S(1)}, u32[]{:S(2)}, u32[]{:S(2)}) collective-permute-start(bf16[128,768]{1,0:T(8,128)(2,1)S(1)} %first.1), channel_id=1, source_target_pairs={{0,2},{8,10},{16,18},{24,26},{33,35},{41,43},{49,51},{57,59},{66,6... | collective-permute-start | bytes 589832 | tf_op jit(solution)/shard_map/ppermute | solution.py:245
  9.4 8.7 %collective-permute-start.1 = (bf16[128,768]{1,0:T(8,128)(2,1)S(1)}, bf16[128,768]{1,0:T(8,128)(2,1)S(1)}, u32[]{:S(2)}, u32[]{:S(2)}) collective-permute-start(bf16[128,768]{1,0:T(8,128)(2,1)S(1)} %first.1), channel_id=1, source_target_pairs={{0,4},{8,12},{16,20},{24,28},{33,37},{41,45},{49,53},{57,61},{66,7... | collective-permute-start | bytes 589832 | tf_op jit(solution)/shard_map/ppermute | solution.py:245
  10.1 8.1 %collective-permute-start.2 = (bf16[128,768]{1,0:T(8,128)(2,1)S(1)}, bf16[128,768]{1,0:T(8,128)(2,1)S(1)}, u32[]{:S(2)}, u32[]{:S(2)}) collective-permute-start(bf16[128,768]{1,0:T(8,128)(2,1)S(1)} %first.1), channel_id=1, source_target_pairs={{0,6},{8,14},{16,22},{24,30},{33,39},{41,47},{49,55},{57,63},{66,6... | collective-permute-start | bytes 589832 | tf_op jit(solution)/shard_map/ppermute | solution.py:245
  12.6 5.7 %collective-permute-start.4 = (bf16[3,32,384]{2,1,0:T(8,128)(2,1)S(1)}, bf16[3,32,384]{2,1,0:T(8,128)(2,1)S(1)}, u32[]{:S(2)}, u32[]{:S(2)}) collective-permute-start(bf16[3,32,384]{2,1,0:T(8,128)(2,1)S(1)} %get-tuple-element.19), channel_id=1, source_target_pairs={{0,1},{1,0},{2,3},{3,2},{4,5},{5,4},{6,7},{7,6},{8,9},{9,8},{10,11... | collective-permute-start | bytes 221192 | tf_op jit(solution)/shard_map/ppermute | solution.py:241
  18.2 1.5 collective-permute-start.3
  53.0 4.4 %collective-permute-start.6 = (bf16[32,384]{1,0:T(8,128)(2,1)S(1)}, bf16[32,384]{1,0:T(8,128)(2,1)S(1)}, u32[]{:S(2)}, u32[]{:S(2)}) collective-permute-start(bf16[32,384]{1,0:T(8,128)(2,1)S(1)} %fusion.2), channel_id=1, source_target_pairs={{0,1},{1,0},{2,3},{3,2},{4,5},{5,4},{6,7},{7,6},{8,9},{9,8},{10,11... | collective-permute-start | bytes 73736 | tf_op jit(solution)/shard_map/ppermute | solution.py:241
  57.4 6.0 %collective-permute-start.7 = (bf16[32,768]{1,0:T(8,128)(2,1)S(1)}, bf16[32,768]{1,0:T(8,128)(2,1)S(1)}, u32[]{:S(2)}, u32[]{:S(2)}) collective-permute-start(bf16[32,768]{1,0:T(8,128)(2,1)S(1)} %maximum_select_fusion), channel_id=1, source_target_pairs={{0,0},{1,3},{2,64},{3,67},{4,128},{5,131},{6,192},{7,195},{8,8},{9... | collective-permute-start | bytes 147464 | tf_op jit(solution)/shard_map/ppermute | solution.py:268
  59.5 4.6 %collective-permute-start.8 = (bf16[32,768]{1,0:T(8,128)(2,1)S(1)}, bf16[32,768]{1,0:T(8,128)(2,1)S(1)}, u32[]{:S(2)}, u32[]{:S(2)}) collective-permute-start(bf16[32,768]{1,0:T(8,128)(2,1)S(1)} %maximum_select_fusion), channel_id=1, source_target_pairs={{0,4},{1,7},{2,68},{3,71},{4,132},{5,135},{6,196},{7,199},{8,12},{... | collective-permute-start | bytes 147464 | tf_op jit(solution)/shard_map/ppermute | solution.py:268
  64.2 4.0 %collective-permute-start.9 = (bf16[2,32,768]{2,1,0:T(8,128)(2,1)S(1)}, bf16[2,32,768]{2,1,0:T(8,128)(2,1)S(1)}, u32[]{:S(2)}, u32[]{:S(2)}) collective-permute-start(bf16[2,32,768]{2,1,0:T(8,128)(2,1)S(1)} %pad_maximum_fusion.refs_0_), channel_id=1, source_target_pairs={{0,1},{1,0},{2,3},{3,2},{4,5},{5,4},{6,7},{7,6},{8,9},{9,8},{10,11... | collective-permute-start | bytes 294920 | tf_op jit(solution)/shard_map/ppermute | solution.py:241
  97.0 5.6 %collective-permute-start.10 = (bf16[32,384]{1,0:T(8,128)(2,1)S(1)}, bf16[32,384]{1,0:T(8,128)(2,1)S(1)}, u32[]{:S(2)}, u32[]{:S(2)}) collective-permute-start(bf16[32,384]{1,0:T(8,128)(2,1)S(1)} %fusion.1), channel_id=1, source_target_pairs={{0,1},{1,0},{2,3},{3,2},{4,5},{5,4},{6,7},{7,6},{8,9},{9,8},{10,11... | collective-permute-start | bytes 73736 | tf_op jit(solution)/shard_map/ppermute | solution.py:241
  102.7 6.0 %collective-permute-start.11 = (bf16[32,768]{1,0:T(8,128)(2,1)S(1)}, bf16[32,768]{1,0:T(8,128)(2,1)S(1)}, u32[]{:S(2)}, u32[]{:S(2)}) collective-permute-start(bf16[32,768]{1,0:T(8,128)(2,1)S(1)} %maximum_select_fusion.1), channel_id=1, source_target_pairs={{0,0},{1,3},{2,64},{3,67},{4,128},{5,131},{6,192},{7,195},{8,8},{9... | collective-permute-start | bytes 147464 | tf_op jit(solution)/shard_map/ppermute | solution.py:268
  104.6 4.1 %collective-permute-start.12 = (bf16[32,768]{1,0:T(8,128)(2,1)S(1)}, bf16[32,768]{1,0:T(8,128)(2,1)S(1)}, u32[]{:S(2)}, u32[]{:S(2)}) collective-permute-start(bf16[32,768]{1,0:T(8,128)(2,1)S(1)} %maximum_select_fusion.1), channel_id=1, source_target_pairs={{0,4},{1,7},{2,68},{3,71},{4,132},{5,135},{6,196},{7,199},{8,12},{... | collective-permute-start | bytes 147464 | tf_op jit(solution)/shard_map/ppermute | solution.py:268
  108.7 2.9 %collective-permute-start.13 = (bf16[2,32,768]{2,1,0:T(8,128)(2,1)S(1)}, bf16[2,32,768]{2,1,0:T(8,128)(2,1)S(1)}, u32[]{:S(2)}, u32[]{:S(2)}) collective-permute-start(bf16[2,32,768]{2,1,0:T(8,128)(2,1)S(1)} %pad_maximum_fusion.1.refs_0_), channel_id=1, source_target_pairs={{0,1},{1,0},{2,3},{3,2},{4,5},{5,4},{6,7},{7,6},{8,9},{9,8},{10,11... | collective-permute-start | bytes 294920 | tf_op jit(solution)/shard_map/ppermute | solution.py:241
  141.3 5.1 %collective-permute-start.14 = (bf16[32,384]{1,0:T(8,128)(2,1)S(1)}, bf16[32,384]{1,0:T(8,128)(2,1)S(1)}, u32[]{:S(2)}, u32[]{:S(2)}) collective-permute-start(bf16[32,384]{1,0:T(8,128)(2,1)S(1)} %fusion), channel_id=1, source_target_pairs={{0,1},{1,0},{2,3},{3,2},{4,5},{5,4},{6,7},{7,6},{8,9},{9,8},{10,11... | collective-permute-start | bytes 73736 | tf_op jit(solution)/shard_map/ppermute | solution.py:241
  146.4 6.0 %collective-permute-start.15 = (bf16[32,768]{1,0:T(8,128)(2,1)S(1)}, bf16[32,768]{1,0:T(8,128)(2,1)S(1)}, u32[]{:S(2)}, u32[]{:S(2)}) collective-permute-start(bf16[32,768]{1,0:T(8,128)(2,1)S(1)} %maximum_select_fusion.2), channel_id=1, source_target_pairs={{0,0},{1,3},{2,64},{3,67},{4,128},{5,131},{6,192},{7,195},{8,8},{9... | collective-permute-start | bytes 147464 | tf_op jit(solution)/shard_map/ppermute | solution.py:268
  148.3 4.1 %collective-permute-start.16 = (bf16[32,768]{1,0:T(8,128)(2,1)S(1)}, bf16[32,768]{1,0:T(8,128)(2,1)S(1)}, u32[]{:S(2)}, u32[]{:S(2)}) collective-permute-start(bf16[32,768]{1,0:T(8,128)(2,1)S(1)} %maximum_select_fusion.2), channel_id=1, source_target_pairs={{0,4},{1,7},{2,68},{3,71},{4,132},{5,135},{6,196},{7,199},{8,12},{... | collective-permute-start | bytes 147464 | tf_op jit(solution)/shard_map/ppermute | solution.py:268
  152.5 3.6 %collective-permute-start.17 = (bf16[2,32,768]{2,1,0:T(8,128)(2,1)S(1)}, bf16[2,32,768]{2,1,0:T(8,128)(2,1)S(1)}, u32[]{:S(2)}, u32[]{:S(2)}) collective-permute-start(bf16[2,32,768]{2,1,0:T(8,128)(2,1)S(1)} %pad_maximum_fusion.2.first_ref), channel_id=1, source_target_pairs={{0,1},{1,0},{2,3},{3,2},{4,5},{5,4},{6,7},{7,6},{8,9},{9,8},{10,11... | collective-permute-start | bytes 294920 | tf_op jit(solution)/shard_map/ppermute | solution.py:241

commit v5 on v4

--- a/solution.py
+++ b/solution.py
@@ -1,5 +1,3 @@
-import functools
-
 import jax
 import jax.numpy as jnp
 from jax import lax
@@ -15,7 +13,7 @@
 QUARTER = 768
 TRIALS = 128
 SLICE = 32
-SPLIT, ROWS, BACK, OUTER, KEEP = 48, 52, 8, 52, 48
+FIRST, BACK, OUTER, KEEP = 52, 8, 52, 48
 COLS = 3072
 VMEM = pl.BlockSpec(memory_space=pltpu.VMEM)
 SMEM = pl.BlockSpec(memory_space=pltpu.SMEM)
@@ -45,91 +43,87 @@
     return pl.CostEstimate(flops=flops, bytes_accessed=moved, transcendentals=0)
 
 
-def first_kernel(at_ref, rates_ref, out_ref, last_ref, zero_ref, sems):
+def first_kernel(at_ref, rates_ref, out_ref, mine_ref, theirs_ref, last_ref, zero_ref, held_ref, turned_ref, sems):
+    core = at_ref[1]
     rows = pl.ds(pl.multiple_of(at_ref[0] * QUARTER, 16), QUARTER)
     copies = [
         pltpu.make_async_copy(rates_ref.at[STEPS, rows], last_ref, sems.at[0]),
         pltpu.make_async_copy(rates_ref.at[0, rows], zero_ref, sems.at[1]),
+        pltpu.make_async_copy(rates_ref.at[1:STEPS, rows], held_ref, sems.at[2]),
     ]
     for copy in copies:
         copy.start()
-    for copy in copies:
-        copy.wait()
+    copies[0].wait()
+    copies[1].wait()
     last = last_ref[...].astype(jnp.float32)
     zero = zero_ref[...].astype(jnp.float32)
     out_ref[...] = ((last - zero) * (1.0 - last * last)).astype(jnp.bfloat16).T
+    copies[2].wait()
+    slot = pl.ds(pl.multiple_of(at_ref[2] * SLICE, SLICE), SLICE)
+    for t in range(STEPS - 1):
+        turned_ref[...] = held_ref[t].T
+        for ref, part in ((theirs_ref, 1 - core), (mine_ref, core)):
+            ref[t] = turned_ref[slot, pl.ds(pl.multiple_of(part * HALF, 128), HALF)]
 
 
 def first(at, rates):
+    small = jax.ShapeDtypeStruct((STEPS - 1, SLICE, HALF), jnp.bfloat16)
     return pl.pallas_call(
         first_kernel,
         in_specs=[SMEM, HBM],
-        out_specs=VMEM,
-        out_shape=jax.ShapeDtypeStruct((TRIALS, QUARTER), jnp.bfloat16),
+        out_specs=[VMEM] * 3,
+        out_shape=[jax.ShapeDtypeStruct((TRIALS, QUARTER), jnp.bfloat16), small, small],
         scratch_shapes=[
             pltpu.VMEM((QUARTER, TRIALS), jnp.bfloat16),
             pltpu.VMEM((QUARTER, TRIALS), jnp.bfloat16),
-            pltpu.SemaphoreType.DMA((2,)),
-        ],
-        compiler_params=params(52),
+            pltpu.VMEM((STEPS - 1, QUARTER, TRIALS), jnp.bfloat16),
+            pltpu.VMEM((TRIALS, QUARTER), jnp.bfloat16),
+            pltpu.SemaphoreType.DMA((3,)),
+        ],
+        compiler_params=params(FIRST),
         name="first",
     )(at, rates)
 
 
-def split_kernel(at_ref, w_ref, out_ref, sems, *, partner):
-    part = 1 - at_ref[1] if partner else at_ref[1]
-    copies = []
+def split_kernel(at_ref, w_ref, mine_ref, theirs_ref, held_ref, sems):
+    core = at_ref[1]
+
+    def columns(q, part):
+        return pl.ds(pl.multiple_of((2 * q + part) * HALF, 128), HALF)
+
+    took = [
+        pltpu.make_async_copy(w_ref.at[:, columns(q, 1 - core)], held_ref.at[q], sems.at[0, q])
+        for q in range(4)
+    ]
+    kept = [
+        pltpu.make_async_copy(w_ref.at[:, columns(q, core)], mine_ref.at[q], sems.at[1, q])
+        for q in range(4)
+    ]
+    gave = [pltpu.make_async_copy(held_ref.at[q], theirs_ref.at[q], sems.at[2, q]) for q in range(4)]
+    for copy in took + kept:
+        copy.start()
     for q in range(4):
-        columns = pl.ds(pl.multiple_of((2 * q + part) * HALF, 128), HALF)
-        copies.append(pltpu.make_async_copy(w_ref.at[:, columns], out_ref.at[q], sems.at[q]))
-    for copy in copies:
-        copy.start()
-    for copy in copies:
+        took[q].wait()
+        gave[q].start()
+    for copy in kept + gave:
         copy.wait()
 
 
-def split(at, weights, partner):
-    return pl.pallas_call(
-        functools.partial(split_kernel, partner=partner),
+def split(at, weights):
+    shape = jax.ShapeDtypeStruct((4, QUARTER, HALF), jnp.bfloat16)
+    return pl.pallas_call(
+        split_kernel,
         in_specs=[SMEM, HBM],
-        out_specs=VMEM,
-        out_shape=jax.ShapeDtypeStruct((4, QUARTER, HALF), jnp.bfloat16),
-        scratch_shapes=[pltpu.SemaphoreType.DMA((4,))],
-        cost_estimate=cost(0, 4_718_592),
-        compiler_params=params(SPLIT if partner else KEEP),
+        out_specs=[VMEM, HBM],
+        out_shape=[shape, shape],
+        scratch_shapes=[
+            pltpu.VMEM((4, QUARTER, HALF), jnp.bfloat16),
+            pltpu.SemaphoreType.DMA((3, 4)),
+        ],
+        cost_estimate=cost(0, 9_437_184),
+        compiler_params=params(KEEP),
         name="split",
     )(at, weights)
-
-
-def rows_kernel(at_ref, rates_ref, mine_ref, theirs_ref, held_ref, turned_ref, sem):
-    core = at_ref[1]
-    rows = pl.ds(pl.multiple_of(at_ref[0] * QUARTER, 16), QUARTER)
-    copy = pltpu.make_async_copy(rates_ref.at[1:STEPS, rows], held_ref, sem)
-    copy.start()
-    copy.wait()
-    slot = pl.ds(pl.multiple_of(at_ref[2] * SLICE, SLICE), SLICE)
-    for t in range(STEPS - 1):
-        for out_ref, part in ((theirs_ref, 1 - core), (mine_ref, core)):
-            turned_ref[...] = held_ref[t, pl.ds(pl.multiple_of(part * HALF, 16), HALF), :].T
-            out_ref[t] = turned_ref[slot, :]
-
-
-def rows(at, rates):
-    shape = jax.ShapeDtypeStruct((STEPS - 1, SLICE, HALF), jnp.bfloat16)
-    return pl.pallas_call(
-        rows_kernel,
-        in_specs=[SMEM, HBM],
-        out_specs=[VMEM, VMEM],
-        out_shape=[shape, shape],
-        scratch_shapes=[
-            pltpu.VMEM((STEPS - 1, QUARTER, TRIALS), jnp.bfloat16),
-            pltpu.VMEM((TRIALS, HALF), jnp.bfloat16),
-            pltpu.SemaphoreType.DMA,
-        ],
-        cost_estimate=cost(0, 600_000),
-        compiler_params=params(ROWS),
-        name="rows",
-    )(at, rates)
 
 
 def fill(at_ref, pair_refs, g_ref):
@@ -241,12 +235,10 @@
         return lax.ppermute(array, "core", SWAP)
 
     is_root_core = core == z // 4
-    root = first(at, rates)
+    root, before, other = first(at, rates)
     parts = [lax.ppermute(root, EVERY, from_root(shift)) for shift in (1, 2, 3)]
-    late_weights, late_rates, _ = lax.optimization_barrier((weights, rates, root))
-    theirs = swapped(split(at, late_weights, True))
-    mine = split(at, late_weights, False)
-    before, other = rows(at, late_rates)
+    mine, theirs = split(at, lax.optimization_barrier((weights, root))[0])
+    theirs = swapped(theirs)
     before = jnp.where(is_root_core, before, swapped(other))
     came = jnp.where(x == y, root, parts[0] + parts[1] + parts[2])
     grad, before = lax.optimization_barrier(

time: 164 us -> 168 us (1.024)
  the two profiles are of different devices: /device:TPU:1 before, /device:TPU:49 now
where the time goes in v5:
time: 168 us; the launch traced here: 167 us
  blocking collectives  86.9 us (52%)
  starting transfers between devices  39 us (23%)
  Pallas kernels  20.5 us (12%)
  waiting for transfers between devices  19.9 us (12%)
    all_to_all x3, blocking collectives, whole(): lax.all_to_all(sums.reshape(Y * Z, SLICE, HALF), ('y', 'z'), 0, 0, tiled=...  86.9 us
    ppermute x9, starting transfers between devices, swapped(): return lax.ppermute(array, 'core', SWAP)  24.5 us
    ppermute x6, waiting for transfers between devices, whole(): lax.ppermute(share, EVERY, across(j))  13.5 us
    ppermute x6, starting transfers between devices, whole(): lax.ppermute(share, EVERY, across(j))  12.5 us
    pallas_call x3, Pallas kernels, back(): pl.pallas_call(back_kernel, in_specs=[SMEM] + [VMEM] * len(pair) + [VMEM,...  8.29 us
    ppermute x9, waiting for transfers between devices, swapped(): return lax.ppermute(array, 'core', SWAP)  6.44 us
    pallas_call x1, Pallas kernels, outer(): pl.pallas_call(outer_kernel, in_specs=[SMEM] + [VMEM] * 5 + [HBM], out_sp...  6.34 us
    pallas_call x1, Pallas kernels, split(): pl.pallas_call(split_kernel, in_specs=[SMEM, HBM], out_specs=[VMEM, HBM],...  3.86 us
  transfers between devices with their start and end apart: 18, of which 13 were waited for; matrix products, arithmetic and copies ran while one was open for 0% of the time, Pallas kernels for 0%

profile of v5, /device:TPU:49, one launch (start us, length us, event | category | flops | bytes accessed | tf_op | source)
XLA Modules:
  0.0 167.3 jit_solution(15818849820069081037)
XLA Ops:
  0.1 2.0 %first.1 = (bf16[128,768]{1,0:T(8,128)(2,1)S(1)}, bf16[3,32,384]{2,1,0:T(8,128)(2,1)S(1)}, bf16[3,32,384]{2,1,0:T(8,128)(2,1)S(1)}) custom-call(s32[4]{0:T(128)S(1)} %pad_add_fusion.at_ref, bf16[5,3072,128]{2,1,0:T(8,128)(2,1)} %rates_ref.3), custom_call_target="tpu_custom_call" | custom-call | tf_op jit(solution)/shard_map/first/pallas_call | solution.py:71
  2.1 3.9 %split.1 = (bf16[4,768,384]{2,1,0:T(8,128)(2,1)S(1)}, bf16[4,768,384]{2,1,0:T(8,128)(2,1)}) custom-call(s32[4]{0:T(128)S(1)} %pad_add_fusion.at_ref, bf16[768,3072]{1,0:T(8,128)(2,1)} %w_ref), custom_call_target="tpu_custom_call" | custom-call | bytes 9437184 | tf_op jit(solution)/shard_map/split/pallas_call | solution.py:114
  9.6 7.7 %collective-permute-start.3 = (bf16[128,768]{1,0:T(8,128)(2,1)S(1)}, bf16[128,768]{1,0:T(8,128)(2,1)S(1)}, u32[]{:S(2)}, u32[]{:S(2)}) collective-permute-start(bf16[128,768]{1,0:T(8,128)(2,1)S(1)} %add_select_fusion), channel_id=1, source_target_pairs={{0,1},{1,0},{2,3},{3,2},{4,5},{5,4},{6,7},{7,6},{8,9},{9,8},{10,11... | collective-permute-start | bytes 589832 | tf_op jit(solution)/shard_map/ppermute | solution.py:235
  18.4 2.7 %back.3 = (bf16[4,8,32,384]{3,2,1,0:T(8,128)(2,1)S(1)}, bf16[128,768]{1,0:T(8,128)(2,1)S(1)}) custom-call(s32[4]{0:T(128)S(1)} %pad_add_fusion.at_ref, bf16[128,768]{1,0:T(8,128)(2,1)S(1)} %broadcast_select_fusion.refs_0_, bf16[4,768,384]{2,1,0:T(8,128)(2,1)S(1)} %get-tuple-element.24.refs_1_.refs_2_, bf16[4,768,384]{2,1,0:T(8,128)(2,1)} %collective-permute-done.5.refs_2_.refs_3_), custom_call_target="tpu_custom_call" | custom-call | flops 603979776 | bytes 6000000 | tf_op jit(solution)/shard_map/back/pallas_call | solution.py:160
  21.2 32.4 %all_to_all.15 = bf16[32,32,384]{2,1,0:T(8,128)(2,1)S(1)} all-to-all(bf16[32,32,384]{2,1,0:T(8,128)(2,1)S(1)} %bitcast.27), channel_id=1, replica_groups=mesh['y'=4,'z'=8,'x'=4,'core'=2] {'y','z'}, dimensions={0} | all-to-all | bytes 1572864 | tf_op jit(solution)/shard_map/all_to_all | solution.py:252
  55.9 1.5 collective-permute-start.8
  57.4 4.0 %collective-permute-start.7 = (bf16[32,768]{1,0:T(8,128)(2,1)S(1)}, bf16[32,768]{1,0:T(8,128)(2,1)S(1)}, u32[]{:S(2)}, u32[]{:S(2)}) collective-permute-start(bf16[32,768]{1,0:T(8,128)(2,1)S(1)} %maximum_select_fusion), channel_id=1, source_target_pairs={{0,0},{1,3},{2,64},{3,67},{4,128},{5,131},{6,192},{7,195},{8,8},{9... | collective-permute-start | bytes 147464 | tf_op jit(solution)/shard_map/ppermute | solution.py:260
  61.6 3.1 %collective-permute-done.7 = bf16[32,768]{1,0:T(8,128)(2,1)S(1)} collective-permute-done((bf16[32,768]{1,0:T(8,128)(2,1)S(1)}, bf16[32,768]{1,0:T(8,128)(2,1)S(1)}, u32[]{:S(2)}, u32[]{:S(2)}) %collective-permute-start.7) | collective-permute-done | bytes 49184 | tf_op jit(solution)/shard_map/ppermute | solution.py:260
  64.7 3.5 %collective-permute-start.9 = (bf16[2,32,768]{2,1,0:T(8,128)(2,1)S(1)}, bf16[2,32,768]{2,1,0:T(8,128)(2,1)S(1)}, u32[]{:S(2)}, u32[]{:S(2)}) collective-permute-start(bf16[2,32,768]{2,1,0:T(8,128)(2,1)S(1)} %pad_maximum_fusion.refs_0_), channel_id=1, source_target_pairs={{0,1},{1,0},{2,3},{3,2},{4,5},{5,4},{6,7},{7,6},{8,9},{9,8},{10,11... | collective-permute-start | bytes 294920 | tf_op jit(solution)/shard_map/ppermute | solution.py:235
  69.1 2.8 %back.4 = (bf16[4,8,32,384]{3,2,1,0:T(8,128)(2,1)S(1)}, bf16[128,768]{1,0:T(8,128)(2,1)S(1)}) custom-call(s32[4]{0:T(128)S(1)} %pad_add_fusion.at_ref, bf16[2,32,768]{2,1,0:T(8,128)(2,1)S(1)} %pad_maximum_fusion.refs_0_, bf16[2,32,768]{2,1,0:T(8,128)(2,1)S(1)} %collective-permute-done.9.refs_1_, bf16[4,768,384]{2,1,0:T(8,128)(2,1)S(1)} %get-tuple-element.24.refs_1_.refs_2_, ...), custom_call_target="tpu_custom_call" | custom-call | flops 603979776 | bytes 6000000 | tf_op jit(solution)/shard_map/back/pallas_call | solution.py:160
  71.9 27.2 %all_to_all.16 = bf16[32,32,384]{2,1,0:T(8,128)(2,1)S(1)} all-to-all(bf16[32,32,384]{2,1,0:T(8,128)(2,1)S(1)} %bitcast.26), channel_id=1, replica_groups=mesh['y'=4,'z'=8,'x'=4,'core'=2] {'y','z'}, dimensions={0} | all-to-all | bytes 1572864 | tf_op jit(solution)/shard_map/all_to_all | solution.py:252
  99.2 1.6 collective-permute-start.10
  102.9 2.8 %collective-permute-start.11 = (bf16[32,768]{1,0:T(8,128)(2,1)S(1)}, bf16[32,768]{1,0:T(8,128)(2,1)S(1)}, u32[]{:S(2)}, u32[]{:S(2)}) collective-permute-start(bf16[32,768]{1,0:T(8,128)(2,1)S(1)} %maximum_select_fusion.1), channel_id=1, source_target_pairs={{0,0},{1,3},{2,64},{3,67},{4,128},{5,131},{6,192},{7,195},{8,8},{9... | collective-permute-start | bytes 147464 | tf_op jit(solution)/shard_map/ppermute | solution.py:260
  105.7 1.4 collective-permute-done.12
  107.2 3.2 %collective-permute-done.11 = bf16[32,768]{1,0:T(8,128)(2,1)S(1)} collective-permute-done((bf16[32,768]{1,0:T(8,128)(2,1)S(1)}, bf16[32,768]{1,0:T(8,128)(2,1)S(1)}, u32[]{:S(2)}, u32[]{:S(2)}) %collective-permute-start.11) | collective-permute-done | bytes 49184 | tf_op jit(solution)/shard_map/ppermute | solution.py:260
  110.4 3.6 %collective-permute-start.13 = (bf16[2,32,768]{2,1,0:T(8,128)(2,1)S(1)}, bf16[2,32,768]{2,1,0:T(8,128)(2,1)S(1)}, u32[]{:S(2)}, u32[]{:S(2)}) collective-permute-start(bf16[2,32,768]{2,1,0:T(8,128)(2,1)S(1)} %pad_maximum_fusion.1.refs_0_), channel_id=1, source_target_pairs={{0,1},{1,0},{2,3},{3,2},{4,5},{5,4},{6,7},{7,6},{8,9},{9,8},{10,11... | collective-permute-start | bytes 294920 | tf_op jit(solution)/shard_map/ppermute | solution.py:235
  114.9 2.8 %back.5 = (bf16[4,8,32,384]{3,2,1,0:T(8,128)(2,1)S(1)}, bf16[128,768]{1,0:T(8,128)(2,1)S(1)}) custom-call(s32[4]{0:T(128)S(1)} %pad_add_fusion.at_ref, bf16[2,32,768]{2,1,0:T(8,128)(2,1)S(1)} %pad_maximum_fusion.1.refs_0_, bf16[2,32,768]{2,1,0:T(8,128)(2,1)S(1)} %collective-permute-done.13.refs_1_, ...), custom_call_target="tpu_custom_call" | custom-call | flops 603979776 | bytes 6000000 | tf_op jit(solution)/shard_map/back/pallas_call | solution.py:160
  117.7 27.2 %all_to_all.17 = bf16[32,32,384]{2,1,0:T(8,128)(2,1)S(1)} all-to-all(bf16[32,32,384]{2,1,0:T(8,128)(2,1)S(1)} %bitcast.25), channel_id=1, replica_groups=mesh['y'=4,'z'=8,'x'=4,'core'=2] {'y','z'}, dimensions={0} | all-to-all | bytes 1572864 | tf_op jit(solution)/shard_map/all_to_all | solution.py:252
  145.1 1.6 collective-permute-start.14
  148.5 2.1 %collective-permute-start.15 = (bf16[32,768]{1,0:T(8,128)(2,1)S(1)}, bf16[32,768]{1,0:T(8,128)(2,1)S(1)}, u32[]{:S(2)}, u32[]{:S(2)}) collective-permute-start(bf16[32,768]{1,0:T(8,128)(2,1)S(1)} %maximum_select_fusion.2), channel_id=1, source_target_pairs={{0,0},{1,3},{2,64},{3,67},{4,128},{5,131},{6,192},{7,195},{8,8},{9... | collective-permute-start | bytes 147464 | tf_op jit(solution)/shard_map/ppermute | solution.py:260
  150.6 2.4 %collective-permute-done.16 = bf16[32,768]{1,0:T(8,128)(2,1)S(1)} collective-permute-done((bf16[32,768]{1,0:T(8,128)(2,1)S(1)}, bf16[32,768]{1,0:T(8,128)(2,1)S(1)}, u32[]{:S(2)}, u32[]{:S(2)}) %collective-permute-start.16) | collective-permute-done | bytes 49184 | tf_op jit(solution)/shard_map/ppermute | solution.py:260
  153.0 3.1 %collective-permute-done.15 = bf16[32,768]{1,0:T(8,128)(2,1)S(1)} collective-permute-done((bf16[32,768]{1,0:T(8,128)(2,1)S(1)}, bf16[32,768]{1,0:T(8,128)(2,1)S(1)}, u32[]{:S(2)}, u32[]{:S(2)}) %collective-permute-start.15) | collective-permute-done | bytes 49184 | tf_op jit(solution)/shard_map/ppermute | solution.py:260
  156.1 3.7 %collective-permute-start.17 = (bf16[2,32,768]{2,1,0:T(8,128)(2,1)S(1)}, bf16[2,32,768]{2,1,0:T(8,128)(2,1)S(1)}, u32[]{:S(2)}, u32[]{:S(2)}) collective-permute-start(bf16[2,32,768]{2,1,0:T(8,128)(2,1)S(1)} %pad_maximum_fusion.2.first_ref), channel_id=1, source_target_pairs={{0,1},{1,0},{2,3},{3,2},{4,5},{5,4},{6,7},{7,6},{8,9},{9,8},{10,11... | collective-permute-start | bytes 294920 | tf_op jit(solution)/shard_map/ppermute | solution.py:235
  160.8 6.3 %outer.1 = bf16[768,3072]{1,0:T(8,128)(2,1)} custom-call(s32[4]{0:T(128)S(1)} %pad_add_fusion.at_ref, bf16[128,768]{1,0:T(8,128)(2,1)S(1)} %get-tuple-element.26.g4, bf16[128,768]{1,0:T(8,128)(2,1)S(1)} %get-tuple-element.29.g3, bf16[128,768]{1,0:T(8,128)(2,1)S(1)} %get-tuple-element.31.g2, bf16[2,32,768]{2,1,0:T(8,128)(2,1)S(1)} %pad_maximum_fusion.2.first_ref, ...), custom_call_target="tpu_custom_call" | custom-call | flops 2415919104 | bytes 8000000 | tf_op jit(solution)/shard_map/outer/pallas_call | solution.py:212
  (37 shorter events, 14.2 us)
Async XLA Ops:
  6.0 12.4 %collective-permute-start.5 = (bf16[4,768,384]{2,1,0:T(8,128)(2,1)}, bf16[4,768,384]{2,1,0:T(8,128)(2,1)}, u32[]{:S(2)}, u32[]{:S(2)}) collective-permute-start(bf16[4,768,384]{2,1,0:T(8,128)(2,1)} %get-tuple-element.25), channel_id=1, source_target_pairs={{0,1},{1,0},{2,3},{3,2},{4,5},{5,4},{6,7},{7,6},{8,9},{9,8},{10,11... | collective-permute-start | bytes 7077896 | tf_op jit(solution)/shard_map/ppermute | solution.py:235
  6.8 2.8 %collective-permute-start.2 = (bf16[128,768]{1,0:T(8,128)(2,1)S(1)}, bf16[128,768]{1,0:T(8,128)(2,1)S(1)}, u32[]{:S(2)}, u32[]{:S(2)}) collective-permute-start(bf16[128,768]{1,0:T(8,128)(2,1)S(1)} %get-tuple-element.19), channel_id=1, source_target_pairs={{0,6},{8,14},{16,22},{24,30},{33,39},{41,47},{49,55},{57,63},{66,6... | collective-permute-start | bytes 589832 | tf_op jit(solution)/shard_map/ppermute | solution.py:239
  7.4 2.1 %collective-permute-start.1 = (bf16[128,768]{1,0:T(8,128)(2,1)S(1)}, bf16[128,768]{1,0:T(8,128)(2,1)S(1)}, u32[]{:S(2)}, u32[]{:S(2)}) collective-permute-start(bf16[128,768]{1,0:T(8,128)(2,1)S(1)} %get-tuple-element.19), channel_id=1, source_target_pairs={{0,4},{8,12},{16,20},{24,28},{33,37},{41,45},{49,53},{57,61},{66,7... | collective-permute-start | bytes 589832 | tf_op jit(solution)/shard_map/ppermute | solution.py:239
  8.1 1.4 collective-permute-start
  8.8 8.5 %collective-permute-start.4 = (bf16[3,32,384]{2,1,0:T(8,128)(2,1)S(1)}, bf16[3,32,384]{2,1,0:T(8,128)(2,1)S(1)}, u32[]{:S(2)}, u32[]{:S(2)}) collective-permute-start(bf16[3,32,384]{2,1,0:T(8,128)(2,1)S(1)} %get-tuple-element.21), channel_id=1, source_target_pairs={{0,1},{1,0},{2,3},{3,2},{4,5},{5,4},{6,7},{7,6},{8,9},{9,8},{10,11... | collective-permute-start | bytes 221192 | tf_op jit(solution)/shard_map/ppermute | solution.py:235
  9.6 8.8 %collective-permute-start.3 = (bf16[128,768]{1,0:T(8,128)(2,1)S(1)}, bf16[128,768]{1,0:T(8,128)(2,1)S(1)}, u32[]{:S(2)}, u32[]{:S(2)}) collective-permute-start(bf16[128,768]{1,0:T(8,128)(2,1)S(1)} %add_select_fusion), channel_id=1, source_target_pairs={{0,1},{1,0},{2,3},{3,2},{4,5},{5,4},{6,7},{7,6},{8,9},{9,8},{10,11... | collective-permute-start | bytes 589832 | tf_op jit(solution)/shard_map/ppermute | solution.py:235
  53.8 2.1 %collective-permute-start.6 = (bf16[32,384]{1,0:T(8,128)(2,1)S(1)}, bf16[32,384]{1,0:T(8,128)(2,1)S(1)}, u32[]{:S(2)}, u32[]{:S(2)}) collective-permute-start(bf16[32,384]{1,0:T(8,128)(2,1)S(1)} %fusion.2), channel_id=1, source_target_pairs={{0,1},{1,0},{2,3},{3,2},{4,5},{5,4},{6,7},{7,6},{8,9},{9,8},{10,11... | collective-permute-start | bytes 73736 | tf_op jit(solution)/shard_map/ppermute | solution.py:235
  55.9 5.7 %collective-permute-start.8 = (bf16[32,768]{1,0:T(8,128)(2,1)S(1)}, bf16[32,768]{1,0:T(8,128)(2,1)S(1)}, u32[]{:S(2)}, u32[]{:S(2)}) collective-permute-start(bf16[32,768]{1,0:T(8,128)(2,1)S(1)} %maximum_select_fusion), channel_id=1, source_target_pairs={{0,4},{1,7},{2,68},{3,71},{4,132},{5,135},{6,196},{7,199},{8,12},{... | collective-permute-start | bytes 147464 | tf_op jit(solution)/shard_map/ppermute | solution.py:260
  57.4 7.3 %collective-permute-start.7 = (bf16[32,768]{1,0:T(8,128)(2,1)S(1)}, bf16[32,768]{1,0:T(8,128)(2,1)S(1)}, u32[]{:S(2)}, u32[]{:S(2)}) collective-permute-start(bf16[32,768]{1,0:T(8,128)(2,1)S(1)} %maximum_select_fusion), channel_id=1, source_target_pairs={{0,0},{1,3},{2,64},{3,67},{4,128},{5,131},{6,192},{7,195},{8,8},{9... | collective-permute-start | bytes 147464 | tf_op jit(solution)/shard_map/ppermute | solution.py:260
  64.7 4.4 %collective-permute-start.9 = (bf16[2,32,768]{2,1,0:T(8,128)(2,1)S(1)}, bf16[2,32,768]{2,1,0:T(8,128)(2,1)S(1)}, u32[]{:S(2)}, u32[]{:S(2)}) collective-permute-start(bf16[2,32,768]{2,1,0:T(8,128)(2,1)S(1)} %pad_maximum_fusion.refs_0_), channel_id=1, source_target_pairs={{0,1},{1,0},{2,3},{3,2},{4,5},{5,4},{6,7},{7,6},{8,9},{9,8},{10,11... | collective-permute-start | bytes 294920 | tf_op jit(solution)/shard_map/ppermute | solution.py:235
  99.2 2.5 %collective-permute-start.10 = (bf16[32,384]{1,0:T(8,128)(2,1)S(1)}, bf16[32,384]{1,0:T(8,128)(2,1)S(1)}, u32[]{:S(2)}, u32[]{:S(2)}) collective-permute-start(bf16[32,384]{1,0:T(8,128)(2,1)S(1)} %fusion.1), channel_id=1, source_target_pairs={{0,1},{1,0},{2,3},{3,2},{4,5},{5,4},{6,7},{7,6},{8,9},{9,8},{10,11... | collective-permute-start | bytes 73736 | tf_op jit(solution)/shard_map/ppermute | solution.py:235
  101.7 5.4 %collective-permute-start.12 = (bf16[32,768]{1,0:T(8,128)(2,1)S(1)}, bf16[32,768]{1,0:T(8,128)(2,1)S(1)}, u32[]{:S(2)}, u32[]{:S(2)}) collective-permute-start(bf16[32,768]{1,0:T(8,128)(2,1)S(1)} %maximum_select_fusion.1), channel_id=1, source_target_pairs={{0,4},{1,7},{2,68},{3,71},{4,132},{5,135},{6,196},{7,199},{8,12},{... | collective-permute-start | bytes 147464 | tf_op jit(solution)/shard_map/ppermute | solution.py:260
  102.9 7.5 %collective-permute-start.11 = (bf16[32,768]{1,0:T(8,128)(2,1)S(1)}, bf16[32,768]{1,0:T(8,128)(2,1)S(1)}, u32[]{:S(2)}, u32[]{:S(2)}) collective-permute-start(bf16[32,768]{1,0:T(8,128)(2,1)S(1)} %maximum_select_fusion.1), channel_id=1, source_target_pairs={{0,0},{1,3},{2,64},{3,67},{4,128},{5,131},{6,192},{7,195},{8,8},{9... | collective-permute-start | bytes 147464 | tf_op jit(solution)/shard_map/ppermute | solution.py:260
  110.4 4.5 %collective-permute-start.13 = (bf16[2,32,768]{2,1,0:T(8,128)(2,1)S(1)}, bf16[2,32,768]{2,1,0:T(8,128)(2,1)S(1)}, u32[]{:S(2)}, u32[]{:S(2)}) collective-permute-start(bf16[2,32,768]{2,1,0:T(8,128)(2,1)S(1)} %pad_maximum_fusion.1.refs_0_), channel_id=1, source_target_pairs={{0,1},{1,0},{2,3},{3,2},{4,5},{5,4},{6,7},{7,6},{8,9},{9,8},{10,11... | collective-permute-start | bytes 294920 | tf_op jit(solution)/shard_map/ppermute | solution.py:235
  145.1 2.5 %collective-permute-start.14 = (bf16[32,384]{1,0:T(8,128)(2,1)S(1)}, bf16[32,384]{1,0:T(8,128)(2,1)S(1)}, u32[]{:S(2)}, u32[]{:S(2)}) collective-permute-start(bf16[32,384]{1,0:T(8,128)(2,1)S(1)} %fusion), channel_id=1, source_target_pairs={{0,1},{1,0},{2,3},{3,2},{4,5},{5,4},{6,7},{7,6},{8,9},{9,8},{10,11... | collective-permute-start | bytes 73736 | tf_op jit(solution)/shard_map/ppermute | solution.py:235
  147.6 5.4 %collective-permute-start.16 = (bf16[32,768]{1,0:T(8,128)(2,1)S(1)}, bf16[32,768]{1,0:T(8,128)(2,1)S(1)}, u32[]{:S(2)}, u32[]{:S(2)}) collective-permute-start(bf16[32,768]{1,0:T(8,128)(2,1)S(1)} %maximum_select_fusion.2), channel_id=1, source_target_pairs={{0,4},{1,7},{2,68},{3,71},{4,132},{5,135},{6,196},{7,199},{8,12},{... | collective-permute-start | bytes 147464 | tf_op jit(solution)/shard_map/ppermute | solution.py:260
  148.5 7.6 %collective-permute-start.15 = (bf16[32,768]{1,0:T(8,128)(2,1)S(1)}, bf16[32,768]{1,0:T(8,128)(2,1)S(1)}, u32[]{:S(2)}, u32[]{:S(2)}) collective-permute-start(bf16[32,768]{1,0:T(8,128)(2,1)S(1)} %maximum_select_fusion.2), channel_id=1, source_target_pairs={{0,0},{1,3},{2,64},{3,67},{4,128},{5,131},{6,192},{7,195},{8,8},{9... | collective-permute-start | bytes 147464 | tf_op jit(solution)/shard_map/ppermute | solution.py:260
  156.1 4.7 %collective-permute-start.17 = (bf16[2,32,768]{2,1,0:T(8,128)(2,1)S(1)}, bf16[2,32,768]{2,1,0:T(8,128)(2,1)S(1)}, u32[]{:S(2)}, u32[]{:S(2)}) collective-permute-start(bf16[2,32,768]{2,1,0:T(8,128)(2,1)S(1)} %pad_maximum_fusion.2.first_ref), channel_id=1, source_target_pairs={{0,1},{1,0},{2,3},{3,2},{4,5},{5,4},{6,7},{7,6},{8,9},{9,8},{10,11... | collective-permute-start | bytes 294920 | tf_op jit(solution)/shard_map/ppermute | solution.py:235

commit v6 on v5

--- a/solution.py
+++ b/solution.py
@@ -13,7 +13,7 @@
 QUARTER = 768
 TRIALS = 128
 SLICE = 32
-FIRST, BACK, OUTER, KEEP = 52, 8, 52, 48
+FIRST, BACK, OUTER, KEEP = 52, 8, 24, 48
 COLS = 3072
 VMEM = pl.BlockSpec(memory_space=pltpu.VMEM)
 SMEM = pl.BlockSpec(memory_space=pltpu.SMEM)
@@ -85,44 +85,62 @@
     )(at, rates)
 
 
-def split_kernel(at_ref, w_ref, mine_ref, theirs_ref, held_ref, sems):
-    core = at_ref[1]
-
-    def columns(q, part):
-        return pl.ds(pl.multiple_of((2 * q + part) * HALF, 128), HALF)
-
+def columns(q, part):
+    return pl.ds(pl.multiple_of((2 * q + part) * HALF, 128), HALF)
+
+
+def give_kernel(at_ref, w_ref, theirs_ref, held_ref, sems):
     took = [
-        pltpu.make_async_copy(w_ref.at[:, columns(q, 1 - core)], held_ref.at[q], sems.at[0, q])
+        pltpu.make_async_copy(w_ref.at[:, columns(q, 1 - at_ref[1])], held_ref.at[q], sems.at[0, q])
         for q in range(4)
     ]
-    kept = [
-        pltpu.make_async_copy(w_ref.at[:, columns(q, core)], mine_ref.at[q], sems.at[1, q])
-        for q in range(4)
-    ]
-    gave = [pltpu.make_async_copy(held_ref.at[q], theirs_ref.at[q], sems.at[2, q]) for q in range(4)]
-    for copy in took + kept:
+    gave = [pltpu.make_async_copy(held_ref.at[q], theirs_ref.at[q], sems.at[1, q]) for q in range(4)]
+    for copy in took:
         copy.start()
     for q in range(4):
         took[q].wait()
         gave[q].start()
-    for copy in kept + gave:
+    for copy in gave:
         copy.wait()
 
 
-def split(at, weights):
-    shape = jax.ShapeDtypeStruct((4, QUARTER, HALF), jnp.bfloat16)
-    return pl.pallas_call(
-        split_kernel,
+def give(at, weights):
+    return pl.pallas_call(
+        give_kernel,
         in_specs=[SMEM, HBM],
-        out_specs=[VMEM, HBM],
-        out_shape=[shape, shape],
+        out_specs=HBM,
+        out_shape=jax.ShapeDtypeStruct((4, QUARTER, HALF), jnp.bfloat16),
         scratch_shapes=[
             pltpu.VMEM((4, QUARTER, HALF), jnp.bfloat16),
-            pltpu.SemaphoreType.DMA((3, 4)),
-        ],
-        cost_estimate=cost(0, 9_437_184),
+            pltpu.SemaphoreType.DMA((2, 4)),
+        ],
+        cost_estimate=cost(0, 4_718_592),
+        compiler_params=params(52),
+        name="give",
+    )(at, weights)
+
+
+def keep_kernel(at_ref, w_ref, mine_ref, sems):
+    copies = [
+        pltpu.make_async_copy(w_ref.at[:, columns(q, at_ref[1])], mine_ref.at[q], sems.at[q])
+        for q in range(4)
+    ]
+    for copy in copies:
+        copy.start()
+    for copy in copies:
+        copy.wait()
+
+
+def keep(at, weights):
+    return pl.pallas_call(
+        keep_kernel,
+        in_specs=[SMEM, HBM],
+        out_specs=VMEM,
+        out_shape=jax.ShapeDtypeStruct((4, QUARTER, HALF), jnp.bfloat16),
+        scratch_shapes=[pltpu.SemaphoreType.DMA((4,))],
+        cost_estimate=cost(0, 4_718_592),
         compiler_params=params(KEEP),
-        name="split",
+        name="keep",
     )(at, weights)
 
 
@@ -180,46 +198,38 @@
 
 
 def outer_kernel(
-    at_ref, g4, g3, g2, first_ref, second_ref, rates_ref, out_ref, g_ref, turned_ref, held_ref, done_ref, sems
+    at_ref, g4, g3, g2, first_ref, second_ref, rates_ref, out_ref, g_ref, turned_ref, done_ref, sems
 ):
-    def came(j):
-        columns = pl.ds(j * TILE, TILE)
-        return pltpu.make_async_copy(rates_ref.at[0:STEPS, columns], held_ref.at[:, columns], sems.at[0, j])
-
-    def went(j):
-        columns = pl.ds(j * TILE, TILE)
-        return pltpu.make_async_copy(done_ref.at[j], out_ref.at[:, columns], sems.at[1, j])
-
-    for j in range(TILES):
-        came(j).start()
+    went = [
+        pltpu.make_async_copy(done_ref.at[j], out_ref.at[:, pl.ds(j * TILE, TILE)], sems.at[j])
+        for j in range(TILES)
+    ]
     for t, ref in ((3, g4), (2, g3), (1, g2)):
         turned_ref[:, t * TRIALS : (t + 1) * TRIALS] = ref[...].T
     fill(at_ref, (first_ref, second_ref), g_ref)
     turned_ref[:, :TRIALS] = g_ref[...].T
     for j in range(TILES):
-        came(j).wait()
-        columns = slice(j * TILE, (j + 1) * TILE)
-        before = jnp.concatenate([held_ref[t, columns, :] for t in range(STEPS)], axis=1)
+        part = slice(j * TILE, (j + 1) * TILE)
+        before = jnp.concatenate([rates_ref[t, part, :] for t in range(STEPS)], axis=1)
         done_ref[j] = lax.dot_general(
             turned_ref[...], before, (((1,), (1,)), ((), ())), preferred_element_type=jnp.float32
         ).astype(jnp.bfloat16)
-        went(j).start()
-    for j in range(TILES):
-        went(j).wait()
+        went[j].start()
+    for copy in went:
+        copy.wait()
 
 
 def outer(at, full, pair, rates):
     return pl.pallas_call(
         outer_kernel,
-        in_specs=[SMEM] + [VMEM] * 5 + [HBM],
+        in_specs=[SMEM] + [VMEM] * 6,
         out_specs=HBM,
         out_shape=jax.ShapeDtypeStruct((QUARTER, COLS), jnp.bfloat16),
         scratch_shapes=[
             pltpu.VMEM((TRIALS, QUARTER), jnp.bfloat16),
             pltpu.VMEM((QUARTER, STEPS * TRIALS), jnp.bfloat16),
-            pltpu.VMEM((STEPS, COLS, TRIALS), jnp.bfloat16),
             pltpu.VMEM((TILES, QUARTER, TILE), jnp.bfloat16),
-            pltpu.SemaphoreType.DMA((2, TILES)),
+            pltpu.SemaphoreType.DMA((TILES,)),
         ],
         cost_estimate=cost(2 * STEPS * TRIALS * QUARTER * COLS, 8_000_000),
         compiler_params=params(OUTER),
@@ -236,9 +246,9 @@
 
     is_root_core = core == z // 4
     root, before, other = first(at, rates)
+    theirs = swapped(give(at, lax.optimization_barrier((weights, root))[0]))
     parts = [lax.ppermute(root, EVERY, from_root(shift)) for shift in (1, 2, 3)]
-    mine, theirs = split(at, lax.optimization_barrier((weights, root))[0])
-    theirs = swapped(theirs)
+    mine = keep(at, lax.optimization_barrier((weights, root))[0])
     before = jnp.where(is_root_core, before, swapped(other))
     came = jnp.where(x == y, root, parts[0] + parts[1] + parts[2])
     grad, before = lax.optimization_barrier(

time: 168 us -> 161 us (0.958)
  the two profiles are of different devices: /device:TPU:49 before, /device:TPU:1 now
where the time goes in v6:
time: 161 us; the launch traced here: 160 us
  blocking collectives  84.6 us (53%)
  starting transfers between devices  42.6 us (26%)
  Pallas kernels  20.1 us (12%)
  waiting for transfers between devices  12 us (7%)
    all_to_all x3, blocking collectives, whole(): lax.all_to_all(sums.reshape(Y * Z, SLICE, HALF), ('y', 'z'), 0, 0, tiled=...  84.6 us
    ppermute x9, starting transfers between devices, swapped(): return lax.ppermute(array, 'core', SWAP)  27.8 us
    ppermute x6, starting transfers between devices, whole(): lax.ppermute(share, EVERY, across(j))  12.7 us
    pallas_call x3, Pallas kernels, back(): pl.pallas_call(back_kernel, in_specs=[SMEM] + [VMEM] * len(pair) + [VMEM,...  8.59 us
    ppermute x9, waiting for transfers between devices, swapped(): return lax.ppermute(array, 'core', SWAP)  6.44 us
    ppermute x6, waiting for transfers between devices, whole(): lax.ppermute(share, EVERY, across(j))  5.6 us
    pallas_call x1, Pallas kernels, outer(): pl.pallas_call(outer_kernel, in_specs=[SMEM] + [VMEM] * 6, out_specs=HBM,...  4.19 us
  transfers between devices with their start and end apart: 18, of which 11 were waited for; matrix products, arithmetic and copies ran while one was open for 0% of the time, Pallas kernels for 1%

profile of v6, /device:TPU:1, one launch (start us, length us, event | category | flops | bytes accessed | tf_op | source)
XLA Modules:
  0.0 160.3 jit_solution(2954815120344063162)
XLA Ops:
  0.1 2.0 %first.1 = (bf16[128,768]{1,0:T(8,128)(2,1)S(1)}, bf16[3,32,384]{2,1,0:T(8,128)(2,1)S(1)}, bf16[3,32,384]{2,1,0:T(8,128)(2,1)S(1)}) custom-call(s32[4]{0:T(128)S(1)} %pad_add_fusion.at_ref, bf16[5,3072,128]{2,1,0:T(8,128)(2,1)} %rates_ref.3), custom_call_target="tpu_custom_call" | custom-call | tf_op jit(solution)/shard_map/first/pallas_call | solution.py:71
  2.1 3.1 %give.1 = bf16[4,768,384]{2,1,0:T(8,128)(2,1)} custom-call(s32[4]{0:T(128)S(1)} %pad_add_fusion.at_ref, bf16[768,3072]{1,0:T(8,128)(2,1)} %w_ref.1), custom_call_target="tpu_custom_call" | custom-call | bytes 4718592 | tf_op jit(solution)/shard_map/give/pallas_call | solution.py:108
  5.2 3.3 %collective-permute-start.5 = (bf16[4,768,384]{2,1,0:T(8,128)(2,1)}, bf16[4,768,384]{2,1,0:T(8,128)(2,1)}, u32[]{:S(2)}, u32[]{:S(2)}) collective-permute-start(bf16[4,768,384]{2,1,0:T(8,128)(2,1)} %give.1), channel_id=1, source_target_pairs={{0,1},{1,0},{2,3},{3,2},{4,5},{5,4},{6,7},{7,6},{8,9},{9,8},{10,11... | collective-permute-start | bytes 7077896 | tf_op jit(solution)/shard_map/ppermute | solution.py:245
  10.5 3.3 %collective-permute-start.4 = (bf16[3,32,384]{2,1,0:T(8,128)(2,1)S(1)}, bf16[3,32,384]{2,1,0:T(8,128)(2,1)S(1)}, u32[]{:S(2)}, u32[]{:S(2)}) collective-permute-start(bf16[3,32,384]{2,1,0:T(8,128)(2,1)S(1)} %get-tuple-element.19), channel_id=1, source_target_pairs={{0,1},{1,0},{2,3},{3,2},{4,5},{5,4},{6,7},{7,6},{8,9},{9,8},{10,11... | collective-permute-start | bytes 221192 | tf_op jit(solution)/shard_map/ppermute | solution.py:245
  13.8 2.2 %keep.1.refs_1_.refs_2_ = bf16[4,768,384]{2,1,0:T(8,128)(2,1)S(1)} custom-call(s32[4]{0:T(128)S(1)} %pad_add_fusion.at_ref, bf16[768,3072]{1,0:T(8,128)(2,1)} %w_ref.1), custom_call_target="tpu_custom_call" | custom-call | bytes 4718592 | tf_op jit(solution)/shard_map/keep/pallas_call | solution.py:135
  18.1 2.8 %back.3 = (bf16[4,8,32,384]{3,2,1,0:T(8,128)(2,1)S(1)}, bf16[128,768]{1,0:T(8,128)(2,1)S(1)}) custom-call(s32[4]{0:T(128)S(1)} %pad_add_fusion.at_ref, bf16[128,768]{1,0:T(8,128)(2,1)S(1)} %broadcast_select_fusion.refs_0_, bf16[4,768,384]{2,1,0:T(8,128)(2,1)S(1)} %keep.1.refs_1_.refs_2_, bf16[4,768,384]{2,1,0:T(8,128)(2,1)} %collective-permute-done.5.refs_2_.refs_3_), custom_call_target="tpu_custom_call" | custom-call | flops 603979776 | bytes 6000000 | tf_op jit(solution)/shard_map/back/pallas_call | solution.py:178
  20.9 31.8 %all_to_all.15 = bf16[32,32,384]{2,1,0:T(8,128)(2,1)S(1)} all-to-all(bf16[32,32,384]{2,1,0:T(8,128)(2,1)S(1)} %bitcast.27), channel_id=1, replica_groups=mesh['y'=4,'z'=8,'x'=4,'core'=2] {'y','z'}, dimensions={0} | all-to-all | bytes 1572864 | tf_op jit(solution)/shard_map/all_to_all | solution.py:262
  52.9 3.5 %collective-permute-start.6 = (bf16[32,384]{1,0:T(8,128)(2,1)S(1)}, bf16[32,384]{1,0:T(8,128)(2,1)S(1)}, u32[]{:S(2)}, u32[]{:S(2)}) collective-permute-start(bf16[32,384]{1,0:T(8,128)(2,1)S(1)} %fusion.2), channel_id=1, source_target_pairs={{0,1},{1,0},{2,3},{3,2},{4,5},{5,4},{6,7},{7,6},{8,9},{9,8},{10,11... | collective-permute-start | bytes 73736 | tf_op jit(solution)/shard_map/ppermute | solution.py:245
  57.3 2.1 %collective-permute-start.7 = (bf16[32,768]{1,0:T(8,128)(2,1)S(1)}, bf16[32,768]{1,0:T(8,128)(2,1)S(1)}, u32[]{:S(2)}, u32[]{:S(2)}) collective-permute-start(bf16[32,768]{1,0:T(8,128)(2,1)S(1)} %maximum_select_fusion), channel_id=1, source_target_pairs={{0,0},{1,3},{2,64},{3,67},{4,128},{5,131},{6,192},{7,195},{8,8},{9... | collective-permute-start | bytes 147464 | tf_op jit(solution)/shard_map/ppermute | solution.py:270
  59.3 2.7 %collective-permute-start.8 = (bf16[32,768]{1,0:T(8,128)(2,1)S(1)}, bf16[32,768]{1,0:T(8,128)(2,1)S(1)}, u32[]{:S(2)}, u32[]{:S(2)}) collective-permute-start(bf16[32,768]{1,0:T(8,128)(2,1)S(1)} %maximum_select_fusion), channel_id=1, source_target_pairs={{0,4},{1,7},{2,68},{3,71},{4,132},{5,135},{6,196},{7,199},{8,12},{... | collective-permute-start | bytes 147464 | tf_op jit(solution)/shard_map/ppermute | solution.py:270
  63.5 3.1 %collective-permute-start.9 = (bf16[2,32,768]{2,1,0:T(8,128)(2,1)S(1)}, bf16[2,32,768]{2,1,0:T(8,128)(2,1)S(1)}, u32[]{:S(2)}, u32[]{:S(2)}) collective-permute-start(bf16[2,32,768]{2,1,0:T(8,128)(2,1)S(1)} %pad_maximum_fusion.refs_0_), channel_id=1, source_target_pairs={{0,1},{1,0},{2,3},{3,2},{4,5},{5,4},{6,7},{7,6},{8,9},{9,8},{10,11... | collective-permute-start | bytes 294920 | tf_op jit(solution)/shard_map/ppermute | solution.py:245
  67.6 2.8 %back.4 = (bf16[4,8,32,384]{3,2,1,0:T(8,128)(2,1)S(1)}, bf16[128,768]{1,0:T(8,128)(2,1)S(1)}) custom-call(s32[4]{0:T(128)S(1)} %pad_add_fusion.at_ref, bf16[2,32,768]{2,1,0:T(8,128)(2,1)S(1)} %pad_maximum_fusion.refs_0_, bf16[2,32,768]{2,1,0:T(8,128)(2,1)S(1)} %collective-permute-done.9.refs_1_, bf16[4,768,384]{2,1,0:T(8,128)(2,1)S(1)} %keep.1.refs_1_.refs_2_, ...), custom_call_target="tpu_custom_call" | custom-call | flops 603979776 | bytes 6000000 | tf_op jit(solution)/shard_map/back/pallas_call | solution.py:178
  70.4 26.1 %all_to_all.16 = bf16[32,32,384]{2,1,0:T(8,128)(2,1)S(1)} all-to-all(bf16[32,32,384]{2,1,0:T(8,128)(2,1)S(1)} %bitcast.26), channel_id=1, replica_groups=mesh['y'=4,'z'=8,'x'=4,'core'=2] {'y','z'}, dimensions={0} | all-to-all | bytes 1572864 | tf_op jit(solution)/shard_map/all_to_all | solution.py:262
  96.6 4.8 %collective-permute-start.10 = (bf16[32,384]{1,0:T(8,128)(2,1)S(1)}, bf16[32,384]{1,0:T(8,128)(2,1)S(1)}, u32[]{:S(2)}, u32[]{:S(2)}) collective-permute-start(bf16[32,384]{1,0:T(8,128)(2,1)S(1)} %fusion.1), channel_id=1, source_target_pairs={{0,1},{1,0},{2,3},{3,2},{4,5},{5,4},{6,7},{7,6},{8,9},{9,8},{10,11... | collective-permute-start | bytes 73736 | tf_op jit(solution)/shard_map/ppermute | solution.py:245
  102.3 1.9 %collective-permute-start.11 = (bf16[32,768]{1,0:T(8,128)(2,1)S(1)}, bf16[32,768]{1,0:T(8,128)(2,1)S(1)}, u32[]{:S(2)}, u32[]{:S(2)}) collective-permute-start(bf16[32,768]{1,0:T(8,128)(2,1)S(1)} %maximum_select_fusion.1), channel_id=1, source_target_pairs={{0,0},{1,3},{2,64},{3,67},{4,128},{5,131},{6,192},{7,195},{8,8},{9... | collective-permute-start | bytes 147464 | tf_op jit(solution)/shard_map/ppermute | solution.py:270
  105.7 2.6 %collective-permute-done.11 = bf16[32,768]{1,0:T(8,128)(2,1)S(1)} collective-permute-done((bf16[32,768]{1,0:T(8,128)(2,1)S(1)}, bf16[32,768]{1,0:T(8,128)(2,1)S(1)}, u32[]{:S(2)}, u32[]{:S(2)}) %collective-permute-start.11) | collective-permute-done | bytes 49184 | tf_op jit(solution)/shard_map/ppermute | solution.py:270
  108.3 1.9 %collective-permute-start.13 = (bf16[2,32,768]{2,1,0:T(8,128)(2,1)S(1)}, bf16[2,32,768]{2,1,0:T(8,128)(2,1)S(1)}, u32[]{:S(2)}, u32[]{:S(2)}) collective-permute-start(bf16[2,32,768]{2,1,0:T(8,128)(2,1)S(1)} %pad_maximum_fusion.1.refs_0_), channel_id=1, source_target_pairs={{0,1},{1,0},{2,3},{3,2},{4,5},{5,4},{6,7},{7,6},{8,9},{9,8},{10,11... | collective-permute-start | bytes 294920 | tf_op jit(solution)/shard_map/ppermute | solution.py:245
  111.2 3.1 %back.5 = (bf16[4,8,32,384]{3,2,1,0:T(8,128)(2,1)S(1)}, bf16[128,768]{1,0:T(8,128)(2,1)S(1)}) custom-call(s32[4]{0:T(128)S(1)} %pad_add_fusion.at_ref, bf16[2,32,768]{2,1,0:T(8,128)(2,1)S(1)} %pad_maximum_fusion.1.refs_0_, bf16[2,32,768]{2,1,0:T(8,128)(2,1)S(1)} %collective-permute-done.13.refs_1_, bf16[4,768,384]{2,1,0:T(8,128)(2,1)S(1)} %keep.1.refs_1_.refs_2_, ...), custom_call_target="tpu_custom_call" | custom-call | flops 603979776 | bytes 6000000 | tf_op jit(solution)/shard_map/back/pallas_call | solution.py:178
  114.3 26.6 %all_to_all.17 = bf16[32,32,384]{2,1,0:T(8,128)(2,1)S(1)} all-to-all(bf16[32,32,384]{2,1,0:T(8,128)(2,1)S(1)} %bitcast.25), channel_id=1, replica_groups=mesh['y'=4,'z'=8,'x'=4,'core'=2] {'y','z'}, dimensions={0} | all-to-all | bytes 1572864 | tf_op jit(solution)/shard_map/all_to_all | solution.py:262
  141.0 4.4 %collective-permute-start.14 = (bf16[32,384]{1,0:T(8,128)(2,1)S(1)}, bf16[32,384]{1,0:T(8,128)(2,1)S(1)}, u32[]{:S(2)}, u32[]{:S(2)}) collective-permute-start(bf16[32,384]{1,0:T(8,128)(2,1)S(1)} %fusion), channel_id=1, source_target_pairs={{0,1},{1,0},{2,3},{3,2},{4,5},{5,4},{6,7},{7,6},{8,9},{9,8},{10,11... | collective-permute-start | bytes 73736 | tf_op jit(solution)/shard_map/ppermute | solution.py:245
  146.3 1.9 %collective-permute-start.15 = (bf16[32,768]{1,0:T(8,128)(2,1)S(1)}, bf16[32,768]{1,0:T(8,128)(2,1)S(1)}, u32[]{:S(2)}, u32[]{:S(2)}) collective-permute-start(bf16[32,768]{1,0:T(8,128)(2,1)S(1)} %maximum_select_fusion.2), channel_id=1, source_target_pairs={{0,0},{1,3},{2,64},{3,67},{4,128},{5,131},{6,192},{7,195},{8,8},{9... | collective-permute-start | bytes 147464 | tf_op jit(solution)/shard_map/ppermute | solution.py:270
  148.2 2.6 %collective-permute-start.16 = (bf16[32,768]{1,0:T(8,128)(2,1)S(1)}, bf16[32,768]{1,0:T(8,128)(2,1)S(1)}, u32[]{:S(2)}, u32[]{:S(2)}) collective-permute-start(bf16[32,768]{1,0:T(8,128)(2,1)S(1)} %maximum_select_fusion.2), channel_id=1, source_target_pairs={{0,4},{1,7},{2,68},{3,71},{4,132},{5,135},{6,196},{7,199},{8,12},{... | collective-permute-start | bytes 147464 | tf_op jit(solution)/shard_map/ppermute | solution.py:270
  152.4 2.6 %collective-permute-start.17 = (bf16[2,32,768]{2,1,0:T(8,128)(2,1)S(1)}, bf16[2,32,768]{2,1,0:T(8,128)(2,1)S(1)}, u32[]{:S(2)}, u32[]{:S(2)}) collective-permute-start(bf16[2,32,768]{2,1,0:T(8,128)(2,1)S(1)} %pad_maximum_fusion.2.first_ref), channel_id=1, source_target_pairs={{0,1},{1,0},{2,3},{3,2},{4,5},{5,4},{6,7},{7,6},{8,9},{9,8},{10,11... | collective-permute-start | bytes 294920 | tf_op jit(solution)/shard_map/ppermute | solution.py:245
  155.9 4.2 %outer.1 = bf16[768,3072]{1,0:T(8,128)(2,1)} custom-call(s32[4]{0:T(128)S(1)} %pad_add_fusion.at_ref, bf16[128,768]{1,0:T(8,128)(2,1)S(1)} %get-tuple-element.22.g4, bf16[128,768]{1,0:T(8,128)(2,1)S(1)} %get-tuple-element.25.g3, bf16[128,768]{1,0:T(8,128)(2,1)S(1)} %get-tuple-element.27.g2, bf16[2,32,768]{2,1,0:T(8,128)(2,1)S(1)} %pad_maximum_fusion.2.first_ref, ...), custom_call_target="tpu_custom_call" | custom-call | flops 2415919104 | bytes 8000000 | tf_op jit(solution)/shard_map/outer/pallas_call | solution.py:223
  (40 shorter events, 14.5 us)
Async XLA Ops:
  5.2 12.9 %collective-permute-start.5 = (bf16[4,768,384]{2,1,0:T(8,128)(2,1)}, bf16[4,768,384]{2,1,0:T(8,128)(2,1)}, u32[]{:S(2)}, u32[]{:S(2)}) collective-permute-start(bf16[4,768,384]{2,1,0:T(8,128)(2,1)} %give.1), channel_id=1, source_target_pairs={{0,1},{1,0},{2,3},{3,2},{4,5},{5,4},{6,7},{7,6},{8,9},{9,8},{10,11... | collective-permute-start | bytes 7077896 | tf_op jit(solution)/shard_map/ppermute | solution.py:245
  8.5 7.6 %collective-permute-start = (bf16[128,768]{1,0:T(8,128)(2,1)S(1)}, bf16[128,768]{1,0:T(8,128)(2,1)S(1)}, u32[]{:S(2)}, u32[]{:S(2)}) collective-permute-start(bf16[128,768]{1,0:T(8,128)(2,1)S(1)} %get-tuple-element.17), channel_id=1, source_target_pairs={{0,2},{8,10},{16,18},{24,26},{33,35},{41,43},{49,51},{57,59},{66,6... | collective-permute-start | bytes 589832 | tf_op jit(solution)/shard_map/ppermute | solution.py:250
  9.2 6.9 %collective-permute-start.1 = (bf16[128,768]{1,0:T(8,128)(2,1)S(1)}, bf16[128,768]{1,0:T(8,128)(2,1)S(1)}, u32[]{:S(2)}, u32[]{:S(2)}) collective-permute-start(bf16[128,768]{1,0:T(8,128)(2,1)S(1)} %get-tuple-element.17), channel_id=1, source_target_pairs={{0,4},{8,12},{16,20},{24,28},{33,37},{41,45},{49,53},{57,61},{66,7... | collective-permute-start | bytes 589832 | tf_op jit(solution)/shard_map/ppermute | solution.py:250
  9.9 6.2 %collective-permute-start.2 = (bf16[128,768]{1,0:T(8,128)(2,1)S(1)}, bf16[128,768]{1,0:T(8,128)(2,1)S(1)}, u32[]{:S(2)}, u32[]{:S(2)}) collective-permute-start(bf16[128,768]{1,0:T(8,128)(2,1)S(1)} %get-tuple-element.17), channel_id=1, source_target_pairs={{0,6},{8,14},{16,22},{24,30},{33,39},{41,47},{49,55},{57,63},{66,6... | collective-permute-start | bytes 589832 | tf_op jit(solution)/shard_map/ppermute | solution.py:250
  10.5 6.5 %collective-permute-start.4 = (bf16[3,32,384]{2,1,0:T(8,128)(2,1)S(1)}, bf16[3,32,384]{2,1,0:T(8,128)(2,1)S(1)}, u32[]{:S(2)}, u32[]{:S(2)}) collective-permute-start(bf16[3,32,384]{2,1,0:T(8,128)(2,1)S(1)} %get-tuple-element.19), channel_id=1, source_target_pairs={{0,1},{1,0},{2,3},{3,2},{4,5},{5,4},{6,7},{7,6},{8,9},{9,8},{10,11... | collective-permute-start | bytes 221192 | tf_op jit(solution)/shard_map/ppermute | solution.py:245
  16.1 2.0 %collective-permute-start.3 = (bf16[128,768]{1,0:T(8,128)(2,1)S(1)}, bf16[128,768]{1,0:T(8,128)(2,1)S(1)}, u32[]{:S(2)}, u32[]{:S(2)}) collective-permute-start(bf16[128,768]{1,0:T(8,128)(2,1)S(1)} %add_select_fusion), channel_id=1, source_target_pairs={{0,1},{1,0},{2,3},{3,2},{4,5},{5,4},{6,7},{7,6},{8,9},{9,8},{10,11... | collective-permute-start | bytes 589832 | tf_op jit(solution)/shard_map/ppermute | solution.py:245
  52.9 4.4 %collective-permute-start.6 = (bf16[32,384]{1,0:T(8,128)(2,1)S(1)}, bf16[32,384]{1,0:T(8,128)(2,1)S(1)}, u32[]{:S(2)}, u32[]{:S(2)}) collective-permute-start(bf16[32,384]{1,0:T(8,128)(2,1)S(1)} %fusion.2), channel_id=1, source_target_pairs={{0,1},{1,0},{2,3},{3,2},{4,5},{5,4},{6,7},{7,6},{8,9},{9,8},{10,11... | collective-permute-start | bytes 73736 | tf_op jit(solution)/shard_map/ppermute | solution.py:245
  57.3 6.0 %collective-permute-start.7 = (bf16[32,768]{1,0:T(8,128)(2,1)S(1)}, bf16[32,768]{1,0:T(8,128)(2,1)S(1)}, u32[]{:S(2)}, u32[]{:S(2)}) collective-permute-start(bf16[32,768]{1,0:T(8,128)(2,1)S(1)} %maximum_select_fusion), channel_id=1, source_target_pairs={{0,0},{1,3},{2,64},{3,67},{4,128},{5,131},{6,192},{7,195},{8,8},{9... | collective-permute-start | bytes 147464 | tf_op jit(solution)/shard_map/ppermute | solution.py:270
  59.3 4.2 %collective-permute-start.8 = (bf16[32,768]{1,0:T(8,128)(2,1)S(1)}, bf16[32,768]{1,0:T(8,128)(2,1)S(1)}, u32[]{:S(2)}, u32[]{:S(2)}) collective-permute-start(bf16[32,768]{1,0:T(8,128)(2,1)S(1)} %maximum_select_fusion), channel_id=1, source_target_pairs={{0,4},{1,7},{2,68},{3,71},{4,132},{5,135},{6,196},{7,199},{8,12},{... | collective-permute-start | bytes 147464 | tf_op jit(solution)/shard_map/ppermute | solution.py:270
  63.5 4.0 %collective-permute-start.9 = (bf16[2,32,768]{2,1,0:T(8,128)(2,1)S(1)}, bf16[2,32,768]{2,1,0:T(8,128)(2,1)S(1)}, u32[]{:S(2)}, u32[]{:S(2)}) collective-permute-start(bf16[2,32,768]{2,1,0:T(8,128)(2,1)S(1)} %pad_maximum_fusion.refs_0_), channel_id=1, source_target_pairs={{0,1},{1,0},{2,3},{3,2},{4,5},{5,4},{6,7},{7,6},{8,9},{9,8},{10,11... | collective-permute-start | bytes 294920 | tf_op jit(solution)/shard_map/ppermute | solution.py:245
  96.6 5.7 %collective-permute-start.10 = (bf16[32,384]{1,0:T(8,128)(2,1)S(1)}, bf16[32,384]{1,0:T(8,128)(2,1)S(1)}, u32[]{:S(2)}, u32[]{:S(2)}) collective-permute-start(bf16[32,384]{1,0:T(8,128)(2,1)S(1)} %fusion.1), channel_id=1, source_target_pairs={{0,1},{1,0},{2,3},{3,2},{4,5},{5,4},{6,7},{7,6},{8,9},{9,8},{10,11... | collective-permute-start | bytes 73736 | tf_op jit(solution)/shard_map/ppermute | solution.py:245
  102.3 6.0 %collective-permute-start.11 = (bf16[32,768]{1,0:T(8,128)(2,1)S(1)}, bf16[32,768]{1,0:T(8,128)(2,1)S(1)}, u32[]{:S(2)}, u32[]{:S(2)}) collective-permute-start(bf16[32,768]{1,0:T(8,128)(2,1)S(1)} %maximum_select_fusion.1), channel_id=1, source_target_pairs={{0,0},{1,3},{2,64},{3,67},{4,128},{5,131},{6,192},{7,195},{8,8},{9... | collective-permute-start | bytes 147464 | tf_op jit(solution)/shard_map/ppermute | solution.py:270
  104.2 4.1 %collective-permute-start.12 = (bf16[32,768]{1,0:T(8,128)(2,1)S(1)}, bf16[32,768]{1,0:T(8,128)(2,1)S(1)}, u32[]{:S(2)}, u32[]{:S(2)}) collective-permute-start(bf16[32,768]{1,0:T(8,128)(2,1)S(1)} %maximum_select_fusion.1), channel_id=1, source_target_pairs={{0,4},{1,7},{2,68},{3,71},{4,132},{5,135},{6,196},{7,199},{8,12},{... | collective-permute-start | bytes 147464 | tf_op jit(solution)/shard_map/ppermute | solution.py:270
  108.3 2.9 %collective-permute-start.13 = (bf16[2,32,768]{2,1,0:T(8,128)(2,1)S(1)}, bf16[2,32,768]{2,1,0:T(8,128)(2,1)S(1)}, u32[]{:S(2)}, u32[]{:S(2)}) collective-permute-start(bf16[2,32,768]{2,1,0:T(8,128)(2,1)S(1)} %pad_maximum_fusion.1.refs_0_), channel_id=1, source_target_pairs={{0,1},{1,0},{2,3},{3,2},{4,5},{5,4},{6,7},{7,6},{8,9},{9,8},{10,11... | collective-permute-start | bytes 294920 | tf_op jit(solution)/shard_map/ppermute | solution.py:245
  111.2 44.7 %copy-start = (bf16[5,3072,128]{2,1,0:T(8,128)(2,1)S(1)}, bf16[5,3072,128]{2,1,0:T(8,128)(2,1)}, u32[]{:S(2)}) copy-start(bf16[5,3072,128]{2,1,0:T(8,128)(2,1)} %rates_ref.3) | copy-start | bytes 11796484
  141.0 5.3 %collective-permute-start.14 = (bf16[32,384]{1,0:T(8,128)(2,1)S(1)}, bf16[32,384]{1,0:T(8,128)(2,1)S(1)}, u32[]{:S(2)}, u32[]{:S(2)}) collective-permute-start(bf16[32,384]{1,0:T(8,128)(2,1)S(1)} %fusion), channel_id=1, source_target_pairs={{0,1},{1,0},{2,3},{3,2},{4,5},{5,4},{6,7},{7,6},{8,9},{9,8},{10,11... | collective-permute-start | bytes 73736 | tf_op jit(solution)/shard_map/ppermute | solution.py:245
  146.3 6.0 %collective-permute-start.15 = (bf16[32,768]{1,0:T(8,128)(2,1)S(1)}, bf16[32,768]{1,0:T(8,128)(2,1)S(1)}, u32[]{:S(2)}, u32[]{:S(2)}) collective-permute-start(bf16[32,768]{1,0:T(8,128)(2,1)S(1)} %maximum_select_fusion.2), channel_id=1, source_target_pairs={{0,0},{1,3},{2,64},{3,67},{4,128},{5,131},{6,192},{7,195},{8,8},{9... | collective-permute-start | bytes 147464 | tf_op jit(solution)/shard_map/ppermute | solution.py:270
  148.2 4.1 %collective-permute-start.16 = (bf16[32,768]{1,0:T(8,128)(2,1)S(1)}, bf16[32,768]{1,0:T(8,128)(2,1)S(1)}, u32[]{:S(2)}, u32[]{:S(2)}) collective-permute-start(bf16[32,768]{1,0:T(8,128)(2,1)S(1)} %maximum_select_fusion.2), channel_id=1, source_target_pairs={{0,4},{1,7},{2,68},{3,71},{4,132},{5,135},{6,196},{7,199},{8,12},{... | collective-permute-start | bytes 147464 | tf_op jit(solution)/shard_map/ppermute | solution.py:270
  152.4 3.6 %collective-permute-start.17 = (bf16[2,32,768]{2,1,0:T(8,128)(2,1)S(1)}, bf16[2,32,768]{2,1,0:T(8,128)(2,1)S(1)}, u32[]{:S(2)}, u32[]{:S(2)}) collective-permute-start(bf16[2,32,768]{2,1,0:T(8,128)(2,1)S(1)} %pad_maximum_fusion.2.first_ref), channel_id=1, source_target_pairs={{0,1},{1,0},{2,3},{3,2},{4,5},{5,4},{6,7},{7,6},{8,9},{9,8},{10,11... | collective-permute-start | bytes 294920 | tf_op jit(solution)/shard_map/ppermute | solution.py:245

commit v7 on v5

--- a/solution.py
+++ b/solution.py
@@ -13,7 +13,7 @@
 QUARTER = 768
 TRIALS = 128
 SLICE = 32
-FIRST, BACK, OUTER, KEEP = 52, 8, 52, 48
+FIRST, BACK, OUTER, KEEP = 52, 8, 24, 48
 COLS = 3072
 VMEM = pl.BlockSpec(memory_space=pltpu.VMEM)
 SMEM = pl.BlockSpec(memory_space=pltpu.SMEM)
@@ -180,46 +180,38 @@
 
 
 def outer_kernel(
-    at_ref, g4, g3, g2, first_ref, second_ref, rates_ref, out_ref, g_ref, turned_ref, held_ref, done_ref, sems
+    at_ref, g4, g3, g2, first_ref, second_ref, rates_ref, out_ref, g_ref, turned_ref, done_ref, sems
 ):
-    def came(j):
-        columns = pl.ds(j * TILE, TILE)
-        return pltpu.make_async_copy(rates_ref.at[0:STEPS, columns], held_ref.at[:, columns], sems.at[0, j])
-
-    def went(j):
-        columns = pl.ds(j * TILE, TILE)
-        return pltpu.make_async_copy(done_ref.at[j], out_ref.at[:, columns], sems.at[1, j])
-
-    for j in range(TILES):
-        came(j).start()
+    went = [
+        pltpu.make_async_copy(done_ref.at[j], out_ref.at[:, pl.ds(j * TILE, TILE)], sems.at[j])
+        for j in range(TILES)
+    ]
     for t, ref in ((3, g4), (2, g3), (1, g2)):
         turned_ref[:, t * TRIALS : (t + 1) * TRIALS] = ref[...].T
     fill(at_ref, (first_ref, second_ref), g_ref)
     turned_ref[:, :TRIALS] = g_ref[...].T
     for j in range(TILES):
-        came(j).wait()
-        columns = slice(j * TILE, (j + 1) * TILE)
-        before = jnp.concatenate([held_ref[t, columns, :] for t in range(STEPS)], axis=1)
+        part = slice(j * TILE, (j + 1) * TILE)
+        before = jnp.concatenate([rates_ref[t, part, :] for t in range(STEPS)], axis=1)
         done_ref[j] = lax.dot_general(
             turned_ref[...], before, (((1,), (1,)), ((), ())), preferred_element_type=jnp.float32
         ).astype(jnp.bfloat16)
-        went(j).start()
-    for j in range(TILES):
-        went(j).wait()
+        went[j].start()
+    for copy in went:
+        copy.wait()
 
 
 def outer(at, full, pair, rates):
     return pl.pallas_call(
         outer_kernel,
-        in_specs=[SMEM] + [VMEM] * 5 + [HBM],
+        in_specs=[SMEM] + [VMEM] * 6,
         out_specs=HBM,
         out_shape=jax.ShapeDtypeStruct((QUARTER, COLS), jnp.bfloat16),
         scratch_shapes=[
             pltpu.VMEM((TRIALS, QUARTER), jnp.bfloat16),
             pltpu.VMEM((QUARTER, STEPS * TRIALS), jnp.bfloat16),
-            pltpu.VMEM((STEPS, COLS, TRIALS), jnp.bfloat16),
             pltpu.VMEM((TILES, QUARTER, TILE), jnp.bfloat16),
-            pltpu.SemaphoreType.DMA((2, TILES)),
+            pltpu.SemaphoreType.DMA((TILES,)),
         ],
         cost_estimate=cost(2 * STEPS * TRIALS * QUARTER * COLS, 8_000_000),
         compiler_params=params(OUTER),
@@ -236,7 +228,8 @@
 
     is_root_core = core == z // 4
     root, before, other = first(at, rates)
-    parts = [lax.ppermute(root, EVERY, from_root(shift)) for shift in (1, 2, 3)]
+    far = lax.ppermute(root, EVERY, from_root(2))
+    parts = [far] + [lax.ppermute(root, EVERY, from_root(shift)) for shift in (1, 3)]
     mine, theirs = split(at, lax.optimization_barrier((weights, root))[0])
     theirs = swapped(theirs)
     before = jnp.where(is_root_core, before, swapped(other))

time: 168 us -> 167 us (level)
  waiting for transfers between devices: 19.9 us -> 22.8 us
  Pallas kernels: 20.5 us -> 18.7 us
    ppermute x6, starting transfers between devices: 12.5 us -> 8.48 us  [whole(): lax.ppermute(share, EVERY, across(j))]
    ppermute x9, starting transfers between devices: 24.5 us -> 27.8 us  [swapped(): return lax.ppermute(array, 'core', SWAP)]
    ppermute x6, waiting for transfers between devices: 13.5 us -> 16.4 us  [whole(): lax.ppermute(share, EVERY, across(j))]
    pallas_call x1, Pallas kernels: 6.34 us -> 4.21 us  [outer(): pl.pallas_call(outer_kernel, in_specs=[SMEM] + [VMEM] * 6, out_specs=HBM,...]
where the time goes in v7:
time: 167 us; the launch traced here: 166 us
  blocking collectives  85.7 us (51%)
  starting transfers between devices  38.3 us (23%)
  waiting for transfers between devices  22.8 us (14%)
  Pallas kernels  18.7 us (11%)
    all_to_all x3, blocking collectives, whole(): lax.all_to_all(sums.reshape(Y * Z, SLICE, HALF), ('y', 'z'), 0, 0, tiled=...  85.7 us
    ppermute x9, starting transfers between devices, swapped(): return lax.ppermute(array, 'core', SWAP)  27.8 us
    ppermute x6, waiting for transfers between devices, whole(): lax.ppermute(share, EVERY, across(j))  16.4 us
    pallas_call x3, Pallas kernels, back(): pl.pallas_call(back_kernel, in_specs=[SMEM] + [VMEM] * len(pair) + [VMEM,...  8.58 us
    ppermute x6, starting transfers between devices, whole(): lax.ppermute(share, EVERY, across(j))  8.48 us
    ppermute x9, waiting for transfers between devices, swapped(): return lax.ppermute(array, 'core', SWAP)  6.44 us
    pallas_call x1, Pallas kernels, outer(): pl.pallas_call(outer_kernel, in_specs=[SMEM] + [VMEM] * 6, out_specs=HBM,...  4.21 us
    pallas_call x1, Pallas kernels, split(): pl.pallas_call(split_kernel, in_specs=[SMEM, HBM], out_specs=[VMEM, HBM],...  3.86 us
  transfers between devices with their start and end apart: 18, of which 13 were waited for; matrix products, arithmetic and copies ran while one was open for 0% of the time, Pallas kernels for 0%

profile of v7, /device:TPU:49, one launch (start us, length us, event | category | flops | bytes accessed | tf_op | source)
XLA Modules:
  0.0 166.4 jit_solution(15704182569312310990)
XLA Ops:
  0.1 2.0 %first.1 = (bf16[128,768]{1,0:T(8,128)(2,1)S(1)}, bf16[3,32,384]{2,1,0:T(8,128)(2,1)S(1)}, bf16[3,32,384]{2,1,0:T(8,128)(2,1)S(1)}) custom-call(s32[4]{0:T(128)S(1)} %pad_add_fusion.at_ref, bf16[5,3072,128]{2,1,0:T(8,128)(2,1)} %rates_ref.3), custom_call_target="tpu_custom_call" | custom-call | tf_op jit(solution)/shard_map/first/pallas_call | solution.py:71
  2.1 3.9 %split.1 = (bf16[4,768,384]{2,1,0:T(8,128)(2,1)S(1)}, bf16[4,768,384]{2,1,0:T(8,128)(2,1)}) custom-call(s32[4]{0:T(128)S(1)} %pad_add_fusion.at_ref, bf16[768,3072]{1,0:T(8,128)(2,1)} %w_ref), custom_call_target="tpu_custom_call" | custom-call | bytes 9437184 | tf_op jit(solution)/shard_map/split/pallas_call | solution.py:114
  9.6 9.9 %collective-permute-start.3 = (bf16[128,768]{1,0:T(8,128)(2,1)S(1)}, bf16[128,768]{1,0:T(8,128)(2,1)S(1)}, u32[]{:S(2)}, u32[]{:S(2)}) collective-permute-start(bf16[128,768]{1,0:T(8,128)(2,1)S(1)} %add_select_fusion), channel_id=1, source_target_pairs={{0,1},{1,0},{2,3},{3,2},{4,5},{5,4},{6,7},{7,6},{8,9},{9,8},{10,11... | collective-permute-start | bytes 589832 | tf_op jit(solution)/shard_map/ppermute | solution.py:227
  20.6 2.7 %back.3 = (bf16[4,8,32,384]{3,2,1,0:T(8,128)(2,1)S(1)}, bf16[128,768]{1,0:T(8,128)(2,1)S(1)}) custom-call(s32[4]{0:T(128)S(1)} %pad_add_fusion.at_ref, bf16[128,768]{1,0:T(8,128)(2,1)S(1)} %broadcast_select_fusion.refs_0_, bf16[4,768,384]{2,1,0:T(8,128)(2,1)S(1)} %get-tuple-element.24.refs_1_.refs_2_, bf16[4,768,384]{2,1,0:T(8,128)(2,1)} %collective-permute-done.5.refs_2_.refs_3_), custom_call_target="tpu_custom_call" | custom-call | flops 603979776 | bytes 6000000 | tf_op jit(solution)/shard_map/back/pallas_call | solution.py:160
  23.3 31.3 %all_to_all.15 = bf16[32,32,384]{2,1,0:T(8,128)(2,1)S(1)} all-to-all(bf16[32,32,384]{2,1,0:T(8,128)(2,1)S(1)} %bitcast.27), channel_id=1, replica_groups=mesh['y'=4,'z'=8,'x'=4,'core'=2] {'y','z'}, dimensions={0} | all-to-all | bytes 1572864 | tf_op jit(solution)/shard_map/all_to_all | solution.py:245
  57.8 2.0 %collective-permute-start.7 = (bf16[32,768]{1,0:T(8,128)(2,1)S(1)}, bf16[32,768]{1,0:T(8,128)(2,1)S(1)}, u32[]{:S(2)}, u32[]{:S(2)}) collective-permute-start(bf16[32,768]{1,0:T(8,128)(2,1)S(1)} %maximum_select_fusion), channel_id=1, source_target_pairs={{0,0},{1,3},{2,64},{3,67},{4,128},{5,131},{6,192},{7,195},{8,8},{9... | collective-permute-start | bytes 147464 | tf_op jit(solution)/shard_map/ppermute | solution.py:253
  59.9 2.5 %collective-permute-done.8 = bf16[32,768]{1,0:T(8,128)(2,1)S(1)} collective-permute-done((bf16[32,768]{1,0:T(8,128)(2,1)S(1)}, bf16[32,768]{1,0:T(8,128)(2,1)S(1)}, u32[]{:S(2)}, u32[]{:S(2)}) %collective-permute-start.8) | collective-permute-done | bytes 49184 | tf_op jit(solution)/shard_map/ppermute | solution.py:253
  62.3 3.1 %collective-permute-done.7 = bf16[32,768]{1,0:T(8,128)(2,1)S(1)} collective-permute-done((bf16[32,768]{1,0:T(8,128)(2,1)S(1)}, bf16[32,768]{1,0:T(8,128)(2,1)S(1)}, u32[]{:S(2)}, u32[]{:S(2)}) %collective-permute-start.7) | collective-permute-done | bytes 49184 | tf_op jit(solution)/shard_map/ppermute | solution.py:253
  65.4 3.7 %collective-permute-start.9 = (bf16[2,32,768]{2,1,0:T(8,128)(2,1)S(1)}, bf16[2,32,768]{2,1,0:T(8,128)(2,1)S(1)}, u32[]{:S(2)}, u32[]{:S(2)}) collective-permute-start(bf16[2,32,768]{2,1,0:T(8,128)(2,1)S(1)} %pad_maximum_fusion.refs_0_), channel_id=1, source_target_pairs={{0,1},{1,0},{2,3},{3,2},{4,5},{5,4},{6,7},{7,6},{8,9},{9,8},{10,11... | collective-permute-start | bytes 294920 | tf_op jit(solution)/shard_map/ppermute | solution.py:227
  70.1 2.8 %back.4 = (bf16[4,8,32,384]{3,2,1,0:T(8,128)(2,1)S(1)}, bf16[128,768]{1,0:T(8,128)(2,1)S(1)}) custom-call(s32[4]{0:T(128)S(1)} %pad_add_fusion.at_ref, bf16[2,32,768]{2,1,0:T(8,128)(2,1)S(1)} %pad_maximum_fusion.refs_0_, bf16[2,32,768]{2,1,0:T(8,128)(2,1)S(1)} %collective-permute-done.9.refs_1_, bf16[4,768,384]{2,1,0:T(8,128)(2,1)S(1)} %get-tuple-element.24.refs_1_.refs_2_, ...), custom_call_target="tpu_custom_call" | custom-call | flops 603979776 | bytes 6000000 | tf_op jit(solution)/shard_map/back/pallas_call | solution.py:160
  72.9 27.2 %all_to_all.16 = bf16[32,32,384]{2,1,0:T(8,128)(2,1)S(1)} all-to-all(bf16[32,32,384]{2,1,0:T(8,128)(2,1)S(1)} %bitcast.26), channel_id=1, replica_groups=mesh['y'=4,'z'=8,'x'=4,'core'=2] {'y','z'}, dimensions={0} | all-to-all | bytes 1572864 | tf_op jit(solution)/shard_map/all_to_all | solution.py:245
  100.2 1.6 collective-permute-start.10
  103.4 2.0 %collective-permute-start.11 = (bf16[32,768]{1,0:T(8,128)(2,1)S(1)}, bf16[32,768]{1,0:T(8,128)(2,1)S(1)}, u32[]{:S(2)}, u32[]{:S(2)}) collective-permute-start(bf16[32,768]{1,0:T(8,128)(2,1)S(1)} %maximum_select_fusion.1), channel_id=1, source_target_pairs={{0,0},{1,3},{2,64},{3,67},{4,128},{5,131},{6,192},{7,195},{8,8},{9... | collective-permute-start | bytes 147464 | tf_op jit(solution)/shard_map/ppermute | solution.py:253
  105.5 2.7 %collective-permute-done.12 = bf16[32,768]{1,0:T(8,128)(2,1)S(1)} collective-permute-done((bf16[32,768]{1,0:T(8,128)(2,1)S(1)}, bf16[32,768]{1,0:T(8,128)(2,1)S(1)}, u32[]{:S(2)}, u32[]{:S(2)}) %collective-permute-start.12) | collective-permute-done | bytes 49184 | tf_op jit(solution)/shard_map/ppermute | solution.py:253
  108.1 3.0 %collective-permute-done.11 = bf16[32,768]{1,0:T(8,128)(2,1)S(1)} collective-permute-done((bf16[32,768]{1,0:T(8,128)(2,1)S(1)}, bf16[32,768]{1,0:T(8,128)(2,1)S(1)}, u32[]{:S(2)}, u32[]{:S(2)}) %collective-permute-start.11) | collective-permute-done | bytes 49184 | tf_op jit(solution)/shard_map/ppermute | solution.py:253
  111.1 3.8 %collective-permute-start.13 = (bf16[2,32,768]{2,1,0:T(8,128)(2,1)S(1)}, bf16[2,32,768]{2,1,0:T(8,128)(2,1)S(1)}, u32[]{:S(2)}, u32[]{:S(2)}) collective-permute-start(bf16[2,32,768]{2,1,0:T(8,128)(2,1)S(1)} %pad_maximum_fusion.1.refs_0_), channel_id=1, source_target_pairs={{0,1},{1,0},{2,3},{3,2},{4,5},{5,4},{6,7},{7,6},{8,9},{9,8},{10,11... | collective-permute-start | bytes 294920 | tf_op jit(solution)/shard_map/ppermute | solution.py:227
  115.9 3.1 %back.5 = (bf16[4,8,32,384]{3,2,1,0:T(8,128)(2,1)S(1)}, bf16[128,768]{1,0:T(8,128)(2,1)S(1)}) custom-call(s32[4]{0:T(128)S(1)} %pad_add_fusion.at_ref, bf16[2,32,768]{2,1,0:T(8,128)(2,1)S(1)} %pad_maximum_fusion.1.refs_0_, bf16[2,32,768]{2,1,0:T(8,128)(2,1)S(1)} %collective-permute-done.13.refs_1_, ...), custom_call_target="tpu_custom_call" | custom-call | flops 603979776 | bytes 6000000 | tf_op jit(solution)/shard_map/back/pallas_call | solution.py:160
  119.0 27.2 %all_to_all.17 = bf16[32,32,384]{2,1,0:T(8,128)(2,1)S(1)} all-to-all(bf16[32,32,384]{2,1,0:T(8,128)(2,1)S(1)} %bitcast.25), channel_id=1, replica_groups=mesh['y'=4,'z'=8,'x'=4,'core'=2] {'y','z'}, dimensions={0} | all-to-all | bytes 1572864 | tf_op jit(solution)/shard_map/all_to_all | solution.py:245
  146.3 1.6 collective-permute-start.14
  149.3 2.3 %collective-permute-start.15 = (bf16[32,768]{1,0:T(8,128)(2,1)S(1)}, bf16[32,768]{1,0:T(8,128)(2,1)S(1)}, u32[]{:S(2)}, u32[]{:S(2)}) collective-permute-start(bf16[32,768]{1,0:T(8,128)(2,1)S(1)} %maximum_select_fusion.2), channel_id=1, source_target_pairs={{0,0},{1,3},{2,64},{3,67},{4,128},{5,131},{6,192},{7,195},{8,8},{9... | collective-permute-start | bytes 147464 | tf_op jit(solution)/shard_map/ppermute | solution.py:253
  151.6 2.7 %collective-permute-done.16 = bf16[32,768]{1,0:T(8,128)(2,1)S(1)} collective-permute-done((bf16[32,768]{1,0:T(8,128)(2,1)S(1)}, bf16[32,768]{1,0:T(8,128)(2,1)S(1)}, u32[]{:S(2)}, u32[]{:S(2)}) %collective-permute-start.16) | collective-permute-done | bytes 49184 | tf_op jit(solution)/shard_map/ppermute | solution.py:253
  154.3 2.5 %collective-permute-done.15 = bf16[32,768]{1,0:T(8,128)(2,1)S(1)} collective-permute-done((bf16[32,768]{1,0:T(8,128)(2,1)S(1)}, bf16[32,768]{1,0:T(8,128)(2,1)S(1)}, u32[]{:S(2)}, u32[]{:S(2)}) %collective-permute-start.15) | collective-permute-done | bytes 49184 | tf_op jit(solution)/shard_map/ppermute | solution.py:253
  156.8 4.3 %collective-permute-start.17 = (bf16[2,32,768]{2,1,0:T(8,128)(2,1)S(1)}, bf16[2,32,768]{2,1,0:T(8,128)(2,1)S(1)}, u32[]{:S(2)}, u32[]{:S(2)}) collective-permute-start(bf16[2,32,768]{2,1,0:T(8,128)(2,1)S(1)} %pad_maximum_fusion.2.first_ref), channel_id=1, source_target_pairs={{0,1},{1,0},{2,3},{3,2},{4,5},{5,4},{6,7},{7,6},{8,9},{9,8},{10,11... | collective-permute-start | bytes 294920 | tf_op jit(solution)/shard_map/ppermute | solution.py:227
  162.0 4.2 %outer.1 = bf16[768,3072]{1,0:T(8,128)(2,1)} custom-call(s32[4]{0:T(128)S(1)} %pad_add_fusion.at_ref, bf16[128,768]{1,0:T(8,128)(2,1)S(1)} %get-tuple-element.26.g4, bf16[128,768]{1,0:T(8,128)(2,1)S(1)} %get-tuple-element.29.g3, bf16[128,768]{1,0:T(8,128)(2,1)S(1)} %get-tuple-element.31.g2, bf16[2,32,768]{2,1,0:T(8,128)(2,1)S(1)} %pad_maximum_fusion.2.first_ref, ...), custom_call_target="tpu_custom_call" | custom-call | flops 2415919104 | bytes 8000000 | tf_op jit(solution)/shard_map/outer/pallas_call | solution.py:205
  (39 shorter events, 14.0 us)
Async XLA Ops:
  6.0 14.6 %collective-permute-start.5 = (bf16[4,768,384]{2,1,0:T(8,128)(2,1)}, bf16[4,768,384]{2,1,0:T(8,128)(2,1)}, u32[]{:S(2)}, u32[]{:S(2)}) collective-permute-start(bf16[4,768,384]{2,1,0:T(8,128)(2,1)} %get-tuple-element.25), channel_id=1, source_target_pairs={{0,1},{1,0},{2,3},{3,2},{4,5},{5,4},{6,7},{7,6},{8,9},{9,8},{10,11... | collective-permute-start | bytes 7077896 | tf_op jit(solution)/shard_map/ppermute | solution.py:227
  6.8 2.8 %collective-permute-start.2 = (bf16[128,768]{1,0:T(8,128)(2,1)S(1)}, bf16[128,768]{1,0:T(8,128)(2,1)S(1)}, u32[]{:S(2)}, u32[]{:S(2)}) collective-permute-start(bf16[128,768]{1,0:T(8,128)(2,1)S(1)} %get-tuple-element.19), channel_id=1, source_target_pairs={{0,6},{8,14},{16,22},{24,30},{33,39},{41,47},{49,55},{57,63},{66,6... | collective-permute-start | bytes 589832 | tf_op jit(solution)/shard_map/ppermute | solution.py:232
  7.4 2.1 %collective-permute-start.1 = (bf16[128,768]{1,0:T(8,128)(2,1)S(1)}, bf16[128,768]{1,0:T(8,128)(2,1)S(1)}, u32[]{:S(2)}, u32[]{:S(2)}) collective-permute-start(bf16[128,768]{1,0:T(8,128)(2,1)S(1)} %get-tuple-element.19), channel_id=1, source_target_pairs={{0,2},{8,10},{16,18},{24,26},{33,35},{41,43},{49,51},{57,59},{66,6... | collective-permute-start | bytes 589832 | tf_op jit(solution)/shard_map/ppermute | solution.py:232
  8.1 1.4 collective-permute-start
  8.8 10.7 %collective-permute-start.4 = (bf16[3,32,384]{2,1,0:T(8,128)(2,1)S(1)}, bf16[3,32,384]{2,1,0:T(8,128)(2,1)S(1)}, u32[]{:S(2)}, u32[]{:S(2)}) collective-permute-start(bf16[3,32,384]{2,1,0:T(8,128)(2,1)S(1)} %get-tuple-element.21), channel_id=1, source_target_pairs={{0,1},{1,0},{2,3},{3,2},{4,5},{5,4},{6,7},{7,6},{8,9},{9,8},{10,11... | collective-permute-start | bytes 221192 | tf_op jit(solution)/shard_map/ppermute | solution.py:227
  9.6 10.9 %collective-permute-start.3 = (bf16[128,768]{1,0:T(8,128)(2,1)S(1)}, bf16[128,768]{1,0:T(8,128)(2,1)S(1)}, u32[]{:S(2)}, u32[]{:S(2)}) collective-permute-start(bf16[128,768]{1,0:T(8,128)(2,1)S(1)} %add_select_fusion), channel_id=1, source_target_pairs={{0,1},{1,0},{2,3},{3,2},{4,5},{5,4},{6,7},{7,6},{8,9},{9,8},{10,11... | collective-permute-start | bytes 589832 | tf_op jit(solution)/shard_map/ppermute | solution.py:227
  54.8 2.1 %collective-permute-start.6 = (bf16[32,384]{1,0:T(8,128)(2,1)S(1)}, bf16[32,384]{1,0:T(8,128)(2,1)S(1)}, u32[]{:S(2)}, u32[]{:S(2)}) collective-permute-start(bf16[32,384]{1,0:T(8,128)(2,1)S(1)} %fusion.2), channel_id=1, source_target_pairs={{0,1},{1,0},{2,3},{3,2},{4,5},{5,4},{6,7},{7,6},{8,9},{9,8},{10,11... | collective-permute-start | bytes 73736 | tf_op jit(solution)/shard_map/ppermute | solution.py:227
  56.9 5.5 %collective-permute-start.8 = (bf16[32,768]{1,0:T(8,128)(2,1)S(1)}, bf16[32,768]{1,0:T(8,128)(2,1)S(1)}, u32[]{:S(2)}, u32[]{:S(2)}) collective-permute-start(bf16[32,768]{1,0:T(8,128)(2,1)S(1)} %maximum_select_fusion), channel_id=1, source_target_pairs={{0,4},{1,7},{2,68},{3,71},{4,132},{5,135},{6,196},{7,199},{8,12},{... | collective-permute-start | bytes 147464 | tf_op jit(solution)/shard_map/ppermute | solution.py:253
  57.8 7.6 %collective-permute-start.7 = (bf16[32,768]{1,0:T(8,128)(2,1)S(1)}, bf16[32,768]{1,0:T(8,128)(2,1)S(1)}, u32[]{:S(2)}, u32[]{:S(2)}) collective-permute-start(bf16[32,768]{1,0:T(8,128)(2,1)S(1)} %maximum_select_fusion), channel_id=1, source_target_pairs={{0,0},{1,3},{2,64},{3,67},{4,128},{5,131},{6,192},{7,195},{8,8},{9... | collective-permute-start | bytes 147464 | tf_op jit(solution)/shard_map/ppermute | solution.py:253
  65.4 4.7 %collective-permute-start.9 = (bf16[2,32,768]{2,1,0:T(8,128)(2,1)S(1)}, bf16[2,32,768]{2,1,0:T(8,128)(2,1)S(1)}, u32[]{:S(2)}, u32[]{:S(2)}) collective-permute-start(bf16[2,32,768]{2,1,0:T(8,128)(2,1)S(1)} %pad_maximum_fusion.refs_0_), channel_id=1, source_target_pairs={{0,1},{1,0},{2,3},{3,2},{4,5},{5,4},{6,7},{7,6},{8,9},{9,8},{10,11... | collective-permute-start | bytes 294920 | tf_op jit(solution)/shard_map/ppermute | solution.py:227
  100.2 2.5 %collective-permute-start.10 = (bf16[32,384]{1,0:T(8,128)(2,1)S(1)}, bf16[32,384]{1,0:T(8,128)(2,1)S(1)}, u32[]{:S(2)}, u32[]{:S(2)}) collective-permute-start(bf16[32,384]{1,0:T(8,128)(2,1)S(1)} %fusion.1), channel_id=1, source_target_pairs={{0,1},{1,0},{2,3},{3,2},{4,5},{5,4},{6,7},{7,6},{8,9},{9,8},{10,11... | collective-permute-start | bytes 73736 | tf_op jit(solution)/shard_map/ppermute | solution.py:227
  102.7 5.4 %collective-permute-start.12 = (bf16[32,768]{1,0:T(8,128)(2,1)S(1)}, bf16[32,768]{1,0:T(8,128)(2,1)S(1)}, u32[]{:S(2)}, u32[]{:S(2)}) collective-permute-start(bf16[32,768]{1,0:T(8,128)(2,1)S(1)} %maximum_select_fusion.1), channel_id=1, source_target_pairs={{0,4},{1,7},{2,68},{3,71},{4,132},{5,135},{6,196},{7,199},{8,12},{... | collective-permute-start | bytes 147464 | tf_op jit(solution)/shard_map/ppermute | solution.py:253
  103.4 7.7 %collective-permute-start.11 = (bf16[32,768]{1,0:T(8,128)(2,1)S(1)}, bf16[32,768]{1,0:T(8,128)(2,1)S(1)}, u32[]{:S(2)}, u32[]{:S(2)}) collective-permute-start(bf16[32,768]{1,0:T(8,128)(2,1)S(1)} %maximum_select_fusion.1), channel_id=1, source_target_pairs={{0,0},{1,3},{2,64},{3,67},{4,128},{5,131},{6,192},{7,195},{8,8},{9... | collective-permute-start | bytes 147464 | tf_op jit(solution)/shard_map/ppermute | solution.py:253
  111.1 4.8 %collective-permute-start.13 = (bf16[2,32,768]{2,1,0:T(8,128)(2,1)S(1)}, bf16[2,32,768]{2,1,0:T(8,128)(2,1)S(1)}, u32[]{:S(2)}, u32[]{:S(2)}) collective-permute-start(bf16[2,32,768]{2,1,0:T(8,128)(2,1)S(1)} %pad_maximum_fusion.1.refs_0_), channel_id=1, source_target_pairs={{0,1},{1,0},{2,3},{3,2},{4,5},{5,4},{6,7},{7,6},{8,9},{9,8},{10,11... | collective-permute-start | bytes 294920 | tf_op jit(solution)/shard_map/ppermute | solution.py:227
  115.9 46.1 %copy-start = (bf16[5,3072,128]{2,1,0:T(8,128)(2,1)S(1)}, bf16[5,3072,128]{2,1,0:T(8,128)(2,1)}, u32[]{:S(2)}) copy-start(bf16[5,3072,128]{2,1,0:T(8,128)(2,1)} %rates_ref.3) | copy-start | bytes 11796484
  146.3 2.5 %collective-permute-start.14 = (bf16[32,384]{1,0:T(8,128)(2,1)S(1)}, bf16[32,384]{1,0:T(8,128)(2,1)S(1)}, u32[]{:S(2)}, u32[]{:S(2)}) collective-permute-start(bf16[32,384]{1,0:T(8,128)(2,1)S(1)} %fusion), channel_id=1, source_target_pairs={{0,1},{1,0},{2,3},{3,2},{4,5},{5,4},{6,7},{7,6},{8,9},{9,8},{10,11... | collective-permute-start | bytes 73736 | tf_op jit(solution)/shard_map/ppermute | solution.py:227
  148.8 5.4 %collective-permute-start.16 = (bf16[32,768]{1,0:T(8,128)(2,1)S(1)}, bf16[32,768]{1,0:T(8,128)(2,1)S(1)}, u32[]{:S(2)}, u32[]{:S(2)}) collective-permute-start(bf16[32,768]{1,0:T(8,128)(2,1)S(1)} %maximum_select_fusion.2), channel_id=1, source_target_pairs={{0,4},{1,7},{2,68},{3,71},{4,132},{5,135},{6,196},{7,199},{8,12},{... | collective-permute-start | bytes 147464 | tf_op jit(solution)/shard_map/ppermute | solution.py:253
  149.3 7.5 %collective-permute-start.15 = (bf16[32,768]{1,0:T(8,128)(2,1)S(1)}, bf16[32,768]{1,0:T(8,128)(2,1)S(1)}, u32[]{:S(2)}, u32[]{:S(2)}) collective-permute-start(bf16[32,768]{1,0:T(8,128)(2,1)S(1)} %maximum_select_fusion.2), channel_id=1, source_target_pairs={{0,0},{1,3},{2,64},{3,67},{4,128},{5,131},{6,192},{7,195},{8,8},{9... | collective-permute-start | bytes 147464 | tf_op jit(solution)/shard_map/ppermute | solution.py:253
  156.8 5.3 %collective-permute-start.17 = (bf16[2,32,768]{2,1,0:T(8,128)(2,1)S(1)}, bf16[2,32,768]{2,1,0:T(8,128)(2,1)S(1)}, u32[]{:S(2)}, u32[]{:S(2)}) collective-permute-start(bf16[2,32,768]{2,1,0:T(8,128)(2,1)S(1)} %pad_maximum_fusion.2.first_ref), channel_id=1, source_target_pairs={{0,1},{1,0},{2,3},{3,2},{4,5},{5,4},{6,7},{7,6},{8,9},{9,8},{10,11... | collective-permute-start | bytes 294920 | tf_op jit(solution)/shard_map/ppermute | solution.py:227

commit v8 on v6

--- a/solution.py
+++ b/solution.py
@@ -13,7 +13,7 @@
 QUARTER = 768
 TRIALS = 128
 SLICE = 32
-FIRST, BACK, OUTER, KEEP = 52, 8, 24, 48
+FIRST, BACK, OUTER, KEEP = 52, 48, 24, 48
 COLS = 3072
 VMEM = pl.BlockSpec(memory_space=pltpu.VMEM)
 SMEM = pl.BlockSpec(memory_space=pltpu.SMEM)
@@ -89,37 +89,6 @@
     return pl.ds(pl.multiple_of((2 * q + part) * HALF, 128), HALF)
 
 
-def give_kernel(at_ref, w_ref, theirs_ref, held_ref, sems):
-    took = [
-        pltpu.make_async_copy(w_ref.at[:, columns(q, 1 - at_ref[1])], held_ref.at[q], sems.at[0, q])
-        for q in range(4)
-    ]
-    gave = [pltpu.make_async_copy(held_ref.at[q], theirs_ref.at[q], sems.at[1, q]) for q in range(4)]
-    for copy in took:
-        copy.start()
-    for q in range(4):
-        took[q].wait()
-        gave[q].start()
-    for copy in gave:
-        copy.wait()
-
-
-def give(at, weights):
-    return pl.pallas_call(
-        give_kernel,
-        in_specs=[SMEM, HBM],
-        out_specs=HBM,
-        out_shape=jax.ShapeDtypeStruct((4, QUARTER, HALF), jnp.bfloat16),
-        scratch_shapes=[
-            pltpu.VMEM((4, QUARTER, HALF), jnp.bfloat16),
-            pltpu.SemaphoreType.DMA((2, 4)),
-        ],
-        cost_estimate=cost(0, 4_718_592),
-        compiler_params=params(52),
-        name="give",
-    )(at, weights)
-
-
 def keep_kernel(at_ref, w_ref, mine_ref, sems):
     copies = [
         pltpu.make_async_copy(w_ref.at[:, columns(q, at_ref[1])], mine_ref.at[q], sems.at[q])
@@ -159,7 +128,8 @@
     *pair_refs, mine_ref, theirs_ref, out_ref, g_ref, held_ref, sems = refs
     core = at_ref[1]
     copies = [
-        pltpu.make_async_copy(theirs_ref.at[q], held_ref.at[q], sems.at[q]) for q in range(4)
+        pltpu.make_async_copy(theirs_ref.at[:, columns(q, core)], held_ref.at[q], sems.at[q])
+        for q in range(4)
     ]
     for copy in copies:
         copy.start()
@@ -246,7 +216,7 @@
 
     is_root_core = core == z // 4
     root, before, other = first(at, rates)
-    theirs = swapped(give(at, lax.optimization_barrier((weights, root))[0]))
+    theirs = swapped(lax.optimization_barrier((weights, root))[0])
     parts = [lax.ppermute(root, EVERY, from_root(shift)) for shift in (1, 2, 3)]
     mine = keep(at, lax.optimization_barrier((weights, root))[0])
     before = jnp.where(is_root_core, before, swapped(other))

time: 161 us -> 163 us (1.012)
  the two profiles are of different devices: /device:TPU:1 before, /device:TPU:49 now
where the time goes in v8:
time: 163 us; the launch traced here: 162 us
  blocking collectives  86.8 us (53%)
  starting transfers between devices  36.8 us (23%)
  waiting for transfers between devices  19.9 us (12%)
  Pallas kernels  17.9 us (11%)
    all_to_all x3, blocking collectives, whole(): lax.all_to_all(sums.reshape(Y * Z, SLICE, HALF), ('y', 'z'), 0, 0, tiled=...  86.8 us
    ppermute x9, starting transfers between devices, swapped(): return lax.ppermute(array, 'core', SWAP)  22.3 us
    ppermute x6, waiting for transfers between devices, whole(): lax.ppermute(share, EVERY, across(j))  13.5 us
    ppermute x6, starting transfers between devices, whole(): lax.ppermute(share, EVERY, across(j))  12.5 us
    pallas_call x3, Pallas kernels, back(): pl.pallas_call(back_kernel, in_specs=[SMEM] + [VMEM] * len(pair) + [VMEM,...  9.45 us
    ppermute x9, waiting for transfers between devices, swapped(): return lax.ppermute(array, 'core', SWAP)  6.44 us
    pallas_call x1, Pallas kernels, outer(): pl.pallas_call(outer_kernel, in_specs=[SMEM] + [VMEM] * 6, out_specs=HBM,...  4.21 us
  transfers between devices with their start and end apart: 18, of which 13 were waited for; matrix products, arithmetic and copies ran while one was open for 0% of the time, Pallas kernels for 1%

profile of v8, /device:TPU:49, one launch (start us, length us, event | category | flops | bytes accessed | tf_op | source)
XLA Modules:
  0.0 162.5 jit_solution(2780720156345064107)
XLA Ops:
  0.1 2.0 %first.1 = (bf16[128,768]{1,0:T(8,128)(2,1)S(1)}, bf16[3,32,384]{2,1,0:T(8,128)(2,1)S(1)}, bf16[3,32,384]{2,1,0:T(8,128)(2,1)S(1)}) custom-call(s32[4]{0:T(128)S(1)} %pad_add_fusion.at_ref, bf16[5,3072,128]{2,1,0:T(8,128)(2,1)} %rates_ref.3), custom_call_target="tpu_custom_call" | custom-call | tf_op jit(solution)/shard_map/first/pallas_call | solution.py:71
  5.7 2.2 %keep.1.refs_1_.refs_2_ = bf16[4,768,384]{2,1,0:T(8,128)(2,1)S(1)} custom-call(s32[4]{0:T(128)S(1)} %pad_add_fusion.at_ref, bf16[768,3072]{1,0:T(8,128)(2,1)} %w_ref), custom_call_target="tpu_custom_call" | custom-call | bytes 4718592 | tf_op jit(solution)/shard_map/keep/pallas_call | solution.py:104
  8.0 5.5 %collective-permute-start.3 = (bf16[128,768]{1,0:T(8,128)(2,1)S(1)}, bf16[128,768]{1,0:T(8,128)(2,1)S(1)}, u32[]{:S(2)}, u32[]{:S(2)}) collective-permute-start(bf16[128,768]{1,0:T(8,128)(2,1)S(1)} %add_select_fusion), channel_id=1, source_target_pairs={{0,1},{1,0},{2,3},{3,2},{4,5},{5,4},{6,7},{7,6},{8,9},{9,8},{10,11... | collective-permute-start | bytes 589832 | tf_op jit(solution)/shard_map/ppermute | solution.py:215
  14.6 3.1 %back.3 = (bf16[4,8,32,384]{3,2,1,0:T(8,128)(2,1)S(1)}, bf16[128,768]{1,0:T(8,128)(2,1)S(1)}) custom-call(s32[4]{0:T(128)S(1)} %pad_add_fusion.at_ref, bf16[128,768]{1,0:T(8,128)(2,1)S(1)} %broadcast_select_fusion.refs_0_, bf16[4,768,384]{2,1,0:T(8,128)(2,1)S(1)} %keep.1.refs_1_.refs_2_, bf16[768,3072]{1,0:T(8,128)(2,1)} %collective-permute-done.5.refs_2_.refs_3_), custom_call_target="tpu_custom_call" | custom-call | flops 603979776 | bytes 6000000 | tf_op jit(solution)/shard_map/back/pallas_call | solution.py:148
  17.7 32.5 %all_to_all.15 = bf16[32,32,384]{2,1,0:T(8,128)(2,1)S(1)} all-to-all(bf16[32,32,384]{2,1,0:T(8,128)(2,1)S(1)} %bitcast.27), channel_id=1, replica_groups=mesh['y'=4,'z'=8,'x'=4,'core'=2] {'y','z'}, dimensions={0} | all-to-all | bytes 1572864 | tf_op jit(solution)/shard_map/all_to_all | solution.py:232
  52.4 1.5 collective-permute-start.8
  53.9 4.0 %collective-permute-start.7 = (bf16[32,768]{1,0:T(8,128)(2,1)S(1)}, bf16[32,768]{1,0:T(8,128)(2,1)S(1)}, u32[]{:S(2)}, u32[]{:S(2)}) collective-permute-start(bf16[32,768]{1,0:T(8,128)(2,1)S(1)} %maximum_select_fusion), channel_id=1, source_target_pairs={{0,0},{1,3},{2,64},{3,67},{4,128},{5,131},{6,192},{7,195},{8,8},{9... | collective-permute-start | bytes 147464 | tf_op jit(solution)/shard_map/ppermute | solution.py:240
  58.1 3.1 %collective-permute-done.7 = bf16[32,768]{1,0:T(8,128)(2,1)S(1)} collective-permute-done((bf16[32,768]{1,0:T(8,128)(2,1)S(1)}, bf16[32,768]{1,0:T(8,128)(2,1)S(1)}, u32[]{:S(2)}, u32[]{:S(2)}) %collective-permute-start.7) | collective-permute-done | bytes 49184 | tf_op jit(solution)/shard_map/ppermute | solution.py:240
  61.2 3.5 %collective-permute-start.9 = (bf16[2,32,768]{2,1,0:T(8,128)(2,1)S(1)}, bf16[2,32,768]{2,1,0:T(8,128)(2,1)S(1)}, u32[]{:S(2)}, u32[]{:S(2)}) collective-permute-start(bf16[2,32,768]{2,1,0:T(8,128)(2,1)S(1)} %pad_maximum_fusion.refs_0_), channel_id=1, source_target_pairs={{0,1},{1,0},{2,3},{3,2},{4,5},{5,4},{6,7},{7,6},{8,9},{9,8},{10,11... | collective-permute-start | bytes 294920 | tf_op jit(solution)/shard_map/ppermute | solution.py:215
  65.6 3.2 %back.4 = (bf16[4,8,32,384]{3,2,1,0:T(8,128)(2,1)S(1)}, bf16[128,768]{1,0:T(8,128)(2,1)S(1)}) custom-call(s32[4]{0:T(128)S(1)} %pad_add_fusion.at_ref, bf16[2,32,768]{2,1,0:T(8,128)(2,1)S(1)} %pad_maximum_fusion.refs_0_, bf16[2,32,768]{2,1,0:T(8,128)(2,1)S(1)} %collective-permute-done.9.refs_1_, bf16[4,768,384]{2,1,0:T(8,128)(2,1)S(1)} %keep.1.refs_1_.refs_2_, ...), custom_call_target="tpu_custom_call" | custom-call | flops 603979776 | bytes 6000000 | tf_op jit(solution)/shard_map/back/pallas_call | solution.py:148
  68.8 27.2 %all_to_all.16 = bf16[32,32,384]{2,1,0:T(8,128)(2,1)S(1)} all-to-all(bf16[32,32,384]{2,1,0:T(8,128)(2,1)S(1)} %bitcast.26), channel_id=1, replica_groups=mesh['y'=4,'z'=8,'x'=4,'core'=2] {'y','z'}, dimensions={0} | all-to-all | bytes 1572864 | tf_op jit(solution)/shard_map/all_to_all | solution.py:232
  96.1 1.6 %collective-permute-start.10 = (bf16[32,384]{1,0:T(8,128)(2,1)S(1)}, bf16[32,384]{1,0:T(8,128)(2,1)S(1)}, u32[]{:S(2)}, u32[]{:S(2)}) collective-permute-start(bf16[32,384]{1,0:T(8,128)(2,1)S(1)} %fusion.1), channel_id=1, source_target_pairs={{0,1},{1,0},{2,3},{3,2},{4,5},{5,4},{6,7},{7,6},{8,9},{9,8},{10,11... | collective-permute-start | bytes 73736 | tf_op jit(solution)/shard_map/ppermute | solution.py:215
  99.8 2.8 %collective-permute-start.11 = (bf16[32,768]{1,0:T(8,128)(2,1)S(1)}, bf16[32,768]{1,0:T(8,128)(2,1)S(1)}, u32[]{:S(2)}, u32[]{:S(2)}) collective-permute-start(bf16[32,768]{1,0:T(8,128)(2,1)S(1)} %maximum_select_fusion.1), channel_id=1, source_target_pairs={{0,0},{1,3},{2,64},{3,67},{4,128},{5,131},{6,192},{7,195},{8,8},{9... | collective-permute-start | bytes 147464 | tf_op jit(solution)/shard_map/ppermute | solution.py:240
  102.6 1.4 collective-permute-done.12
  104.1 3.2 %collective-permute-done.11 = bf16[32,768]{1,0:T(8,128)(2,1)S(1)} collective-permute-done((bf16[32,768]{1,0:T(8,128)(2,1)S(1)}, bf16[32,768]{1,0:T(8,128)(2,1)S(1)}, u32[]{:S(2)}, u32[]{:S(2)}) %collective-permute-start.11) | collective-permute-done | bytes 49184 | tf_op jit(solution)/shard_map/ppermute | solution.py:240
  107.3 3.6 %collective-permute-start.13 = (bf16[2,32,768]{2,1,0:T(8,128)(2,1)S(1)}, bf16[2,32,768]{2,1,0:T(8,128)(2,1)S(1)}, u32[]{:S(2)}, u32[]{:S(2)}) collective-permute-start(bf16[2,32,768]{2,1,0:T(8,128)(2,1)S(1)} %pad_maximum_fusion.1.refs_0_), channel_id=1, source_target_pairs={{0,1},{1,0},{2,3},{3,2},{4,5},{5,4},{6,7},{7,6},{8,9},{9,8},{10,11... | collective-permute-start | bytes 294920 | tf_op jit(solution)/shard_map/ppermute | solution.py:215
  111.8 3.2 %back.5 = (bf16[4,8,32,384]{3,2,1,0:T(8,128)(2,1)S(1)}, bf16[128,768]{1,0:T(8,128)(2,1)S(1)}) custom-call(s32[4]{0:T(128)S(1)} %pad_add_fusion.at_ref, bf16[2,32,768]{2,1,0:T(8,128)(2,1)S(1)} %pad_maximum_fusion.1.refs_0_, bf16[2,32,768]{2,1,0:T(8,128)(2,1)S(1)} %collective-permute-done.13.refs_1_, bf16[4,768,384]{2,1,0:T(8,128)(2,1)S(1)} %keep.1.refs_1_.refs_2_, ...), custom_call_target="tpu_custom_call" | custom-call | flops 603979776 | bytes 6000000 | tf_op jit(solution)/shard_map/back/pallas_call | solution.py:148
  115.0 27.2 %all_to_all.17 = bf16[32,32,384]{2,1,0:T(8,128)(2,1)S(1)} all-to-all(bf16[32,32,384]{2,1,0:T(8,128)(2,1)S(1)} %bitcast.25), channel_id=1, replica_groups=mesh['y'=4,'z'=8,'x'=4,'core'=2] {'y','z'}, dimensions={0} | all-to-all | bytes 1572864 | tf_op jit(solution)/shard_map/all_to_all | solution.py:232
  142.4 1.6 %collective-permute-start.14 = (bf16[32,384]{1,0:T(8,128)(2,1)S(1)}, bf16[32,384]{1,0:T(8,128)(2,1)S(1)}, u32[]{:S(2)}, u32[]{:S(2)}) collective-permute-start(bf16[32,384]{1,0:T(8,128)(2,1)S(1)} %fusion), channel_id=1, source_target_pairs={{0,1},{1,0},{2,3},{3,2},{4,5},{5,4},{6,7},{7,6},{8,9},{9,8},{10,11... | collective-permute-start | bytes 73736 | tf_op jit(solution)/shard_map/ppermute | solution.py:215
  145.8 2.1 %collective-permute-start.15 = (bf16[32,768]{1,0:T(8,128)(2,1)S(1)}, bf16[32,768]{1,0:T(8,128)(2,1)S(1)}, u32[]{:S(2)}, u32[]{:S(2)}) collective-permute-start(bf16[32,768]{1,0:T(8,128)(2,1)S(1)} %maximum_select_fusion.2), channel_id=1, source_target_pairs={{0,0},{1,3},{2,64},{3,67},{4,128},{5,131},{6,192},{7,195},{8,8},{9... | collective-permute-start | bytes 147464 | tf_op jit(solution)/shard_map/ppermute | solution.py:240
  147.9 2.4 %collective-permute-done.16 = bf16[32,768]{1,0:T(8,128)(2,1)S(1)} collective-permute-done((bf16[32,768]{1,0:T(8,128)(2,1)S(1)}, bf16[32,768]{1,0:T(8,128)(2,1)S(1)}, u32[]{:S(2)}, u32[]{:S(2)}) %collective-permute-start.16) | collective-permute-done | bytes 49184 | tf_op jit(solution)/shard_map/ppermute | solution.py:240
  150.3 3.1 %collective-permute-done.15 = bf16[32,768]{1,0:T(8,128)(2,1)S(1)} collective-permute-done((bf16[32,768]{1,0:T(8,128)(2,1)S(1)}, bf16[32,768]{1,0:T(8,128)(2,1)S(1)}, u32[]{:S(2)}, u32[]{:S(2)}) %collective-permute-start.15) | collective-permute-done | bytes 49184 | tf_op jit(solution)/shard_map/ppermute | solution.py:240
  153.4 3.7 %collective-permute-start.17 = (bf16[2,32,768]{2,1,0:T(8,128)(2,1)S(1)}, bf16[2,32,768]{2,1,0:T(8,128)(2,1)S(1)}, u32[]{:S(2)}, u32[]{:S(2)}) collective-permute-start(bf16[2,32,768]{2,1,0:T(8,128)(2,1)S(1)} %pad_maximum_fusion.2.first_ref), channel_id=1, source_target_pairs={{0,1},{1,0},{2,3},{3,2},{4,5},{5,4},{6,7},{7,6},{8,9},{9,8},{10,11... | collective-permute-start | bytes 294920 | tf_op jit(solution)/shard_map/ppermute | solution.py:215
  158.1 4.2 %outer.1 = bf16[768,3072]{1,0:T(8,128)(2,1)} custom-call(s32[4]{0:T(128)S(1)} %pad_add_fusion.at_ref, bf16[128,768]{1,0:T(8,128)(2,1)S(1)} %get-tuple-element.22.g4, bf16[128,768]{1,0:T(8,128)(2,1)S(1)} %get-tuple-element.25.g3, bf16[128,768]{1,0:T(8,128)(2,1)S(1)} %get-tuple-element.27.g2, bf16[2,32,768]{2,1,0:T(8,128)(2,1)S(1)} %pad_maximum_fusion.2.first_ref, ...), custom_call_target="tpu_custom_call" | custom-call | flops 2415919104 | bytes 8000000 | tf_op jit(solution)/shard_map/outer/pallas_call | solution.py:193
  (39 shorter events, 14.2 us)
Async XLA Ops:
  2.1 12.4 %collective-permute-start.5 = (bf16[768,3072]{1,0:T(8,128)(2,1)}, bf16[768,3072]{1,0:T(8,128)(2,1)}, u32[]{:S(2)}, u32[]{:S(2)}) collective-permute-start(bf16[768,3072]{1,0:T(8,128)(2,1)} %w_ref), channel_id=1, source_target_pairs={{0,1},{1,0},{2,3},{3,2},{4,5},{5,4},{6,7},{7,6},{8,9},{9,8},{10,11... | collective-permute-start | bytes 14155784 | tf_op jit(solution)/shard_map/ppermute | solution.py:215
  2.9 5.0 %collective-permute-start.2 = (bf16[128,768]{1,0:T(8,128)(2,1)S(1)}, bf16[128,768]{1,0:T(8,128)(2,1)S(1)}, u32[]{:S(2)}, u32[]{:S(2)}) collective-permute-start(bf16[128,768]{1,0:T(8,128)(2,1)S(1)} %get-tuple-element.17), channel_id=1, source_target_pairs={{0,6},{8,14},{16,22},{24,30},{33,39},{41,47},{49,55},{57,63},{66,6... | collective-permute-start | bytes 589832 | tf_op jit(solution)/shard_map/ppermute | solution.py:220
  3.6 4.3 %collective-permute-start.1 = (bf16[128,768]{1,0:T(8,128)(2,1)S(1)}, bf16[128,768]{1,0:T(8,128)(2,1)S(1)}, u32[]{:S(2)}, u32[]{:S(2)}) collective-permute-start(bf16[128,768]{1,0:T(8,128)(2,1)S(1)} %get-tuple-element.17), channel_id=1, source_target_pairs={{0,4},{8,12},{16,20},{24,28},{33,37},{41,45},{49,53},{57,61},{66,7... | collective-permute-start | bytes 589832 | tf_op jit(solution)/shard_map/ppermute | solution.py:220
  4.2 3.7 %collective-permute-start = (bf16[128,768]{1,0:T(8,128)(2,1)S(1)}, bf16[128,768]{1,0:T(8,128)(2,1)S(1)}, u32[]{:S(2)}, u32[]{:S(2)}) collective-permute-start(bf16[128,768]{1,0:T(8,128)(2,1)S(1)} %get-tuple-element.17), channel_id=1, source_target_pairs={{0,2},{8,10},{16,18},{24,26},{33,35},{41,43},{49,51},{57,59},{66,6... | collective-permute-start | bytes 589832 | tf_op jit(solution)/shard_map/ppermute | solution.py:220
  4.9 8.5 %collective-permute-start.4 = (bf16[3,32,384]{2,1,0:T(8,128)(2,1)S(1)}, bf16[3,32,384]{2,1,0:T(8,128)(2,1)S(1)}, u32[]{:S(2)}, u32[]{:S(2)}) collective-permute-start(bf16[3,32,384]{2,1,0:T(8,128)(2,1)S(1)} %get-tuple-element.19), channel_id=1, source_target_pairs={{0,1},{1,0},{2,3},{3,2},{4,5},{5,4},{6,7},{7,6},{8,9},{9,8},{10,11... | collective-permute-start | bytes 221192 | tf_op jit(solution)/shard_map/ppermute | solution.py:215
  8.0 6.6 %collective-permute-start.3 = (bf16[128,768]{1,0:T(8,128)(2,1)S(1)}, bf16[128,768]{1,0:T(8,128)(2,1)S(1)}, u32[]{:S(2)}, u32[]{:S(2)}) collective-permute-start(bf16[128,768]{1,0:T(8,128)(2,1)S(1)} %add_select_fusion), channel_id=1, source_target_pairs={{0,1},{1,0},{2,3},{3,2},{4,5},{5,4},{6,7},{7,6},{8,9},{9,8},{10,11... | collective-permute-start | bytes 589832 | tf_op jit(solution)/shard_map/ppermute | solution.py:215
  50.3 2.1 %collective-permute-start.6 = (bf16[32,384]{1,0:T(8,128)(2,1)S(1)}, bf16[32,384]{1,0:T(8,128)(2,1)S(1)}, u32[]{:S(2)}, u32[]{:S(2)}) collective-permute-start(bf16[32,384]{1,0:T(8,128)(2,1)S(1)} %fusion.2), channel_id=1, source_target_pairs={{0,1},{1,0},{2,3},{3,2},{4,5},{5,4},{6,7},{7,6},{8,9},{9,8},{10,11... | collective-permute-start | bytes 73736 | tf_op jit(solution)/shard_map/ppermute | solution.py:215
  52.4 5.7 %collective-permute-start.8 = (bf16[32,768]{1,0:T(8,128)(2,1)S(1)}, bf16[32,768]{1,0:T(8,128)(2,1)S(1)}, u32[]{:S(2)}, u32[]{:S(2)}) collective-permute-start(bf16[32,768]{1,0:T(8,128)(2,1)S(1)} %maximum_select_fusion), channel_id=1, source_target_pairs={{0,4},{1,7},{2,68},{3,71},{4,132},{5,135},{6,196},{7,199},{8,12},{... | collective-permute-start | bytes 147464 | tf_op jit(solution)/shard_map/ppermute | solution.py:240
  53.9 7.3 %collective-permute-start.7 = (bf16[32,768]{1,0:T(8,128)(2,1)S(1)}, bf16[32,768]{1,0:T(8,128)(2,1)S(1)}, u32[]{:S(2)}, u32[]{:S(2)}) collective-permute-start(bf16[32,768]{1,0:T(8,128)(2,1)S(1)} %maximum_select_fusion), channel_id=1, source_target_pairs={{0,0},{1,3},{2,64},{3,67},{4,128},{5,131},{6,192},{7,195},{8,8},{9... | collective-permute-start | bytes 147464 | tf_op jit(solution)/shard_map/ppermute | solution.py:240
  61.2 4.4 %collective-permute-start.9 = (bf16[2,32,768]{2,1,0:T(8,128)(2,1)S(1)}, bf16[2,32,768]{2,1,0:T(8,128)(2,1)S(1)}, u32[]{:S(2)}, u32[]{:S(2)}) collective-permute-start(bf16[2,32,768]{2,1,0:T(8,128)(2,1)S(1)} %pad_maximum_fusion.refs_0_), channel_id=1, source_target_pairs={{0,1},{1,0},{2,3},{3,2},{4,5},{5,4},{6,7},{7,6},{8,9},{9,8},{10,11... | collective-permute-start | bytes 294920 | tf_op jit(solution)/shard_map/ppermute | solution.py:215
  96.1 2.5 %collective-permute-start.10 = (bf16[32,384]{1,0:T(8,128)(2,1)S(1)}, bf16[32,384]{1,0:T(8,128)(2,1)S(1)}, u32[]{:S(2)}, u32[]{:S(2)}) collective-permute-start(bf16[32,384]{1,0:T(8,128)(2,1)S(1)} %fusion.1), channel_id=1, source_target_pairs={{0,1},{1,0},{2,3},{3,2},{4,5},{5,4},{6,7},{7,6},{8,9},{9,8},{10,11... | collective-permute-start | bytes 73736 | tf_op jit(solution)/shard_map/ppermute | solution.py:215
  98.6 5.4 %collective-permute-start.12 = (bf16[32,768]{1,0:T(8,128)(2,1)S(1)}, bf16[32,768]{1,0:T(8,128)(2,1)S(1)}, u32[]{:S(2)}, u32[]{:S(2)}) collective-permute-start(bf16[32,768]{1,0:T(8,128)(2,1)S(1)} %maximum_select_fusion.1), channel_id=1, source_target_pairs={{0,4},{1,7},{2,68},{3,71},{4,132},{5,135},{6,196},{7,199},{8,12},{... | collective-permute-start | bytes 147464 | tf_op jit(solution)/shard_map/ppermute | solution.py:240
  99.8 7.5 %collective-permute-start.11 = (bf16[32,768]{1,0:T(8,128)(2,1)S(1)}, bf16[32,768]{1,0:T(8,128)(2,1)S(1)}, u32[]{:S(2)}, u32[]{:S(2)}) collective-permute-start(bf16[32,768]{1,0:T(8,128)(2,1)S(1)} %maximum_select_fusion.1), channel_id=1, source_target_pairs={{0,0},{1,3},{2,64},{3,67},{4,128},{5,131},{6,192},{7,195},{8,8},{9... | collective-permute-start | bytes 147464 | tf_op jit(solution)/shard_map/ppermute | solution.py:240
  107.3 50.8 %copy-start = (bf16[5,3072,128]{2,1,0:T(8,128)(2,1)S(1)}, bf16[5,3072,128]{2,1,0:T(8,128)(2,1)}, u32[]{:S(2)}) copy-start(bf16[5,3072,128]{2,1,0:T(8,128)(2,1)} %rates_ref.3) | copy-start | bytes 11796484
  107.3 4.5 %collective-permute-start.13 = (bf16[2,32,768]{2,1,0:T(8,128)(2,1)S(1)}, bf16[2,32,768]{2,1,0:T(8,128)(2,1)S(1)}, u32[]{:S(2)}, u32[]{:S(2)}) collective-permute-start(bf16[2,32,768]{2,1,0:T(8,128)(2,1)S(1)} %pad_maximum_fusion.1.refs_0_), channel_id=1, source_target_pairs={{0,1},{1,0},{2,3},{3,2},{4,5},{5,4},{6,7},{7,6},{8,9},{9,8},{10,11... | collective-permute-start | bytes 294920 | tf_op jit(solution)/shard_map/ppermute | solution.py:215
  142.4 2.5 %collective-permute-start.14 = (bf16[32,384]{1,0:T(8,128)(2,1)S(1)}, bf16[32,384]{1,0:T(8,128)(2,1)S(1)}, u32[]{:S(2)}, u32[]{:S(2)}) collective-permute-start(bf16[32,384]{1,0:T(8,128)(2,1)S(1)} %fusion), channel_id=1, source_target_pairs={{0,1},{1,0},{2,3},{3,2},{4,5},{5,4},{6,7},{7,6},{8,9},{9,8},{10,11... | collective-permute-start | bytes 73736 | tf_op jit(solution)/shard_map/ppermute | solution.py:215
  144.9 5.4 %collective-permute-start.16 = (bf16[32,768]{1,0:T(8,128)(2,1)S(1)}, bf16[32,768]{1,0:T(8,128)(2,1)S(1)}, u32[]{:S(2)}, u32[]{:S(2)}) collective-permute-start(bf16[32,768]{1,0:T(8,128)(2,1)S(1)} %maximum_select_fusion.2), channel_id=1, source_target_pairs={{0,4},{1,7},{2,68},{3,71},{4,132},{5,135},{6,196},{7,199},{8,12},{... | collective-permute-start | bytes 147464 | tf_op jit(solution)/shard_map/ppermute | solution.py:240
  145.8 7.6 %collective-permute-start.15 = (bf16[32,768]{1,0:T(8,128)(2,1)S(1)}, bf16[32,768]{1,0:T(8,128)(2,1)S(1)}, u32[]{:S(2)}, u32[]{:S(2)}) collective-permute-start(bf16[32,768]{1,0:T(8,128)(2,1)S(1)} %maximum_select_fusion.2), channel_id=1, source_target_pairs={{0,0},{1,3},{2,64},{3,67},{4,128},{5,131},{6,192},{7,195},{8,8},{9... | collective-permute-start | bytes 147464 | tf_op jit(solution)/shard_map/ppermute | solution.py:240
  153.4 4.7 %collective-permute-start.17 = (bf16[2,32,768]{2,1,0:T(8,128)(2,1)S(1)}, bf16[2,32,768]{2,1,0:T(8,128)(2,1)S(1)}, u32[]{:S(2)}, u32[]{:S(2)}) collective-permute-start(bf16[2,32,768]{2,1,0:T(8,128)(2,1)S(1)} %pad_maximum_fusion.2.first_ref), channel_id=1, source_target_pairs={{0,1},{1,0},{2,3},{3,2},{4,5},{5,4},{6,7},{7,6},{8,9},{9,8},{10,11... | collective-permute-start | bytes 294920 | tf_op jit(solution)/shard_map/ppermute | solution.py:215
